TPU v7x, 32 devices: a whole 2x2x4 slice. The times are simulated.
32 devices in a mesh: dp: 8 (over z, x), tensor: 4 (over y, core).
Axes of the slice: x: 2, y: 2, z: 4, core: 2. Of those that a mesh axis runs over, the one named last changes fastest.
Arguments:
- momentum: float32 [8, 8192, 1024], P('dp', None, 'tensor'), may hold values from -6 to 6
- gradient: bfloat16 [8, 8192, 1024], P('dp', None, 'tensor'), may hold values from -6 to 6
- masters: float32 [8192, 1024], P('dp', 'tensor'), may hold values from -6 to 6
- tokens: bfloat16 [1024, 8192], P('dp', 'tensor'), may hold values from -6 to 6
- freq_index: int32 [8, 1024], P('tensor'), may hold values from 0 to 8191, as said below
Outputs:
- residual: float32 [8, 8192, 1024], P('dp', None, 'tensor')
- new_masters: float32 [8192, 1024], P('dp', 'tensor')
- keys_out: bfloat16 [1024, 1024], P('dp', 'tensor')
Inputs may be any that keep to these rules, and one draw needn't show every extreme that they name: `freq_index`: each row lists 1024 distinct frequencies, 0 and 8191 among them; the same list serves every replica.
All inputs are finite; a program needn't handle non-finite values.
Results may differ from a plain program's by a relative error of at most 0.007.
Values may be sent and summed in bfloat16 or wider, within the bound.
No kernel may reach another device: no remote copies, remote signals or barrier semaphores. Data moves between devices by JAX's collectives and lax.ppermute only.
A program may use at most 128 MiB of HBM per device.

v0:
```python
import math

import jax
import jax.numpy as jnp
from jax import lax
from jax.sharding import PartitionSpec as P

momentum_decay = 0.9
step_rate = 1.0


def cosine_rows(frequency, first_row, row_count, model_width):
    positions = first_row + lax.iota(jnp.int32, row_count)
    phases = (2 * positions + 1)[None, :] * frequency[:, None] % (4 * model_width)
    angles = phases.astype(jnp.float32) * (math.pi / (2 * model_width))
    scales = jnp.where(
        frequency == 0, math.sqrt(1.0 / model_width), math.sqrt(2.0 / model_width)
    ).astype(jnp.float32)
    return (scales[:, None] * jnp.cos(angles)).astype(jnp.bfloat16)


def body(momentum, gradient, masters, tokens, freq_index):
    highest = lax.Precision.HIGHEST
    replica_count = lax.axis_size("dp")
    own_rows = masters.shape[0]
    model_width = momentum.shape[1]
    cols_dev = momentum.shape[2]
    blocks = freq_index.shape[0]
    block_cols = cols_dev // blocks
    freq_count = freq_index.shape[1]
    piece_rows = min(512, freq_count)
    gathered = lax.all_gather(tokens, "tensor", axis=1, tiled=True)
    states = momentum_decay * momentum[0] + gradient[0].astype(jnp.float32)
    states_low = states.astype(jnp.bfloat16)
    own_coeffs = []
    remains = []
    for column_block in range(blocks):
        block_state = states[:, column_block * block_cols : (column_block + 1) * block_cols]
        block_low = states_low[:, column_block * block_cols : (column_block + 1) * block_cols]
        remain = block_state
        pieces = []
        for freq_piece in range(freq_count // piece_rows):
            lower = freq_piece * piece_rows
            cosines = cosine_rows(
                freq_index[column_block, lower : lower + piece_rows], 0, model_width, model_width
            )
            coefficient = jnp.dot(cosines, block_low, preferred_element_type=jnp.float32).astype(
                jnp.bfloat16
            )
            remain = remain - jnp.dot(cosines.T, coefficient, preferred_element_type=jnp.float32)
            pieces.append(coefficient)
        own_coeffs.append(jnp.concatenate(pieces, axis=0))
        remains.append(remain)
    residual = jnp.concatenate(remains, axis=1)[None]
    stacked = jnp.stack(own_coeffs)
    summed = lax.psum(stacked.astype(jnp.float32).astype(jnp.bfloat16), "dp").astype(jnp.float32)
    averaged = summed / replica_count
    row_start = lax.axis_index("dp") * own_rows
    update = jnp.concatenate(
        [
            jnp.dot(
                cosine_rows(freq_index[column_block], row_start, own_rows, model_width)
                .astype(jnp.float32)
                .T,
                averaged[column_block],
                precision=highest,
            )
            for column_block in range(blocks)
        ],
        axis=1,
    )
    new_masters = masters - step_rate * update
    weights = new_masters.astype(jnp.bfloat16)
    products = jnp.dot(
        gathered,
        lax.all_gather(weights, "dp", axis=0, tiled=True),
        preferred_element_type=jnp.float32,
    )
    projected = (products * model_width ** (-0.5)).astype(jnp.bfloat16)
    return (residual, new_masters, projected)


def solution(mesh):
    return jax.shard_map(
        body,
        mesh=mesh,
        in_specs=(
            P("dp", None, "tensor"),
            P("dp", None, "tensor"),
            P("dp", "tensor"),
            P("dp", "tensor"),
            P("tensor", None),
        ),
        out_specs=(P("dp", None, "tensor"), P("dp", "tensor"), P("dp", "tensor")),
        check_vma=False,
    )
```

profile of v0, /device:TPU:0, one launch (start us, length us, event | category | flops | bytes accessed | tf_op | source)
XLA Modules:
  0.0 619.9 jit_solution(11259473456085211382)
XLA Ops:
  8.0 0.0 all-reduce.2.cloned.1.call-start
  8.1 8.9 %copy.8 = f32[1,8192,256]{1,2,0:T(8,128)} copy(f32[1,8192,256]{2,1,0:T(8,128)} %param.5) | data formatting | bytes 16777216 | tf_op args[0]
  17.0 6.4 %copy.9 = bf16[1,8192,256]{1,2,0:T(8,128)(2,1)} copy(bf16[1,8192,256]{2,1,0:T(8,128)(2,1)} %param.6) | data formatting | bytes 8388608 | tf_op args[1]
  23.3 9.9 %fusion.103 = (bf16[8192,256]{0,1:T(8,128)(2,1)S(1)}, f32[8192,256]{0,1:T(8,128)}) fusion(bf16[1,8192,256]{1,2,0:T(8,128)(2,1)} %copy.9, f32[1,8192,256]{1,2,0:T(8,128)} %copy.8), kind=kLoop, calls=%fused_computation.145 | loop fusion | flops 8388608 | bytes 25165824 | tf_op jit(solution)/shard_map/convert_element_type | solution.py:34
  33.2 0.0 copy-start.1
  33.2 0.1 fusion.139
  33.4 0.1 fusion.143
  33.5 0.1 fusion.145
  33.7 0.1 fusion.141
  33.8 0.1 copy-done.1
  33.9 0.0 copy-start.2
  33.9 0.0 copy-start.4
  34.0 62.8 %fusion.25 = bf16[512,128]{1,0:T(8,128)(2,1)S(1)} fusion(s32[512]{0:T(512)S(1)} %bitcast.41, f32[512]{0:T(512)S(1)} %compare_select_fusion.2, s32[8192]{0:T(1024)S(1)} %multiply_add_fusion, bf16[8192,128]{0,1:T(8,128)(2,1)S(1)} %fusion.139), kind=kOutput, calls=%fused_computation.49 | convolution fusion | flops 1140850688 | bytes 2265088 | tf_op jit(solution)/shard_map/dot_general | solution.py:47
  96.8 0.0 copy-done.2
  96.8 0.0 copy-done.4
  96.9 63.1 %fusion.31 = bf16[512,128]{1,0:T(8,128)(2,1)S(1)} fusion(s32[512]{0:T(512)S(1)} %bitcast.47, f32[512]{0:T(512)S(1)} %compare_select_fusion.4, s32[8192]{0:T(1024)S(1)} %multiply_add_fusion, bf16[8192,128]{0,1:T(8,128)(2,1)S(1)} %fusion.143), kind=kOutput, calls=%fused_computation.51 | convolution fusion | flops 1140850688 | bytes 2265088 | tf_op jit(solution)/shard_map/dot_general | solution.py:47
  159.9 62.8 %fusion.34 = bf16[512,128]{1,0:T(8,128)(2,1)S(1)} fusion(s32[512]{0:T(512)S(1)} %bitcast.50, s32[8192]{0:T(1024)S(1)} %multiply_add_fusion, f32[512]{0:T(512)S(1)} %compare_select_fusion.5, bf16[8192,128]{0,1:T(8,128)(2,1)S(1)} %fusion.145), kind=kOutput, calls=%fused_computation.52 | convolution fusion | flops 1140850688 | bytes 2265088 | tf_op jit(solution)/shard_map/dot_general | solution.py:47
  222.8 0.0 copy-start
  222.8 63.2 %fusion.28 = bf16[512,128]{1,0:T(8,128)(2,1)S(1)} fusion(s32[512]{0:T(512)S(1)} %bitcast.44, f32[512]{0:T(512)S(1)} %compare_select_fusion.3, s32[8192]{0:T(1024)S(1)} %multiply_add_fusion, bf16[8192,128]{0,1:T(8,128)(2,1)S(1)} %fusion.141), kind=kOutput, calls=%fused_computation.50 | convolution fusion | flops 1140850688 | bytes 2265088 | tf_op jit(solution)/shard_map/dot_general | solution.py:47
  286.1 0.8 pad_maximum_fusion
  286.9 0.0 all-reduce.2.cloned.1.call-update
  286.9 0.0 all-gather.5.cloned.1.call-start
  287.0 0.5 all-gather.5.cloned.1.call-update
  287.5 0.0 all-gather.3.cloned.1.call-start
  287.6 0.0 copy-done
  287.6 0.3 copy.10
  288.0 64.9 %convolution_subtract_fusion.3 = f32[8192,128]{0,1:T(8,128)} fusion(s32[512]{0:T(512)S(1)} %bitcast.51, s32[8192]{0:T(1024)S(1)} %multiply_add_fusion, f32[512]{0:T(512)S(1)} %compare_select_fusion.5, f32[8192,256]{0,1:T(8,128)} %get-tuple-element.9, bf16[512,128]{1,0:T(8,128)(2,1)S(1)} %fusion.34), kind=kOutput, calls=%fused_computation.47 | convolution fusion | flops 1141899264 | bytes 8556544 | tf_op jit(solution)/shard_map/dot_general | solution.py:50
  352.9 9.7 %all-reduce.2.cloned.1.call-done = bf16[2,1024,128]{2,1,0:T(8,128)(2,1)} async-done(((bf16[2,1024,128]{2,1,0:T(8,128)(2,1)}), bf16[2,1024,128]{2,1,0:T(8,128)(2,1)}) %all-reduce.2.cloned.1.call-update) | async-done | bytes 524304 | tf_op jit(solution)/shard_map/psum | solution.py:56
  362.6 1.1 convert_multiply_fusion
  363.7 16.6 %fusion.54 = f32[1024,128]{0,1:T(8,128)S(1)} fusion(s32[1024]{0:T(1024)S(1)} %bitcast.39, s32[1024]{0:T(1024)S(1)} %multiply_add_fusion.1, f32[1024]{0:T(1024)S(1)} %compare_select_fusion.1, f32[2,1024,128]{2,1,0:T(8,128)S(1)} %convert_multiply_fusion), kind=kOutput, calls=%fused_computation.81 | convolution fusion | flops 1627389952 | bytes 1060864 | tf_op jit(solution)/shard_map/dot_general | solution.py:61
  380.4 16.9 %fusion.52 = f32[1024,128]{0,1:T(8,128)S(1)} fusion(s32[1024]{0:T(1024)S(1)} %bitcast.37, f32[1024]{0:T(1024)S(1)} %compare_select_fusion, s32[1024]{0:T(1024)S(1)} %multiply_add_fusion.1, f32[2,1024,128]{2,1,0:T(8,128)S(1)} %convert_multiply_fusion), kind=kOutput, calls=%fused_computation.80 | convolution fusion | flops 1627389952 | bytes 1060864 | tf_op jit(solution)/shard_map/dot_general | solution.py:61
  397.3 1.0 fusion.102
  398.3 0.0 all-gather.3.cloned.1.call-update
  398.3 65.4 %convolution_subtract_fusion.2 = f32[8192,128]{0,1:T(8,128)S(1)} fusion(f32[8192,128]{0,1:T(8,128)} %convolution_subtract_fusion.3, s32[512]{0:T(512)S(1)} %bitcast.48, f32[512]{0:T(512)S(1)} %compare_select_fusion.4, s32[8192]{0:T(1024)S(1)} %multiply_add_fusion, bf16[512,128]{1,0:T(8,128)(2,1)S(1)} %fusion.31), kind=kOutput, calls=%fused_computation.46 | convolution fusion | flops 1141899264 | bytes 8556544 | tf_op jit(solution)/shard_map/dot_general | solution.py:50
  463.8 0.0 copy-start.3
  463.8 0.0 copy-start.5
  463.8 65.8 %convolution_subtract_fusion.1 = f32[8192,128]{0,1:T(8,128)S(1)} fusion(s32[512]{0:T(512)S(1)} %bitcast.45, f32[512]{0:T(512)S(1)} %compare_select_fusion.3, s32[8192]{0:T(1024)S(1)} %multiply_add_fusion, f32[8192,256]{0,1:T(8,128)} %get-tuple-element.9, bf16[512,128]{1,0:T(8,128)(2,1)S(1)} %fusion.28), kind=kOutput, calls=%fused_computation.45 | convolution fusion | flops 1141899264 | bytes 8556544 | tf_op jit(solution)/shard_map/dot_general | solution.py:50
  529.6 0.0 copy-done.3
  529.6 0.0 copy-done.5
  529.6 63.6 %convolution_subtract_fusion = f32[8192,128]{0,1:T(8,128)S(1)} fusion(f32[8192,128]{0,1:T(8,128)S(1)} %convolution_subtract_fusion.1, s32[512]{0:T(512)S(1)} %bitcast.42, f32[512]{0:T(512)S(1)} %copy-done.5, s32[8192]{0:T(1024)S(1)} %multiply_add_fusion, bf16[512,128]{1,0:T(8,128)(2,1)S(1)} %fusion.25), kind=kOutput, calls=%fused_computation.44 | convolution fusion | flops 1141899264 | bytes 8556544 | tf_op jit(solution)/shard_map/dot_general | solution.py:50
  593.3 3.8 maximum_bitcast_fusion
  597.1 9.0 %copy.11 = f32[1,8192,256]{2,1,0:T(8,128)} copy(f32[1,8192,256]{1,2,0:T(8,128)} %maximum_bitcast_fusion) | data formatting | bytes 16777216
  606.1 1.3 copy.12
  607.4 0.0 all-gather.5.cloned.1.call-done
  607.4 0.0 all-gather.3.cloned.1.call-done
  607.4 4.1 fusion.61
  611.5 0.7 copy.13
  (11 shorter events, 0.1 us)
Async XLA Ops:
  8.0 354.6 %all-reduce.2.cloned.1.call-start = ((), (), s32[]{:S(2)}) async-start(), calls=%async_computation | async-start | bytes 1048576 | tf_op jit(solution)/shard_map/psum | solution.py:56
  33.2 0.7 copy-start.1
  33.9 62.9 %copy-start.2 = (s32[1,512]{1,0:T(1,128)}, s32[1,512]{1,0:T(1,128)S(1)}, u32[]{:S(2)}) copy-start(s32[1,512]{1,0:T(1,128)S(1)} %get-tuple-element.13) | copy-start | bytes 6148
  33.9 62.9 %copy-start.4 = (f32[512]{0:T(512)}, f32[512]{0:T(512)S(1)}, u32[]{:S(2)}) copy-start(f32[512]{0:T(512)S(1)} %compare_select_fusion.2) | copy-start | bytes 6148
  222.8 64.9 %copy-start = (f32[1024,256]{1,0:T(8,128)S(1)}, f32[1024,256]{1,0:T(8,128)}, u32[]{:S(2)}) copy-start(f32[1024,256]{1,0:T(8,128)} %param.7) | copy-start | bytes 3145732
  286.9 320.5 %all-gather.5.cloned.1.call-start = ((), (), s32[]{:S(2)}) async-start(), calls=%async_computation.2 | async-start | bytes 2621440 | tf_op jit(solution)/shard_map/all_gather | solution.py:32
  287.5 319.9 %all-gather.3.cloned.1.call-start = ((), (), s32[]{:S(2)}) async-start(), calls=%async_computation.1 | async-start | bytes 4718592 | tf_op jit(solution)/shard_map/all_gather | solution.py:76
  463.8 65.9 %copy-start.3 = (s32[1,512]{1,0:T(1,128)S(1)}, s32[1,512]{1,0:T(1,128)}, u32[]{:S(2)}) copy-start(s32[1,512]{1,0:T(1,128)} %copy-done.2) | copy-start | bytes 6148
  463.8 65.9 %copy-start.5 = (f32[512]{0:T(512)S(1)}, f32[512]{0:T(512)}, u32[]{:S(2)}) copy-start(f32[512]{0:T(512)} %copy-done.4) | copy-start | bytes 6148
Sparse Core Ops, SparseCore 0:
  287.0 75.5 all-reduce.1
Sparse Core Ops, SparseCore 1:
  289.0 25.1 all-gather.4
  398.4 71.7 all-gather.2
where the time goes:
time: 623 us; the launch traced here: 620 us
  matrix products  549 us (88%)
  local copies, waits for them, and re-layouts  27.3 us (4%)
  other arithmetic  16.7 us (3%)
  between operations  16 us (3%)
  waiting for transfers between devices  10.3 us (2%)
    dot_general x4, matrix products, body(): jnp.dot(cosines.T, coefficient, preferred_element_type=jnp.float32)  260 us
    dot_general x4, matrix products, body(): jnp.dot(cosines, block_low, preferred_element_type=jnp.float32)  252 us
    dot_general x2, matrix products, body(): jnp.dot(cosine_rows(freq_index[column_block], row_start, own_rows, model_...  33.5 us
    unnamed x18, local copies, waits for them, and re-layouts  26.8 us
  transfers between devices with their start and end apart: 3, of which 1 were waited for; matrix products, arithmetic and copies ran while one was open for 50% of the time, Pallas kernels for 0%

commit v1 on v0

v1 whole, which is shorter than its diff:
```python
import math

import jax
import jax.numpy as jnp
from jax import lax
from jax.experimental import pallas as pl
from jax.experimental.pallas import tpu as pltpu
from jax.sharding import PartitionSpec as P

momentum_decay = 0.9
step_rate = 1.0
fine_rows = 64
flip_rows = 128
f32 = jnp.float32
bf16 = jnp.bfloat16


def sine_cosine(phase, model_width):
    quarter = (phase + model_width // 2) // model_width
    x = (phase - quarter * model_width).astype(f32) * (math.pi / (2 * model_width))
    z = x * x
    sine = x + x * z * (-1.6666654611e-1 + z * (8.3321608736e-3 + z * -1.9515295891e-4))
    cosine = 1.0 - 0.5 * z + z * z * (
        4.166664568298827e-2 + z * (-1.388731625493765e-3 + z * 2.443315711809948e-5)
    )
    swapped = (quarter & 1) == 1
    cos_sign = jnp.where(((quarter + 1) & 2) == 2, -1.0, 1.0).astype(f32)
    sin_sign = jnp.where((quarter & 2) == 2, -1.0, 1.0).astype(f32)
    return (
        cos_sign * jnp.where(swapped, sine, cosine),
        sin_sign * jnp.where(swapped, cosine, sine),
    )


def fill_tables(frequency, first_row, coarse_cos, coarse_sin, fine_cos, fine_sin, model_width):
    period = 4 * model_width
    freqs = frequency.shape[1]
    coarse = lax.broadcasted_iota(jnp.int32, (coarse_cos.shape[0], freqs), 0)
    fine = lax.broadcasted_iota(jnp.int32, (fine_rows, freqs), 0)
    scale = jnp.where(
        frequency == 0, math.sqrt(1.0 / model_width), math.sqrt(2.0 / model_width)
    ).astype(f32)
    cosine, sine = sine_cosine(
        (2 * (first_row + coarse * fine_rows)) * frequency % period, model_width
    )
    coarse_cos[...] = cosine * scale
    coarse_sin[...] = sine * scale
    cosine, sine = sine_cosine((2 * fine + 1) * frequency % period, model_width)
    fine_cos[...] = cosine
    fine_sin[...] = sine


def fill_cosines(target, first_coarse, count, coarse_cos, coarse_sin, fine_cos, fine_sin):
    for lane in range(0, target.shape[1], 128):
        lanes = pl.ds(lane, 128)
        cosine = fine_cos[:, lanes]
        sine = fine_sin[:, lanes]
        coarse_c = coarse_cos[pl.ds(first_coarse, count), lanes]
        coarse_s = coarse_sin[pl.ds(first_coarse, count), lanes]
        for k in range(count):
            target[pl.ds(k * fine_rows, fine_rows), lanes] = (
                coarse_c[k : k + 1] * cosine - coarse_s[k : k + 1] * sine
            ).astype(bf16)


def reversal():
    rows = lax.broadcasted_iota(jnp.int32, (flip_rows, flip_rows), 0)
    cols = lax.broadcasted_iota(jnp.int32, (flip_rows, flip_rows), 1)
    return jnp.where(rows + cols == flip_rows - 1, 1.0, 0.0).astype(bf16)


def flip_low(value):
    flips = reversal()
    pieces = [
        jnp.dot(flips, value[lower : lower + flip_rows], preferred_element_type=f32)
        for lower in range(value.shape[0] - flip_rows, -1, -flip_rows)
    ]
    return jnp.concatenate(pieces, axis=0)


def flip_wide(value):
    high = value.astype(bf16)
    low = (value - high.astype(f32)).astype(bf16)
    return flip_low(high) + flip_low(low)


def parity_sign(frequency):
    return (1 - 2 * (frequency & 1)).astype(f32)


def dot_tn(a, b):
    return lax.dot_general(a, b, (((0,), (0,)), ((), ())), preferred_element_type=f32)


def dot_nt(a, b):
    return lax.dot_general(a, b, (((1,), (1,)), ((), ())), preferred_element_type=f32)


def forward(column_block, momentum, gradient, freq_rows, meta, group):
    model_width = momentum.shape[1]
    block_cols = momentum.shape[2] // freq_rows.shape[0]
    freqs = freq_rows.shape[2]
    half = model_width // 2
    tile = min(512, half)
    steps = half // tile
    piece = block_cols // group

    def kernel(meta_ref, freq, mom_a, mom_b, grad_a, grad_b, coeff, *rest):
        pieces = rest[:group]
        table, total, coarse_cos, coarse_sin, fine_cos, fine_sin = rest[group:]
        step = pl.program_id(0)
        frequency = freq[0]

        @pl.when(step == 0)
        def _():
            fill_tables(frequency, 0, coarse_cos, coarse_sin, fine_cos, fine_sin, model_width)

        fill_cosines(
            table, pl.multiple_of(step * (tile // fine_rows), tile // fine_rows),
            tile // fine_rows,
            coarse_cos, coarse_sin, fine_cos, fine_sin,
        )
        low_a = (momentum_decay * mom_a[0] + grad_a[0].astype(f32)).astype(bf16)
        low_b = (momentum_decay * mom_b[0] + grad_b[0].astype(f32)).astype(bf16)
        both = jnp.concatenate([low_a, flip_low(low_b).astype(bf16)], axis=1)
        partial = dot_tn(both, table[...])

        @pl.when(step == 0)
        def _():
            total[...] = partial

        @pl.when(step > 0)
        def _():
            total[...] += partial

        @pl.when(step == steps - 1)
        def _():
            coeff[...] = (
                total[:block_cols] + parity_sign(frequency) * total[block_cols:]
            ).astype(bf16)
            for k in range(group):
                start = ((meta_ref[0] % group) ^ k) * piece
                pieces[k][...] = coeff[pl.ds(pl.multiple_of(start, piece), piece), :]

    def rows(which):
        def index(step, meta_ref):
            return (0, 2 * steps - 1 - step if which else step, column_block)

        return pl.BlockSpec((1, tile, block_cols), index)

    whole = lambda step, meta_ref: (0, 0)
    return pl.pallas_call(
        kernel,
        name=f"forward_{column_block}",
        grid_spec=pltpu.PrefetchScalarGridSpec(
            num_scalar_prefetch=1,
            grid=(steps,),
            in_specs=[
                pl.BlockSpec((1, 1, freqs), lambda step, meta_ref: (column_block, 0, 0)),
                rows(0), rows(1), rows(0), rows(1),
            ],
            out_specs=[pl.BlockSpec((block_cols, freqs), whole)]
            + [pl.BlockSpec((piece, freqs), whole)] * group
            + [pl.BlockSpec((tile, freqs), lambda step, meta_ref: (step, 0))],
            scratch_shapes=[pltpu.VMEM((2 * block_cols, freqs), f32)]
            + [pltpu.VMEM((half // fine_rows, freqs), f32)] * 2
            + [pltpu.VMEM((fine_rows, freqs), f32)] * 2,
        ),
        out_shape=[jax.ShapeDtypeStruct((block_cols, freqs), bf16)]
        + [jax.ShapeDtypeStruct((piece, freqs), bf16)] * group
        + [jax.ShapeDtypeStruct((half, freqs), bf16)],
    )(meta, freq_rows, momentum, momentum, gradient, gradient)


def remain(column_block, momentum, gradient, freq_rows, coeff, table, previous):
    model_width = momentum.shape[1]
    block_cols = momentum.shape[2] // freq_rows.shape[0]
    freqs = freq_rows.shape[2]
    half = model_width // 2
    tile = min(512, half)
    steps = half // tile

    def kernel(freq, mom_a, mom_b, grad_a, grad_b, coeff_ref, table_ref, *rest):
        residual, both, buffer, sems = rest[-4:]
        step = pl.program_id(0)
        slot = step % 2

        def copies(at, where):
            lanes = pl.ds(column_block * block_cols, block_cols)
            return [
                pltpu.make_async_copy(
                    buffer.at[where, k], residual.at[0, pl.ds(start * tile, tile), lanes],
                    sems.at[where, k],
                )
                for k, start in enumerate((at, 2 * steps - 1 - at))
            ]

        @pl.when(step == 0)
        def _():
            both[:block_cols] = coeff_ref[...]
            both[block_cols:] = (coeff_ref[...].astype(f32) * parity_sign(freq[0])).astype(bf16)

        back = dot_nt(table_ref[...], both[...])

        @pl.when(step >= 2)
        def _():
            for copy in copies(step - 2, slot):
                copy.wait()

        buffer[slot, 0] = (
            momentum_decay * mom_a[0] + grad_a[0].astype(f32) - back[:, :block_cols]
        )
        buffer[slot, 1] = (
            momentum_decay * mom_b[0] + grad_b[0].astype(f32) - flip_wide(back[:, block_cols:])
        )
        for copy in copies(step, slot):
            copy.start()

        @pl.when(step == steps - 1)
        def _():
            if steps > 1:
                for copy in copies(step - 1, 1 - slot):
                    copy.wait()
            for copy in copies(step, slot):
                copy.wait()

    def rows(which):
        def index(step):
            return (0, 2 * steps - 1 - step if which else step, column_block)

        return pl.BlockSpec((1, tile, block_cols), index)

    operands = [freq_rows, momentum, momentum, gradient, gradient, coeff, table]
    specs = [
        pl.BlockSpec((1, 1, freqs), lambda step: (column_block, 0, 0)),
        rows(0), rows(1), rows(0), rows(1),
        pl.BlockSpec((block_cols, freqs), lambda step: (0, 0)),
        pl.BlockSpec((tile, freqs), lambda step: (step, 0)),
    ]
    aliases = {}
    if previous is not None:
        aliases = {len(operands): 0}
        operands.append(previous)
        specs.append(pl.BlockSpec(memory_space=pl.ANY))
    return pl.pallas_call(
        kernel,
        name=f"remain_{column_block}",
        grid=(steps,),
        in_specs=specs,
        out_specs=pl.BlockSpec(memory_space=pl.ANY),
        scratch_shapes=[
            pltpu.VMEM((2 * block_cols, freqs), bf16),
            pltpu.VMEM((2, 2, tile, block_cols), f32),
            pltpu.SemaphoreType.DMA((2, 2)),
        ],
        out_shape=jax.ShapeDtypeStruct(momentum.shape, f32),
        input_output_aliases=aliases,
    )(*operands)


def spread(tokens, meta, dp, tensor):
    token_rows, width = tokens.shape
    ratio = dp // tensor
    rows, lanes = token_rows // tensor, width // ratio

    def kernel(meta_ref, tokens_ref, *outs):
        for k in range(dp):
            part = meta_ref[0] ^ k
            outs[k][...] = tokens_ref[
                pl.ds(pl.multiple_of((part % tensor) * rows, rows), rows),
                pl.ds(pl.multiple_of((part // tensor) * lanes, lanes), lanes),
            ]

    return pl.pallas_call(
        kernel,
        name="spread",
        in_specs=[pl.BlockSpec(memory_space=pltpu.SMEM), pl.BlockSpec(memory_space=pltpu.VMEM)],
        out_specs=[pl.BlockSpec(memory_space=pltpu.VMEM)] * dp,
        out_shape=[jax.ShapeDtypeStruct((rows, lanes), bf16)] * dp,
    )(meta, tokens)


def apply(masters, freq_rows, means, feature_parts, meta, model_width, dp, tensor, group):
    own_rows, cols = masters.shape
    blocks, _, freqs = freq_rows.shape
    block_cols = cols // blocks
    piece = block_cols // group
    _, part_rows, part_lanes = feature_parts[0].shape
    token_rows = part_rows * tensor
    ratio = dp // tensor

    def kernel(meta_ref, freq, masters_ref, *rest):
        mean_refs = rest[: blocks * group]
        feature_refs = rest[blocks * group : blocks * group + tensor]
        rest = rest[blocks * group + tensor :]
        new_ref, outs = rest[0], rest[1 : 1 + dp]
        table, mean, weights, coarse_cos, coarse_sin, fine_cos, fine_sin = rest[1 + dp :]
        device, rank = meta_ref[0], meta_ref[1]
        for block in range(blocks):
            fill_tables(
                freq[block], device * own_rows, coarse_cos, coarse_sin, fine_cos, fine_sin,
                model_width,
            )
            fill_cosines(
                table, 0, own_rows // fine_rows, coarse_cos, coarse_sin, fine_cos, fine_sin
            )
            for k in range(group):
                start = ((device % group) ^ k) * piece
                mean[pl.ds(pl.multiple_of(start, piece), piece), :] = mean_refs[
                    block * group + k
                ][...]
            update = dot_nt(table[...], mean[...]) * (1.0 / dp)
            lanes = pl.ds(block * block_cols, block_cols)
            fresh = masters_ref[:, lanes] - step_rate * update
            new_ref[:, lanes] = fresh
            weights[:, lanes] = fresh.astype(bf16)
        for k in range(dp):
            target = device ^ k
            gathered = []
            for other in range(tensor):
                holder = rank ^ other
                message = target ^ ((device % ratio) * tensor + holder)
                gathered.append(feature_refs[other][message])
            products = jnp.dot(
                jnp.concatenate(gathered, axis=0), weights[...], preferred_element_type=f32
            )
            for other in range(tensor):
                start = (rank ^ other) * part_rows
                outs[k][pl.ds(pl.multiple_of(start, part_rows), part_rows), :] = products[
                    other * part_rows : (other + 1) * part_rows
                ].astype(bf16)

    vmem = pl.BlockSpec(memory_space=pltpu.VMEM)
    return pl.pallas_call(
        kernel,
        name="apply",
        in_specs=[pl.BlockSpec(memory_space=pltpu.SMEM)]
        + [vmem] * (2 + blocks * group + tensor),
        out_specs=[vmem] * (1 + dp),
        out_shape=[jax.ShapeDtypeStruct((own_rows, cols), f32)]
        + [jax.ShapeDtypeStruct((token_rows, cols), bf16)] * dp,
        scratch_shapes=[
            pltpu.VMEM((own_rows, freqs), bf16),
            pltpu.VMEM((block_cols, freqs), bf16),
            pltpu.VMEM((own_rows, cols), bf16),
        ]
        + [pltpu.VMEM((own_rows // fine_rows, freqs), f32)] * 2
        + [pltpu.VMEM((fine_rows, freqs), f32)] * 2,
    )(meta, freq_rows, masters, *means, *feature_parts)


def swap(value, axis, mask, size):
    return lax.ppermute(value, axis, [(k, k ^ mask) for k in range(size)])


def sum_low(values):
    total = values[0].astype(f32)
    for value in values[1:]:
        total = total + value.astype(f32)
    return total.astype(bf16)


def body(momentum, gradient, masters, tokens, freq_index):
    dp, tensor = lax.axis_size("dp"), lax.axis_size("tensor")
    group = min(4, dp)
    ratio = dp // tensor
    blocks = freq_index.shape[0]
    model_width = momentum.shape[1]
    device, rank = lax.axis_index("dp"), lax.axis_index("tensor")
    meta = jnp.stack([device, rank]).astype(jnp.int32)
    freq_rows = freq_index[:, None, :]

    sent = spread(tokens, meta, dp, tensor)
    received = []
    for k in range(dp):
        pairs = []
        for source in range(dp):
            for holder in range(tensor):
                part = source ^ k
                target = (holder * ratio + part // tensor) * tensor + part % tensor
                pairs.append((source * tensor + holder, target))
        received.append(lax.ppermute(sent[k], ("dp", "tensor"), pairs))
    features = {0: jnp.stack(received)}
    mask = tensor // 2
    while mask > 0:
        for held in sorted(features):
            features[held ^ mask] = swap(features[held], "tensor", mask, tensor)
        mask //= 2
    feature_parts = [features[k] for k in range(tensor)]

    residual = None
    means = []
    forwards = [
        forward(block, momentum, gradient, freq_rows, meta, group) for block in range(blocks)
    ]
    for block in range(blocks):
        pieces = forwards[block][1 : 1 + group]
        summed = sum_low(
            [pieces[0]] + [swap(pieces[k], "dp", k, dp) for k in range(1, group)]
        )
        summed = sum_low(
            [summed] + [swap(summed, "dp", k * group, dp) for k in range(1, dp // group)]
        )
        means += [summed] + [swap(summed, "dp", k, dp) for k in range(1, group)]
    for block in range(blocks):
        residual = remain(
            block, momentum, gradient, freq_rows, forwards[block][0], forwards[block][-1], residual
        )
    new_masters, *partials = apply(
        masters, freq_rows, means, feature_parts, meta, model_width, dp, tensor, group
    )
    total = partials[0].astype(f32)
    for k in range(1, dp):
        total = total + swap(partials[k], "dp", k, dp).astype(f32)
    projected = (total * model_width ** (-0.5)).astype(bf16)
    return (residual, new_masters, projected)


def solution(mesh):
    return jax.shard_map(
        body,
        mesh=mesh,
        in_specs=(
            P("dp", None, "tensor"),
            P("dp", None, "tensor"),
            P("dp", "tensor"),
            P("dp", "tensor"),
            P("tensor", None),
        ),
        out_specs=(P("dp", None, "tensor"), P("dp", "tensor"), P("dp", "tensor")),
        check_vma=False,
    )
```

time: 623 us -> 138 us (0.22)
  matrix products: 549 us -> 0 us
  Pallas kernels: 0 us -> 60.3 us
  starting transfers between devices: 0.12 us -> 50.9 us
  local copies, waits for them, and re-layouts: 27.3 us -> 2.96 us
  between operations: 16 us -> 1 us
  other arithmetic: 16.7 us -> 2.39 us
  waiting for transfers between devices: 10.3 us -> 19.2 us
    dot_general x11 -> x0, matrix products: 549 us -> none  [the longest x4 260 us: body(): jnp.dot(cosines.T, coefficient, preferred_element_type=jnp.float32)]
    pallas_call x0 -> x6, Pallas kernels: none -> 60.3 us  [the longest x2 26.8 us: forward(): pl.pallas_call(kernel, name=f'forward_{column_block}', grid_spec=pltpu.Pr...]
    ppermute x0 -> x32, starting transfers between devices: none -> 50.9 us  [the longest x24 27.1 us: swap(): return lax.ppermute(value, axis, [(k, k ^ mask) for k in range(size)])]
    unnamed x18 -> x35, local copies, waits for them, and re-layouts: 26.8 us -> 1.66 us
    ppermute x0 -> x32, waiting for transfers between devices: none -> 19.2 us  [the longest x24 12.1 us: swap(): return lax.ppermute(value, axis, [(k, k ^ mask) for k in range(size)])]
    psum x1 -> x0, waiting for transfers between devices: 9.74 us -> none  [body(): lax.psum(stacked.astype(jnp.float32).astype(jnp.bfloat16), 'dp')]
    convert_element_type x2 -> x5, other arithmetic: 10.9 us -> 1.75 us  [the longest x4 1.04 us: sum_low(): return total.astype(bf16)]
  transfers between devices with their start and end apart: 3 -> 32, of which waited for: 1 -> 10; matrix products, arithmetic and copies ran while one was open for 50% -> 2% of each run, Pallas kernels for 0% -> 37%
where the time goes in v1:
time: 138 us; the launch traced here: 137 us
  Pallas kernels  60.3 us (44%)
  starting transfers between devices  50.9 us (37%)
  waiting for transfers between devices  19.2 us (14%)
  local copies, waits for them, and re-layouts  2.96 us (2%)
  other arithmetic  2.39 us (2%)
    ppermute x24, starting transfers between devices, swap(): return lax.ppermute(value, axis, [(k, k ^ mask) for k in range(size)])  27.1 us
    pallas_call x2, Pallas kernels, forward(): pl.pallas_call(kernel, name=f'forward_{column_block}', grid_spec=pltpu.Pr...  26.8 us
    pallas_call x2, Pallas kernels, remain(): pl.pallas_call(kernel, name=f'remain_{column_block}', grid=(steps,), in_s...  24.3 us
    ppermute x8, starting transfers between devices, body(): received.append(lax.ppermute(sent[k], ('dp', 'tensor'), pairs))  23.8 us
    ppermute x24, waiting for transfers between devices, swap(): return lax.ppermute(value, axis, [(k, k ^ mask) for k in range(size)])  12.1 us
    pallas_call x1, Pallas kernels, apply(): pl.pallas_call(kernel, name='apply', in_specs=[pl.BlockSpec(memory_space=...  7.29 us
    ppermute x8, waiting for transfers between devices, body(): received.append(lax.ppermute(sent[k], ('dp', 'tensor'), pairs))  7.15 us
  transfers between devices with their start and end apart: 32, of which 10 were waited for; matrix products, arithmetic and copies ran while one was open for 2% of the time, Pallas kernels for 37%

profile of v1, /device:TPU:0, one launch (start us, length us, event | category | flops | bytes accessed | tf_op | source)
XLA Modules:
  0.0 136.8 jit_solution(9447099649489677952)
XLA Ops:
  0.6 0.6 pad_add_fusion.meta_ref
  1.3 1.9 %spread.1 = (bf16[32,1024]{1,0:T(8,128)(2,1)}, bf16[32,1024]{1,0:T(8,128)(2,1)}, bf16[32,1024]{1,0:T(8,128)(2,1)}, bf16[32,1024]{1,0:T(8,128)(2,1)}, bf16[32,102...) custom-call(s32[2]{0:T(128)} %pad_add_fusion.meta_ref, ...), custom_call_target="tpu_custom_call" | custom-call | tf_op jit(solution)/shard_map/spread/pallas_call | solution.py:274
  3.2 1.5 %collective-permute-start.14 = (bf16[32,1024]{1,0:T(8,128)(2,1)}, bf16[32,1024]{1,0:T(8,128)(2,1)S(1)}, u32[]{:S(2)}, u32[]{:S(2)}) collective-permute-start(bf16[32,1024]{1,0:T(8,128)(2,1)} %get-tuple-element.44), channel_id=1, source_target_pairs={{0,0},{1,8},{2,16},{3,24},{4,1},{5,9},{6,17},{7,25},{8,2},{9,10},{... | collective-permute-start | bytes 196616 | tf_op jit(solution)/shard_map/ppermute | solution.py:382
  4.7 3.6 %collective-permute-start.15 = (bf16[32,1024]{1,0:T(8,128)(2,1)}, bf16[32,1024]{1,0:T(8,128)(2,1)S(1)}, u32[]{:S(2)}, u32[]{:S(2)}) collective-permute-start(bf16[32,1024]{1,0:T(8,128)(2,1)} %get-tuple-element.45), channel_id=1, source_target_pairs={{0,1},{1,9},{2,17},{3,25},{4,0},{5,8},{6,16},{7,24},{8,3},{9,11},{... | collective-permute-start | bytes 196616 | tf_op jit(solution)/shard_map/ppermute | solution.py:382
  8.3 3.5 %collective-permute-start.16 = (bf16[32,1024]{1,0:T(8,128)(2,1)}, bf16[32,1024]{1,0:T(8,128)(2,1)S(1)}, u32[]{:S(2)}, u32[]{:S(2)}) collective-permute-start(bf16[32,1024]{1,0:T(8,128)(2,1)} %get-tuple-element.46), channel_id=1, source_target_pairs={{0,2},{1,10},{2,18},{3,26},{4,3},{5,11},{6,19},{7,27},{8,0},{9,8},... | collective-permute-start | bytes 196616 | tf_op jit(solution)/shard_map/ppermute | solution.py:382
  11.8 3.6 %collective-permute-start.17 = (bf16[32,1024]{1,0:T(8,128)(2,1)}, bf16[32,1024]{1,0:T(8,128)(2,1)S(1)}, u32[]{:S(2)}, u32[]{:S(2)}) collective-permute-start(bf16[32,1024]{1,0:T(8,128)(2,1)} %get-tuple-element.47), channel_id=1, source_target_pairs={{0,3},{1,11},{2,19},{3,27},{4,2},{5,10},{6,18},{7,26},{8,1},{9,9},... | collective-permute-start | bytes 196616 | tf_op jit(solution)/shard_map/ppermute | solution.py:382
  15.4 1.4 collective-permute-start.18
  16.8 0.0 collective-permute-done.14
  16.8 1.9 %collective-permute-start.19 = (bf16[32,1024]{1,0:T(8,128)(2,1)}, bf16[32,1024]{1,0:T(8,128)(2,1)S(1)}, u32[]{:S(2)}, u32[]{:S(2)}) collective-permute-start(bf16[32,1024]{1,0:T(8,128)(2,1)} %get-tuple-element.49), channel_id=1, source_target_pairs={{0,5},{1,13},{2,21},{3,29},{4,4},{5,12},{6,20},{7,28},{8,7},{9,15}... | collective-permute-start | bytes 196616 | tf_op jit(solution)/shard_map/ppermute | solution.py:382
  18.7 8.3 %collective-permute-start.20 = (bf16[32,1024]{1,0:T(8,128)(2,1)}, bf16[32,1024]{1,0:T(8,128)(2,1)S(1)}, u32[]{:S(2)}, u32[]{:S(2)}) collective-permute-start(bf16[32,1024]{1,0:T(8,128)(2,1)} %get-tuple-element.50), channel_id=1, source_target_pairs={{0,6},{1,14},{2,22},{3,30},{4,7},{5,15},{6,23},{7,31},{8,4},{9,12}... | collective-permute-start | bytes 196616 | tf_op jit(solution)/shard_map/ppermute | solution.py:382
  27.0 0.1 collective-permute-start.21
  27.2 0.2 collective-permute-done.19
  27.4 3.6 %collective-permute-done.20 = bf16[32,1024]{1,0:T(8,128)(2,1)S(1)} collective-permute-done((bf16[32,1024]{1,0:T(8,128)(2,1)}, bf16[32,1024]{1,0:T(8,128)(2,1)S(1)}, u32[]{:S(2)}, u32[]{:S(2)}) %collective-permute-start.20) | collective-permute-done | bytes 65568 | tf_op jit(solution)/shard_map/ppermute | solution.py:382
  31.0 3.3 %collective-permute-done.21 = bf16[32,1024]{1,0:T(8,128)(2,1)S(1)} collective-permute-done((bf16[32,1024]{1,0:T(8,128)(2,1)}, bf16[32,1024]{1,0:T(8,128)(2,1)S(1)}, u32[]{:S(2)}, u32[]{:S(2)}) %collective-permute-start.21) | collective-permute-done | bytes 65568 | tf_op jit(solution)/shard_map/ppermute | solution.py:382
  34.3 1.1 collective-permute-start.23
  35.4 1.3 broadcast_in_dim.3.freq
  36.7 13.4 %forward_0.1 = (bf16[128,1024]{1,0:T(8,128)(2,1)}, bf16[32,1024]{1,0:T(8,128)(2,1)}, bf16[32,1024]{1,0:T(8,128)(2,1)}, bf16[32,1024]{1,0:T(8,128)(2,1)}, bf16[32...) custom-call(s32[2]{0:T(128)} %pad_add_fusion.meta_ref, s32[2,1,1024]{2,1,0:T(1,128)} %broadcast_in_dim.3.freq, ...), custom_call_target="tpu_custom_call" | custom-call | tf_op jit(solution)/shard_map/forward_0/pallas_call | solution.py:152
  50.1 0.1 collective-permute-start.1
  50.2 3.4 %collective-permute-start = (bf16[32,1024]{1,0:T(8,128)(2,1)}, bf16[32,1024]{1,0:T(8,128)(2,1)S(1)}, u32[]{:S(2)}, u32[]{:S(2)}) collective-permute-start(bf16[32,1024]{1,0:T(8,128)(2,1)} %get-tuple-element.37), channel_id=1, source_target_pairs={{0,4},{4,0},{8,12},{12,8},{16,20},{20,16},{24,28},{28,24},{1,5},{5... | collective-permute-start | bytes 196616 | tf_op jit(solution)/shard_map/ppermute | solution.py:353
  53.6 13.4 %forward_1.1 = (bf16[128,1024]{1,0:T(8,128)(2,1)}, bf16[32,1024]{1,0:T(8,128)(2,1)}, bf16[32,1024]{1,0:T(8,128)(2,1)}, bf16[32,1024]{1,0:T(8,128)(2,1)}, bf16[32...) custom-call(s32[2]{0:T(128)} %pad_add_fusion.meta_ref, s32[2,1,1024]{2,1,0:T(1,128)} %broadcast_in_dim.3.freq, ...), custom_call_target="tpu_custom_call" | custom-call | tf_op jit(solution)/shard_map/forward_1/pallas_call | solution.py:152
  67.0 0.1 collective-permute-start.9
  67.0 0.0 collective-permute-done.2
  67.0 1.5 %collective-permute-start.8 = (bf16[32,1024]{1,0:T(8,128)(2,1)}, bf16[32,1024]{1,0:T(8,128)(2,1)S(1)}, u32[]{:S(2)}, u32[]{:S(2)}) collective-permute-start(bf16[32,1024]{1,0:T(8,128)(2,1)} %get-tuple-element.42), channel_id=1, source_target_pairs={{0,8},{4,12},{8,0},{12,4},{16,24},{20,28},{24,16},{28,20},{1,9},{5... | collective-permute-start | bytes 196616 | tf_op jit(solution)/shard_map/ppermute | solution.py:353
  68.6 1.9 %collective-permute-start.7 = (bf16[32,1024]{1,0:T(8,128)(2,1)}, bf16[32,1024]{1,0:T(8,128)(2,1)S(1)}, u32[]{:S(2)}, u32[]{:S(2)}) collective-permute-start(bf16[32,1024]{1,0:T(8,128)(2,1)} %get-tuple-element.41), channel_id=1, source_target_pairs={{0,4},{4,0},{8,12},{12,8},{16,20},{20,16},{24,28},{28,24},{1,5},{5... | collective-permute-start | bytes 196616 | tf_op jit(solution)/shard_map/ppermute | solution.py:353
  70.5 0.0 collective-permute-done
  70.5 1.8 %collective-permute-done.9 = bf16[32,1024]{1,0:T(8,128)(2,1)S(1)} collective-permute-done((bf16[32,1024]{1,0:T(8,128)(2,1)}, bf16[32,1024]{1,0:T(8,128)(2,1)S(1)}, u32[]{:S(2)}, u32[]{:S(2)}) %collective-permute-start.9) | collective-permute-done | bytes 65568 | tf_op jit(solution)/shard_map/ppermute | solution.py:353
  72.3 0.9 collective-permute-start.3
  73.2 0.0 collective-permute-done.23.rest_10_
  73.2 0.0 collective-permute-start.24
  73.2 0.0 collective-permute-done.7
  73.2 1.0 add_convert_fusion.1
  74.2 2.1 %collective-permute-start.10 = (bf16[32,1024]{1,0:T(8,128)(2,1)S(1)}, bf16[32,1024]{1,0:T(8,128)(2,1)S(1)}, u32[]{:S(2)}, u32[]{:S(2)}) collective-permute-start(bf16[32,1024]{1,0:T(8,128)(2,1)S(1)} %add_convert_fusion.1), channel_id=1, source_target_pairs={{0,16},{4,20},{8,24},{12,28},{16,0},{20,4},{24,8},{28,12},{1,17},{... | collective-permute-start | bytes 196616 | tf_op jit(solution)/shard_map/ppermute | solution.py:353
  76.3 1.9 %collective-permute-done.3 = bf16[32,1024]{1,0:T(8,128)(2,1)S(1)} collective-permute-done((bf16[32,1024]{1,0:T(8,128)(2,1)S(1)}, bf16[32,1024]{1,0:T(8,128)(2,1)S(1)}, u32[]{:S(2)}, u32[]{:S(2)}) %collective-permute-start.3) | collective-permute-done | bytes 65568 | tf_op jit(solution)/shard_map/ppermute | solution.py:353
  78.3 0.0 copy-start.4
  78.3 0.2 collective-permute-start.4
  78.5 0.3 collective-permute-start.5
  78.8 2.2 %collective-permute-done.10 = bf16[32,1024]{1,0:T(8,128)(2,1)S(1)} collective-permute-done((bf16[32,1024]{1,0:T(8,128)(2,1)S(1)}, bf16[32,1024]{1,0:T(8,128)(2,1)S(1)}, u32[]{:S(2)}, u32[]{:S(2)}) %collective-permute-start.10) | collective-permute-done | bytes 65568 | tf_op jit(solution)/shard_map/ppermute | solution.py:353
  81.0 1.3 collective-permute-start.6
  82.4 0.2 collective-permute-done.4.rest_1_
  82.6 0.2 collective-permute-start.11
  82.8 0.5 collective-permute-done.5.rest_2_
  83.3 1.3 collective-permute-start.12
  84.6 1.7 %collective-permute-done.6.rest_3_ = bf16[32,1024]{1,0:T(8,128)(2,1)S(1)} collective-permute-done((bf16[32,1024]{1,0:T(8,128)(2,1)S(1)}, bf16[32,1024]{1,0:T(8,128)(2,1)S(1)}, u32[]{:S(2)}, u32[]{:S(2)}) %collective-permute-start.6) | collective-permute-done | bytes 65568 | tf_op jit(solution)/shard_map/ppermute | solution.py:353
  86.4 1.5 %collective-permute-start.13 = (bf16[32,1024]{1,0:T(8,128)(2,1)S(1)}, bf16[32,1024]{1,0:T(8,128)(2,1)S(1)}, u32[]{:S(2)}, u32[]{:S(2)}) collective-permute-start(bf16[32,1024]{1,0:T(8,128)(2,1)S(1)} %add_convert_fusion.rest_4_), channel_id=1, source_target_pairs={{0,12},{4,8},{8,4},{12,0},{16,28},{20,24},{24,20},{28,16},{1,13},{... | collective-permute-start | bytes 196616 | tf_op jit(solution)/shard_map/ppermute | solution.py:353
  87.9 0.0 collective-permute-done.12.rest_6_
  87.9 3.6 %collective-permute-done.13.rest_7_ = bf16[32,1024]{1,0:T(8,128)(2,1)S(1)} collective-permute-done((bf16[32,1024]{1,0:T(8,128)(2,1)S(1)}, bf16[32,1024]{1,0:T(8,128)(2,1)S(1)}, u32[]{:S(2)}, u32[]{:S(2)}) %collective-permute-start.13) | collective-permute-done | bytes 65568 | tf_op jit(solution)/shard_map/ppermute | solution.py:353
  91.5 0.0 collective-permute-done.22.rest_9_
  91.6 0.0 collective-permute-done.24.rest_11_
  91.6 0.5 copy-done.11
  92.2 0.2 copy-done.2
  92.4 0.8 copy-done.3
  93.2 7.3 %apply.1 = (f32[1024,256]{1,0:T(8,128)}, bf16[128,256]{1,0:T(8,128)(2,1)}, bf16[128,256]{1,0:T(8,128)(2,1)}, bf16[128,256]{1,0:T(8,128)(2,1)}, bf16[128,256]{1,0...) custom-call(s32[2]{0:T(128)} %pad_add_fusion.meta_ref, ...), custom_call_target="tpu_custom_call" | custom-call | tf_op jit(solution)/shard_map/apply/pallas_call | solution.py:334
  100.5 3.1 %collective-permute-start.31 = (bf16[128,256]{1,0:T(8,128)(2,1)}, bf16[128,256]{1,0:T(8,128)(2,1)S(1)}, u32[]{:S(2)}, u32[]{:S(2)}) collective-permute-start(bf16[128,256]{1,0:T(8,128)(2,1)} %get-tuple-element.60), channel_id=1, source_target_pairs={{0,28},{4,24},{8,20},{12,16},{16,12},{20,8},{24,4},{28,0},{1,29},{... | collective-permute-start | bytes 196616 | tf_op jit(solution)/shard_map/ppermute | solution.py:353
  103.6 1.5 %collective-permute-start.30 = (bf16[128,256]{1,0:T(8,128)(2,1)}, bf16[128,256]{1,0:T(8,128)(2,1)S(1)}, u32[]{:S(2)}, u32[]{:S(2)}) collective-permute-start(bf16[128,256]{1,0:T(8,128)(2,1)} %get-tuple-element.59), channel_id=1, source_target_pairs={{0,24},{4,28},{8,16},{12,20},{16,8},{20,12},{24,0},{28,4},{1,25},{... | collective-permute-start | bytes 196616 | tf_op jit(solution)/shard_map/ppermute | solution.py:353
  105.2 1.2 collective-permute-start.29
  106.3 1.9 %collective-permute-start.28 = (bf16[128,256]{1,0:T(8,128)(2,1)}, bf16[128,256]{1,0:T(8,128)(2,1)S(1)}, u32[]{:S(2)}, u32[]{:S(2)}) collective-permute-start(bf16[128,256]{1,0:T(8,128)(2,1)} %get-tuple-element.57), channel_id=1, source_target_pairs={{0,16},{4,20},{8,24},{12,28},{16,0},{20,4},{24,8},{28,12},{1,17},{... | collective-permute-start | bytes 196616 | tf_op jit(solution)/shard_map/ppermute | solution.py:353
  108.2 0.7 collective-permute-start.27
  108.9 0.0 collective-permute-done.31
  108.9 2.1 %collective-permute-start.26 = (bf16[128,256]{1,0:T(8,128)(2,1)}, bf16[128,256]{1,0:T(8,128)(2,1)S(1)}, u32[]{:S(2)}, u32[]{:S(2)}) collective-permute-start(bf16[128,256]{1,0:T(8,128)(2,1)} %get-tuple-element.55), channel_id=1, source_target_pairs={{0,8},{4,12},{8,0},{12,4},{16,24},{20,28},{24,16},{28,20},{1,9},{5... | collective-permute-start | bytes 196616 | tf_op jit(solution)/shard_map/ppermute | solution.py:353
  111.0 0.0 collective-permute-done.30
  111.0 0.7 collective-permute-start.25
  111.7 12.1 %remain_0.1.rest_0_ = f32[1,8192,256]{2,1,0:T(8,128)} custom-call(s32[2,1,1024]{2,1,0:T(1,128)} %broadcast_in_dim.3.freq, f32[1,8192,256]{2,1,0:T(8,128)} %mom_b.7, f32[1,8192,256]{2,1,0:T(8,128)} %mom_b.7, bf16[1,8192,256]{2,1,0:T(8,128)(2,1)} %grad_b.7, bf16[1,8192,256]{2,1,0:T(8,128)(2,1)} %grad_b.7, bf16[128,1024]{1,0:T(8,128)(2,1)} %get-tuple-element.34.coeff_ref, ...), custom_call_target="tpu_custom_call" | custom-call | tf_op jit(solution)/shard_map/remain_0/pallas_call | solution.py:245
  123.8 12.2 %remain_1.1 = f32[1,8192,256]{2,1,0:T(8,128)} custom-call(s32[2,1,1024]{2,1,0:T(1,128)} %broadcast_in_dim.3.freq, f32[1,8192,256]{2,1,0:T(8,128)} %mom_b.7, f32[1,8192,256]{2,1,0:T(8,128)} %mom_b.7, bf16[1,8192,256]{2,1,0:T(8,128)(2,1)} %grad_b.7, bf16[1,8192,256]{2,1,0:T(8,128)(2,1)} %grad_b.7, ...), custom_call_target="tpu_custom_call", output_to_operand_aliasing={{}: (7, {})} | custom-call | tf_op jit(solution)/shard_map/remain_1/pallas_call | solution.py:245
  136.1 0.7 multiply_convert_fusion
  (49 shorter events, 0.2 us)
Async XLA Ops:
  3.2 13.6 %collective-permute-start.14 = (bf16[32,1024]{1,0:T(8,128)(2,1)}, bf16[32,1024]{1,0:T(8,128)(2,1)S(1)}, u32[]{:S(2)}, u32[]{:S(2)}) collective-permute-start(bf16[32,1024]{1,0:T(8,128)(2,1)} %get-tuple-element.44), channel_id=1, source_target_pairs={{0,0},{1,8},{2,16},{3,24},{4,1},{5,9},{6,17},{7,25},{8,2},{9,10},{... | collective-permute-start | bytes 196616 | tf_op jit(solution)/shard_map/ppermute | solution.py:382
  4.7 14.0 %collective-permute-start.15 = (bf16[32,1024]{1,0:T(8,128)(2,1)}, bf16[32,1024]{1,0:T(8,128)(2,1)S(1)}, u32[]{:S(2)}, u32[]{:S(2)}) collective-permute-start(bf16[32,1024]{1,0:T(8,128)(2,1)} %get-tuple-element.45), channel_id=1, source_target_pairs={{0,1},{1,9},{2,17},{3,25},{4,0},{5,8},{6,16},{7,24},{8,3},{9,11},{... | collective-permute-start | bytes 196616 | tf_op jit(solution)/shard_map/ppermute | solution.py:382
  8.3 18.7 %collective-permute-start.16 = (bf16[32,1024]{1,0:T(8,128)(2,1)}, bf16[32,1024]{1,0:T(8,128)(2,1)S(1)}, u32[]{:S(2)}, u32[]{:S(2)}) collective-permute-start(bf16[32,1024]{1,0:T(8,128)(2,1)} %get-tuple-element.46), channel_id=1, source_target_pairs={{0,2},{1,10},{2,18},{3,26},{4,3},{5,11},{6,19},{7,27},{8,0},{9,8},... | collective-permute-start | bytes 196616 | tf_op jit(solution)/shard_map/ppermute | solution.py:382
  11.8 15.3 %collective-permute-start.17 = (bf16[32,1024]{1,0:T(8,128)(2,1)}, bf16[32,1024]{1,0:T(8,128)(2,1)S(1)}, u32[]{:S(2)}, u32[]{:S(2)}) collective-permute-start(bf16[32,1024]{1,0:T(8,128)(2,1)} %get-tuple-element.47), channel_id=1, source_target_pairs={{0,3},{1,11},{2,19},{3,27},{4,2},{5,10},{6,18},{7,26},{8,1},{9,9},... | collective-permute-start | bytes 196616 | tf_op jit(solution)/shard_map/ppermute | solution.py:382
  15.4 11.7 %collective-permute-start.18 = (bf16[32,1024]{1,0:T(8,128)(2,1)}, bf16[32,1024]{1,0:T(8,128)(2,1)S(1)}, u32[]{:S(2)}, u32[]{:S(2)}) collective-permute-start(bf16[32,1024]{1,0:T(8,128)(2,1)} %get-tuple-element.48), channel_id=1, source_target_pairs={{0,4},{1,12},{2,20},{3,28},{4,5},{5,13},{6,21},{7,29},{8,6},{9,14}... | collective-permute-start | bytes 196616 | tf_op jit(solution)/shard_map/ppermute | solution.py:382
  16.8 10.6 %collective-permute-start.19 = (bf16[32,1024]{1,0:T(8,128)(2,1)}, bf16[32,1024]{1,0:T(8,128)(2,1)S(1)}, u32[]{:S(2)}, u32[]{:S(2)}) collective-permute-start(bf16[32,1024]{1,0:T(8,128)(2,1)} %get-tuple-element.49), channel_id=1, source_target_pairs={{0,5},{1,13},{2,21},{3,29},{4,4},{5,12},{6,20},{7,28},{8,7},{9,15}... | collective-permute-start | bytes 196616 | tf_op jit(solution)/shard_map/ppermute | solution.py:382
  18.7 12.3 %collective-permute-start.20 = (bf16[32,1024]{1,0:T(8,128)(2,1)}, bf16[32,1024]{1,0:T(8,128)(2,1)S(1)}, u32[]{:S(2)}, u32[]{:S(2)}) collective-permute-start(bf16[32,1024]{1,0:T(8,128)(2,1)} %get-tuple-element.50), channel_id=1, source_target_pairs={{0,6},{1,14},{2,22},{3,30},{4,7},{5,15},{6,23},{7,31},{8,4},{9,12}... | collective-permute-start | bytes 196616 | tf_op jit(solution)/shard_map/ppermute | solution.py:382
  27.0 7.3 %collective-permute-start.21 = (bf16[32,1024]{1,0:T(8,128)(2,1)}, bf16[32,1024]{1,0:T(8,128)(2,1)S(1)}, u32[]{:S(2)}, u32[]{:S(2)}) collective-permute-start(bf16[32,1024]{1,0:T(8,128)(2,1)} %get-tuple-element.51), channel_id=1, source_target_pairs={{0,7},{1,15},{2,23},{3,31},{4,6},{5,14},{6,22},{7,30},{8,5},{9,13}... | collective-permute-start | bytes 196616 | tf_op jit(solution)/shard_map/ppermute | solution.py:382
  34.3 36.2 %copy-start = (bf16[8,32,1024]{2,1,0:T(8,128)(2,1)}, bf16[8,32,1024]{2,1,0:T(8,128)(2,1)S(1)}, u32[]{:S(2)}) copy-start(bf16[8,32,1024]{2,1,0:T(8,128)(2,1)S(1)} %bitcast_dynamic-update-slice_fusion.rest_8_) | copy-start | bytes 1572868
  34.3 38.9 %collective-permute-start.23 = (bf16[8,32,1024]{2,1,0:T(8,128)(2,1)S(1)}, bf16[8,32,1024]{2,1,0:T(8,128)(2,1)S(1)}, u32[]{:S(2)}, u32[]{:S(2)}) collective-permute-start(bf16[8,32,1024]{2,1,0:T(8,128)(2,1)S(1)} %bitcast_dynamic-update-slice_fusion.rest_8_), channel_id=1, source_target_pairs={{0,2},{1,3},{2,0},{3,1},{4,6},{5,7},{6,4},{7,5},{8,10},{9,11},{10,... | collective-permute-start | bytes 1572872 | tf_op jit(solution)/shard_map/ppermute | solution.py:353
  50.1 16.9 %collective-permute-start.2 = (bf16[32,1024]{1,0:T(8,128)(2,1)}, bf16[32,1024]{1,0:T(8,128)(2,1)S(1)}, u32[]{:S(2)}, u32[]{:S(2)}) collective-permute-start(bf16[32,1024]{1,0:T(8,128)(2,1)} %get-tuple-element.39), channel_id=1, source_target_pairs={{0,12},{4,8},{8,4},{12,0},{16,28},{20,24},{24,20},{28,16},{1,13},{... | collective-permute-start | bytes 196616 | tf_op jit(solution)/shard_map/ppermute | solution.py:353
  50.1 18.5 %collective-permute-start.1 = (bf16[32,1024]{1,0:T(8,128)(2,1)}, bf16[32,1024]{1,0:T(8,128)(2,1)S(1)}, u32[]{:S(2)}, u32[]{:S(2)}) collective-permute-start(bf16[32,1024]{1,0:T(8,128)(2,1)} %get-tuple-element.38), channel_id=1, source_target_pairs={{0,8},{4,12},{8,0},{12,4},{16,24},{20,28},{24,16},{28,20},{1,9},{5... | collective-permute-start | bytes 196616 | tf_op jit(solution)/shard_map/ppermute | solution.py:353
  50.2 20.3 %copy-start.13 = (bf16[32,1024]{1,0:T(8,128)(2,1)S(1)}, bf16[32,1024]{1,0:T(8,128)(2,1)}, u32[]{:S(2)}) copy-start(bf16[32,1024]{1,0:T(8,128)(2,1)} %get-tuple-element.36) | copy-start | bytes 196612
  50.2 20.3 %collective-permute-start = (bf16[32,1024]{1,0:T(8,128)(2,1)}, bf16[32,1024]{1,0:T(8,128)(2,1)S(1)}, u32[]{:S(2)}, u32[]{:S(2)}) collective-permute-start(bf16[32,1024]{1,0:T(8,128)(2,1)} %get-tuple-element.37), channel_id=1, source_target_pairs={{0,4},{4,0},{8,12},{12,8},{16,20},{20,16},{24,28},{28,24},{1,5},{5... | collective-permute-start | bytes 196616 | tf_op jit(solution)/shard_map/ppermute | solution.py:353
  67.0 5.4 %collective-permute-start.9 = (bf16[32,1024]{1,0:T(8,128)(2,1)}, bf16[32,1024]{1,0:T(8,128)(2,1)S(1)}, u32[]{:S(2)}, u32[]{:S(2)}) collective-permute-start(bf16[32,1024]{1,0:T(8,128)(2,1)} %get-tuple-element.43), channel_id=1, source_target_pairs={{0,12},{4,8},{8,4},{12,0},{16,28},{20,24},{24,20},{28,16},{1,13},{... | collective-permute-start | bytes 196616 | tf_op jit(solution)/shard_map/ppermute | solution.py:353
  67.0 6.2 %collective-permute-start.8 = (bf16[32,1024]{1,0:T(8,128)(2,1)}, bf16[32,1024]{1,0:T(8,128)(2,1)S(1)}, u32[]{:S(2)}, u32[]{:S(2)}) collective-permute-start(bf16[32,1024]{1,0:T(8,128)(2,1)} %get-tuple-element.42), channel_id=1, source_target_pairs={{0,8},{4,12},{8,0},{12,4},{16,24},{20,28},{24,16},{28,20},{1,9},{5... | collective-permute-start | bytes 196616 | tf_op jit(solution)/shard_map/ppermute | solution.py:353
  68.6 4.7 %collective-permute-start.7 = (bf16[32,1024]{1,0:T(8,128)(2,1)}, bf16[32,1024]{1,0:T(8,128)(2,1)S(1)}, u32[]{:S(2)}, u32[]{:S(2)}) collective-permute-start(bf16[32,1024]{1,0:T(8,128)(2,1)} %get-tuple-element.41), channel_id=1, source_target_pairs={{0,4},{4,0},{8,12},{12,8},{16,20},{20,16},{24,28},{28,24},{1,5},{5... | collective-permute-start | bytes 196616 | tf_op jit(solution)/shard_map/ppermute | solution.py:353
  70.5 21.1 %collective-permute-start.22 = (bf16[8,32,1024]{2,1,0:T(8,128)(2,1)S(1)}, bf16[8,32,1024]{2,1,0:T(8,128)(2,1)S(1)}, u32[]{:S(2)}, u32[]{:S(2)}) collective-permute-start(bf16[8,32,1024]{2,1,0:T(8,128)(2,1)S(1)} %bitcast_dynamic-update-slice_fusion.rest_8_), channel_id=1, source_target_pairs={{0,1},{1,0},{2,3},{3,2},{4,5},{5,4},{6,7},{7,6},{8,9},{9,8},{10,11... | collective-permute-start | bytes 1572872 | tf_op jit(solution)/shard_map/ppermute | solution.py:353
  72.3 5.9 %collective-permute-start.3 = (bf16[32,1024]{1,0:T(8,128)(2,1)S(1)}, bf16[32,1024]{1,0:T(8,128)(2,1)S(1)}, u32[]{:S(2)}, u32[]{:S(2)}) collective-permute-start(bf16[32,1024]{1,0:T(8,128)(2,1)S(1)} %add_convert_fusion.3), channel_id=1, source_target_pairs={{0,16},{4,20},{8,24},{12,28},{16,0},{20,4},{24,8},{28,12},{1,17},{... | collective-permute-start | bytes 196616 | tf_op jit(solution)/shard_map/ppermute | solution.py:353
  73.2 18.3 %copy-start.1 = (bf16[8,32,1024]{2,1,0:T(8,128)(2,1)}, bf16[8,32,1024]{2,1,0:T(8,128)(2,1)S(1)}, u32[]{:S(2)}) copy-start(bf16[8,32,1024]{2,1,0:T(8,128)(2,1)S(1)} %collective-permute-done.23.rest_10_) | copy-start | bytes 1572868
  73.2 18.3 %collective-permute-start.24 = (bf16[8,32,1024]{2,1,0:T(8,128)(2,1)S(1)}, bf16[8,32,1024]{2,1,0:T(8,128)(2,1)S(1)}, u32[]{:S(2)}, u32[]{:S(2)}) collective-permute-start(bf16[8,32,1024]{2,1,0:T(8,128)(2,1)S(1)} %collective-permute-done.23.rest_10_), channel_id=1, source_target_pairs={{0,1},{1,0},{2,3},{3,2},{4,5},{5,4},{6,7},{7,6},{8,9},{9,8},{10,11... | collective-permute-start | bytes 1572872 | tf_op jit(solution)/shard_map/ppermute | solution.py:353
  74.2 6.8 %collective-permute-start.10 = (bf16[32,1024]{1,0:T(8,128)(2,1)S(1)}, bf16[32,1024]{1,0:T(8,128)(2,1)S(1)}, u32[]{:S(2)}, u32[]{:S(2)}) collective-permute-start(bf16[32,1024]{1,0:T(8,128)(2,1)S(1)} %add_convert_fusion.1), channel_id=1, source_target_pairs={{0,16},{4,20},{8,24},{12,28},{16,0},{20,4},{24,8},{28,12},{1,17},{... | collective-permute-start | bytes 196616 | tf_op jit(solution)/shard_map/ppermute | solution.py:353
  78.3 13.3 %copy-start.4 = (bf16[32,1024]{1,0:T(8,128)(2,1)}, bf16[32,1024]{1,0:T(8,128)(2,1)S(1)}, u32[]{:S(2)}) copy-start(bf16[32,1024]{1,0:T(8,128)(2,1)S(1)} %add_convert_fusion.2.rest_0_) | copy-start | bytes 196612
  78.3 4.3 %collective-permute-start.4 = (bf16[32,1024]{1,0:T(8,128)(2,1)S(1)}, bf16[32,1024]{1,0:T(8,128)(2,1)S(1)}, u32[]{:S(2)}, u32[]{:S(2)}) collective-permute-start(bf16[32,1024]{1,0:T(8,128)(2,1)S(1)} %add_convert_fusion.2.rest_0_), channel_id=1, source_target_pairs={{0,4},{4,0},{8,12},{12,8},{16,20},{20,16},{24,28},{28,24},{1,5},{5... | collective-permute-start | bytes 196616 | tf_op jit(solution)/shard_map/ppermute | solution.py:353
  78.5 4.8 %collective-permute-start.5 = (bf16[32,1024]{1,0:T(8,128)(2,1)S(1)}, bf16[32,1024]{1,0:T(8,128)(2,1)S(1)}, u32[]{:S(2)}, u32[]{:S(2)}) collective-permute-start(bf16[32,1024]{1,0:T(8,128)(2,1)S(1)} %add_convert_fusion.2.rest_0_), channel_id=1, source_target_pairs={{0,8},{4,12},{8,0},{12,4},{16,24},{20,28},{24,16},{28,20},{1,9},{5... | collective-permute-start | bytes 196616 | tf_op jit(solution)/shard_map/ppermute | solution.py:353
  81.0 5.4 %collective-permute-start.6 = (bf16[32,1024]{1,0:T(8,128)(2,1)S(1)}, bf16[32,1024]{1,0:T(8,128)(2,1)S(1)}, u32[]{:S(2)}, u32[]{:S(2)}) collective-permute-start(bf16[32,1024]{1,0:T(8,128)(2,1)S(1)} %add_convert_fusion.2.rest_0_), channel_id=1, source_target_pairs={{0,12},{4,8},{8,4},{12,0},{16,28},{20,24},{24,20},{28,16},{1,13},{... | collective-permute-start | bytes 196616 | tf_op jit(solution)/shard_map/ppermute | solution.py:353
  82.4 9.2 %copy-start.5 = (bf16[32,1024]{1,0:T(8,128)(2,1)}, bf16[32,1024]{1,0:T(8,128)(2,1)S(1)}, u32[]{:S(2)}) copy-start(bf16[32,1024]{1,0:T(8,128)(2,1)S(1)} %add_convert_fusion.rest_4_) | copy-start | bytes 196612
  82.6 9.0 %copy-start.6 = (bf16[32,1024]{1,0:T(8,128)(2,1)}, bf16[32,1024]{1,0:T(8,128)(2,1)S(1)}, u32[]{:S(2)}) copy-start(bf16[32,1024]{1,0:T(8,128)(2,1)S(1)} %collective-permute-done.4.rest_1_) | copy-start | bytes 196612
  82.6 5.3 %collective-permute-start.11 = (bf16[32,1024]{1,0:T(8,128)(2,1)S(1)}, bf16[32,1024]{1,0:T(8,128)(2,1)S(1)}, u32[]{:S(2)}, u32[]{:S(2)}) collective-permute-start(bf16[32,1024]{1,0:T(8,128)(2,1)S(1)} %add_convert_fusion.rest_4_), channel_id=1, source_target_pairs={{0,4},{4,0},{8,12},{12,8},{16,20},{20,16},{24,28},{28,24},{1,5},{5... | collective-permute-start | bytes 196616 | tf_op jit(solution)/shard_map/ppermute | solution.py:353
  83.3 8.3 %copy-start.7 = (bf16[32,1024]{1,0:T(8,128)(2,1)}, bf16[32,1024]{1,0:T(8,128)(2,1)S(1)}, u32[]{:S(2)}) copy-start(bf16[32,1024]{1,0:T(8,128)(2,1)S(1)} %collective-permute-done.5.rest_2_) | copy-start | bytes 196612
  83.3 4.6 %collective-permute-start.12 = (bf16[32,1024]{1,0:T(8,128)(2,1)S(1)}, bf16[32,1024]{1,0:T(8,128)(2,1)S(1)}, u32[]{:S(2)}, u32[]{:S(2)}) collective-permute-start(bf16[32,1024]{1,0:T(8,128)(2,1)S(1)} %add_convert_fusion.rest_4_), channel_id=1, source_target_pairs={{0,8},{4,12},{8,0},{12,4},{16,24},{20,28},{24,16},{28,20},{1,9},{5... | collective-permute-start | bytes 196616 | tf_op jit(solution)/shard_map/ppermute | solution.py:353
  86.4 5.2 %copy-start.8 = (bf16[32,1024]{1,0:T(8,128)(2,1)}, bf16[32,1024]{1,0:T(8,128)(2,1)S(1)}, u32[]{:S(2)}) copy-start(bf16[32,1024]{1,0:T(8,128)(2,1)S(1)} %collective-permute-done.6.rest_3_) | copy-start | bytes 196612
  86.4 5.2 %collective-permute-start.13 = (bf16[32,1024]{1,0:T(8,128)(2,1)S(1)}, bf16[32,1024]{1,0:T(8,128)(2,1)S(1)}, u32[]{:S(2)}, u32[]{:S(2)}) collective-permute-start(bf16[32,1024]{1,0:T(8,128)(2,1)S(1)} %add_convert_fusion.rest_4_), channel_id=1, source_target_pairs={{0,12},{4,8},{8,4},{12,0},{16,28},{20,24},{24,20},{28,16},{1,13},{... | collective-permute-start | bytes 196616 | tf_op jit(solution)/shard_map/ppermute | solution.py:353
  87.9 3.7 %copy-start.9 = (bf16[32,1024]{1,0:T(8,128)(2,1)}, bf16[32,1024]{1,0:T(8,128)(2,1)S(1)}, u32[]{:S(2)}) copy-start(bf16[32,1024]{1,0:T(8,128)(2,1)S(1)} %collective-permute-done.11.rest_5_) | copy-start | bytes 196612
  87.9 3.7 %copy-start.10 = (bf16[32,1024]{1,0:T(8,128)(2,1)}, bf16[32,1024]{1,0:T(8,128)(2,1)S(1)}, u32[]{:S(2)}) copy-start(bf16[32,1024]{1,0:T(8,128)(2,1)S(1)} %collective-permute-done.12.rest_6_) | copy-start | bytes 196612
  91.5 0.6 copy-start.11
  91.6 0.8 copy-start.2
  92.4 0.8 copy-start.3
  100.5 8.4 %collective-permute-start.31 = (bf16[128,256]{1,0:T(8,128)(2,1)}, bf16[128,256]{1,0:T(8,128)(2,1)S(1)}, u32[]{:S(2)}, u32[]{:S(2)}) collective-permute-start(bf16[128,256]{1,0:T(8,128)(2,1)} %get-tuple-element.60), channel_id=1, source_target_pairs={{0,28},{4,24},{8,20},{12,16},{16,12},{20,8},{24,4},{28,0},{1,29},{... | collective-permute-start | bytes 196616 | tf_op jit(solution)/shard_map/ppermute | solution.py:353
  103.6 7.4 %collective-permute-start.30 = (bf16[128,256]{1,0:T(8,128)(2,1)}, bf16[128,256]{1,0:T(8,128)(2,1)S(1)}, u32[]{:S(2)}, u32[]{:S(2)}) collective-permute-start(bf16[128,256]{1,0:T(8,128)(2,1)} %get-tuple-element.59), channel_id=1, source_target_pairs={{0,24},{4,28},{8,16},{12,20},{16,8},{20,12},{24,0},{28,4},{1,25},{... | collective-permute-start | bytes 196616 | tf_op jit(solution)/shard_map/ppermute | solution.py:353
  105.2 30.9 %collective-permute-start.29 = (bf16[128,256]{1,0:T(8,128)(2,1)}, bf16[128,256]{1,0:T(8,128)(2,1)S(1)}, u32[]{:S(2)}, u32[]{:S(2)}) collective-permute-start(bf16[128,256]{1,0:T(8,128)(2,1)} %get-tuple-element.58), channel_id=1, source_target_pairs={{0,20},{4,16},{8,28},{12,24},{16,4},{20,0},{24,12},{28,8},{1,21},{... | collective-permute-start | bytes 196616 | tf_op jit(solution)/shard_map/ppermute | solution.py:353
  106.3 29.7 %collective-permute-start.28 = (bf16[128,256]{1,0:T(8,128)(2,1)}, bf16[128,256]{1,0:T(8,128)(2,1)S(1)}, u32[]{:S(2)}, u32[]{:S(2)}) collective-permute-start(bf16[128,256]{1,0:T(8,128)(2,1)} %get-tuple-element.57), channel_id=1, source_target_pairs={{0,16},{4,20},{8,24},{12,28},{16,0},{20,4},{24,8},{28,12},{1,17},{... | collective-permute-start | bytes 196616 | tf_op jit(solution)/shard_map/ppermute | solution.py:353
  108.2 27.9 %collective-permute-start.27 = (bf16[128,256]{1,0:T(8,128)(2,1)}, bf16[128,256]{1,0:T(8,128)(2,1)S(1)}, u32[]{:S(2)}, u32[]{:S(2)}) collective-permute-start(bf16[128,256]{1,0:T(8,128)(2,1)} %get-tuple-element.56), channel_id=1, source_target_pairs={{0,12},{4,8},{8,4},{12,0},{16,28},{20,24},{24,20},{28,16},{1,13},{... | collective-permute-start | bytes 196616 | tf_op jit(solution)/shard_map/ppermute | solution.py:353
  108.9 27.2 %collective-permute-start.26 = (bf16[128,256]{1,0:T(8,128)(2,1)}, bf16[128,256]{1,0:T(8,128)(2,1)S(1)}, u32[]{:S(2)}, u32[]{:S(2)}) collective-permute-start(bf16[128,256]{1,0:T(8,128)(2,1)} %get-tuple-element.55), channel_id=1, source_target_pairs={{0,8},{4,12},{8,0},{12,4},{16,24},{20,28},{24,16},{28,20},{1,9},{5... | collective-permute-start | bytes 196616 | tf_op jit(solution)/shard_map/ppermute | solution.py:353
  111.0 25.1 %collective-permute-start.25 = (bf16[128,256]{1,0:T(8,128)(2,1)}, bf16[128,256]{1,0:T(8,128)(2,1)S(1)}, u32[]{:S(2)}, u32[]{:S(2)}) collective-permute-start(bf16[128,256]{1,0:T(8,128)(2,1)} %get-tuple-element.54), channel_id=1, source_target_pairs={{0,4},{4,0},{8,12},{12,8},{16,20},{20,16},{24,28},{28,24},{1,5},{5... | collective-permute-start | bytes 196616 | tf_op jit(solution)/shard_map/ppermute | solution.py:353
  123.8 12.3 %copy-start.12 = (bf16[128,256]{1,0:T(8,128)(2,1)S(1)}, bf16[128,256]{1,0:T(8,128)(2,1)}, u32[]{:S(2)}) copy-start(bf16[128,256]{1,0:T(8,128)(2,1)} %get-tuple-element.53) | copy-start | bytes 196612

commit v2 on v1

v2 whole, which is shorter than its diff:
```python
import math

import jax
import jax.numpy as jnp
from jax import lax
from jax.experimental import pallas as pl
from jax.experimental.pallas import tpu as pltpu
from jax.sharding import PartitionSpec as P


momentum_decay = 0.9
step_rate = 1.0
fine_rows = 64
forward_tile = 1024
flip_rows = 128
f32 = jnp.float32
bf16 = jnp.bfloat16


def wrap(phase, period):
    return phase & (period - 1) if period & (period - 1) == 0 else phase % period


def sine_cosine(phase, model_width):
    shifted = phase + model_width // 2
    if model_width & (model_width - 1) == 0:
        quarter = shifted >> (model_width.bit_length() - 1)
    else:
        quarter = shifted // model_width
    x = (phase - quarter * model_width).astype(f32) * (math.pi / (2 * model_width))
    z = x * x
    sine = x + x * z * (-1.6666654611e-1 + z * (8.3321608736e-3 + z * -1.9515295891e-4))
    cosine = 1.0 - 0.5 * z + z * z * (
        4.166664568298827e-2 + z * (-1.388731625493765e-3 + z * 2.443315711809948e-5)
    )
    swapped = (quarter & 1) == 1
    cos_sign = (1 - ((quarter + 1) & 2)).astype(f32)
    sin_sign = (1 - (quarter & 2)).astype(f32)
    return (
        cos_sign * jnp.where(swapped, sine, cosine),
        sin_sign * jnp.where(swapped, cosine, sine),
    )


def fill_tables(frequency, coarse_cos, coarse_sin, fine_cos, fine_sin, model_width):
    freqs = frequency.shape[1]
    digit = lax.broadcasted_iota(jnp.int32, (8, freqs), 0)
    scale = jnp.where(
        frequency == 0, math.sqrt(1.0 / model_width), math.sqrt(2.0 / model_width)
    ).astype(f32)

    def angles(multiplier):
        return sine_cosine(wrap(multiplier * frequency, 4 * model_width), model_width)

    def combine(high, low, cos_ref, sin_ref):
        for k in range(cos_ref.shape[0] // 8):
            rows = pl.ds(8 * k, 8)
            cosine, sine = high[0][k : k + 1], high[1][k : k + 1]
            cos_ref[rows, :] = cosine * low[0] - sine * low[1]
            sin_ref[rows, :] = sine * low[0] + cosine * low[1]

    cosine, sine = angles(2 * fine_rows * digit)
    combine(
        angles(16 * fine_rows * digit), (cosine * scale, sine * scale), coarse_cos, coarse_sin
    )
    combine(angles(16 * digit), angles(2 * digit + 1), fine_cos, fine_sin)


def fill_cosines(target, first_coarse, count, coarse_cos, coarse_sin, fine_cos, fine_sin):
    for lane in range(0, target.shape[1], 128):
        lanes = pl.ds(lane, 128)
        cosine = fine_cos[:, lanes]
        sine = fine_sin[:, lanes]
        coarse_c = coarse_cos[pl.ds(first_coarse, count), lanes]
        coarse_s = coarse_sin[pl.ds(first_coarse, count), lanes]
        for k in range(count):
            target[pl.ds(k * fine_rows, fine_rows), lanes] = (
                coarse_c[k : k + 1] * cosine - coarse_s[k : k + 1] * sine
            ).astype(bf16)


def reversal():
    rows = lax.broadcasted_iota(jnp.int32, (flip_rows, flip_rows), 0)
    cols = lax.broadcasted_iota(jnp.int32, (flip_rows, flip_rows), 1)
    return jnp.where(rows + cols == flip_rows - 1, 1.0, 0.0).astype(bf16)


def flip_low(value):
    flips = reversal()
    pieces = [
        jnp.dot(flips, value[lower : lower + flip_rows], preferred_element_type=f32)
        for lower in range(value.shape[0] - flip_rows, -1, -flip_rows)
    ]
    return jnp.concatenate(pieces, axis=0)


def flip_wide(value):
    high = value.astype(bf16)
    low = (value - high.astype(f32)).astype(bf16)
    return flip_low(high) + flip_low(low)


def parity_sign(frequency):
    return (1 - 2 * (frequency & 1)).astype(f32)


def dot_tn(a, b):
    return lax.dot_general(a, b, (((0,), (0,)), ((), ())), preferred_element_type=f32)


def dot_nt(a, b):
    return lax.dot_general(a, b, (((1,), (1,)), ((), ())), preferred_element_type=f32)


def forward(momentum, gradient, freq_rows, meta, group):
    model_width = momentum.shape[1]
    blocks, _, freqs = freq_rows.shape
    cols = momentum.shape[2]
    block_cols = cols // blocks
    half = model_width // 2
    tile = min(forward_tile, half)
    steps = half // tile
    piece = cols // group

    def kernel(meta_ref, freq, mom_a, mom_b, grad_a, grad_b, coeff, *rest):
        pieces = rest[:group]
        table, total, coarse_cos, coarse_sin, fine_cos, fine_sin = rest[group:]
        block, step = pl.program_id(0), pl.program_id(1)
        frequency = freq[0]

        @pl.when(step == 0)
        def _():
            fill_tables(frequency, coarse_cos, coarse_sin, fine_cos, fine_sin, model_width)

        fill_cosines(
            table, pl.multiple_of(step * (tile // fine_rows), tile // fine_rows),
            tile // fine_rows, coarse_cos, coarse_sin, fine_cos, fine_sin,
        )
        low_a = (momentum_decay * mom_a[0] + grad_a[0].astype(f32)).astype(bf16)
        low_b = (momentum_decay * mom_b[0] + grad_b[0].astype(f32)).astype(bf16)
        both = jnp.concatenate([low_a, flip_low(low_b).astype(bf16)], axis=1)
        partial = dot_tn(both, table[...])

        @pl.when(step == 0)
        def _():
            total[...] = partial

        @pl.when(step > 0)
        def _():
            total[...] += partial

        @pl.when(step == steps - 1)
        def _():
            rows = pl.ds(pl.multiple_of(block * block_cols, block_cols), block_cols)
            coeff[rows, :] = (
                total[:block_cols] + parity_sign(frequency) * total[block_cols:]
            ).astype(bf16)

        @pl.when((step == steps - 1) & (block == blocks - 1))
        def _():
            for k in range(group):
                start = ((meta_ref[0] % group) ^ k) * piece
                pieces[k][...] = coeff[pl.ds(pl.multiple_of(start, piece), piece), :]

    def rows(which):
        def index(block, step, meta_ref):
            return (0, 2 * steps - 1 - step if which else step, block)

        return pl.BlockSpec((1, tile, block_cols), index)

    whole = lambda block, step, meta_ref: (0, 0)
    return pl.pallas_call(
        kernel,
        name="forward",
        grid_spec=pltpu.PrefetchScalarGridSpec(
            num_scalar_prefetch=1,
            grid=(blocks, steps),
            in_specs=[
                pl.BlockSpec((1, 1, freqs), lambda block, step, meta_ref: (block, 0, 0)),
                rows(0), rows(1), rows(0), rows(1),
            ],
            out_specs=[pl.BlockSpec((cols, freqs), whole)]
            + [pl.BlockSpec((piece, freqs), whole)] * group
            + [pl.BlockSpec(
                (tile, freqs), lambda block, step, meta_ref: (block * steps + step, 0)
            )],
            scratch_shapes=[pltpu.VMEM((2 * block_cols, freqs), f32)]
            + [pltpu.VMEM((half // fine_rows, freqs), f32)] * 2
            + [pltpu.VMEM((fine_rows, freqs), f32)] * 2,
        ),
        out_shape=[jax.ShapeDtypeStruct((cols, freqs), bf16)]
        + [jax.ShapeDtypeStruct((piece, freqs), bf16)] * group
        + [jax.ShapeDtypeStruct((blocks * half, freqs), bf16)],
    )(meta, freq_rows, momentum, momentum, gradient, gradient)


def remain(part, parts, momentum, gradient, freq_rows, coeff, table, previous):
    model_width = momentum.shape[1]
    block_cols = momentum.shape[2] // freq_rows.shape[0]
    freqs = freq_rows.shape[2]
    half = model_width // 2
    tile = min(512, half)
    all_steps = half // tile
    blocks = freq_rows.shape[0]
    column_block = part * blocks // parts
    steps = all_steps * blocks // parts
    first = part * steps - column_block * all_steps

    def kernel(freq, mom_a, mom_b, grad_a, grad_b, coeff_ref, table_ref, *rest):
        residual, both, buffer, sems = rest[-4:]
        step = pl.program_id(0)
        slot = step % 2

        def copies(at, where):
            lanes = pl.ds(column_block * block_cols, block_cols)
            return [
                pltpu.make_async_copy(
                    buffer.at[where, k], residual.at[0, pl.ds(start * tile, tile), lanes],
                    sems.at[where, k],
                )
                for k, start in enumerate((first + at, 2 * all_steps - 1 - first - at))
            ]

        @pl.when(step == 0)
        def _():
            both[:block_cols] = coeff_ref[...]
            both[block_cols:] = (coeff_ref[...].astype(f32) * parity_sign(freq[0])).astype(bf16)

        back = dot_nt(table_ref[...], both[...])

        @pl.when(step >= 2)
        def _():
            for copy in copies(step - 2, slot):
                copy.wait()

        buffer[slot, 0] = (
            momentum_decay * mom_a[0] + grad_a[0].astype(f32) - back[:, :block_cols]
        )
        buffer[slot, 1] = (
            momentum_decay * mom_b[0] + grad_b[0].astype(f32) - flip_wide(back[:, block_cols:])
        )
        for copy in copies(step, slot):
            copy.start()

        @pl.when(step == steps - 1)
        def _():
            if steps > 1:
                for copy in copies(step - 1, 1 - slot):
                    copy.wait()
            for copy in copies(step, slot):
                copy.wait()

    def rows(which):
        def index(step):
            at = first + step
            return (0, 2 * all_steps - 1 - at if which else at, column_block)

        return pl.BlockSpec((1, tile, block_cols), index)

    operands = [freq_rows, momentum, momentum, gradient, gradient, coeff, table]
    specs = [
        pl.BlockSpec((1, 1, freqs), lambda step: (column_block, 0, 0)),
        rows(0), rows(1), rows(0), rows(1),
        pl.BlockSpec((block_cols, freqs), lambda step: (column_block, 0)),
        pl.BlockSpec(
            (tile, freqs), lambda step: (column_block * all_steps + first + step, 0)
        ),
    ]
    aliases = {}
    if previous is not None:
        aliases = {len(operands): 0}
        operands.append(previous)
        specs.append(pl.BlockSpec(memory_space=pl.ANY))
    return pl.pallas_call(
        kernel,
        grid=(steps,),
        in_specs=specs,
        out_specs=pl.BlockSpec(memory_space=pl.ANY),
        scratch_shapes=[
            pltpu.VMEM((2 * block_cols, freqs), bf16),
            pltpu.VMEM((2, 2, tile, block_cols), f32),
            pltpu.SemaphoreType.DMA((2, 2)),
        ],
        out_shape=jax.ShapeDtypeStruct(momentum.shape, f32),
        input_output_aliases=aliases,
    )(*operands)


def apply(masters, freq_rows, table, means, features, meta, dp, tensor, group):
    own_rows, cols = masters.shape
    blocks, _, freqs = freq_rows.shape
    block_cols = cols // blocks
    piece = cols // group
    ratio, token_rows, _ = features[0].shape
    half_parts = table.shape[0] // blocks // own_rows
    crosses = dp // group

    def kernel(meta_ref, freq, masters_ref, *rest):
        tables = rest[:blocks]
        mean_refs = rest[blocks : blocks + group]
        feature_refs = rest[blocks + group : blocks + group + tensor]
        new_ref, *outs, mean, weights, products = rest[blocks + group + tensor :]
        device, rank = meta_ref[0], meta_ref[1]
        mirrored = device >= half_parts
        for k in range(group):
            start = ((device % group) ^ k) * piece
            mean[pl.ds(pl.multiple_of(start, piece), piece), :] = mean_refs[k][...]
        for block in range(blocks):
            sign = jnp.where(mirrored, parity_sign(freq[block]), 1.0)
            lanes = pl.ds(block * block_cols, block_cols)
            own = (mean[lanes, :].astype(f32) * sign).astype(bf16)
            update = dot_nt(tables[block][...], own) * (1.0 / dp)

            @pl.when(mirrored)
            def _():
                new_ref[:, lanes] = masters_ref[:, lanes] - step_rate * flip_wide(update)

            @pl.when(jnp.logical_not(mirrored))
            def _():
                new_ref[:, lanes] = masters_ref[:, lanes] - step_rate * update

        weights[...] = new_ref[...].astype(bf16)
        for other in range(tensor):
            for k in range(ratio):
                target = (rank ^ other) * ratio + ((device % ratio) ^ k)
                products[target ^ device] = jnp.dot(
                    feature_refs[other][k], weights[...], preferred_element_type=f32
                ).astype(bf16)
        for k in range(group):
            for cross in range(crosses):
                outs[k][cross] = products[cross * group + k]

    def whole(*shape):
        return pl.BlockSpec(shape, lambda step, meta_ref: (0,) * len(shape))

    def own_table(block):
        def index(step, meta_ref):
            device = meta_ref[0]
            row = jnp.where(device >= half_parts, 2 * half_parts - 1 - device, device)
            return (block * half_parts + row, 0)

        return pl.BlockSpec((own_rows, freqs), index)

    return pl.pallas_call(
        kernel,
        name="apply",
        grid_spec=pltpu.PrefetchScalarGridSpec(
            num_scalar_prefetch=1,
            grid=(1,),
            in_specs=[whole(*freq_rows.shape), whole(own_rows, cols)]
            + [own_table(block) for block in range(blocks)]
            + [whole(piece, freqs)] * group
            + [whole(*features[0].shape)] * tensor,
            out_specs=[whole(own_rows, cols)] + [whole(crosses, token_rows, cols)] * group,
            scratch_shapes=[
                pltpu.VMEM((cols, freqs), bf16),
                pltpu.VMEM((own_rows, cols), bf16),
                pltpu.VMEM((dp, token_rows, cols), bf16),
            ],
        ),
        out_shape=[jax.ShapeDtypeStruct((own_rows, cols), f32)]
        + [jax.ShapeDtypeStruct((crosses, token_rows, cols), bf16)] * group,
    )(meta, freq_rows, masters, *[table] * blocks, *means, *features)


def swap(value, axis, mask, size):
    return lax.ppermute(value, axis, [(k, k ^ mask) for k in range(size)])


def sum_low(values):
    total = values[0].astype(f32)
    for value in values[1:]:
        total = total + value.astype(f32)
    return total.astype(bf16)


def step(momentum, gradient, masters, tokens, freq_index):
    dp, tensor = lax.axis_size("dp"), lax.axis_size("tensor")
    group = min(4, dp)
    ratio = dp // tensor
    model_width = momentum.shape[1]
    device, rank = lax.axis_index("dp"), lax.axis_index("tensor")
    meta = jnp.stack([device, rank]).astype(jnp.int32)
    freq_rows = freq_index[:, None, :]

    pairs = [
        ((J * ratio + h) * tensor + j, (j * ratio + h) * tensor + J)
        for J in range(tensor) for h in range(ratio) for j in range(tensor)
    ]
    traded = lax.ppermute(tokens, ("dp", "tensor"), pairs)
    width = tokens.shape[1] // ratio

    coeff, *pieces, table = forward(momentum, gradient, freq_rows, meta, group)

    def feature_piece(k):
        start = ((device % ratio) ^ k) * width
        return lax.dynamic_slice_in_dim(traded, start, width, axis=1)

    parts = [feature_piece(0)]
    for k in range(1, ratio):
        parts.append(swap(feature_piece(k), "dp", k, dp))
    first = [swap(pieces[k], "dp", k, dp) for k in range(1, group)]

    residual = None
    remain_parts = 4

    def next_remain(part, residual):
        return remain(
            part, remain_parts, momentum, gradient, freq_rows, coeff, table, residual
        )

    residual = next_remain(0, residual)
    features = {0: jnp.stack(parts)}
    mask = tensor // 2
    while mask > 0:
        for held in sorted(features):
            features[held ^ mask] = swap(features[held], "tensor", mask, tensor)
        mask //= 2
    summed = sum_low([pieces[0]] + first)
    summed = sum_low([summed] + [swap(summed, "dp", k * group, dp) for k in range(1, dp // group)])
    residual = next_remain(1, residual)
    means = [summed] + [swap(summed, "dp", k, dp) for k in range(1, group)]
    residual = next_remain(2, residual)
    new_masters, *partials = apply(
        masters, freq_rows, table, means, [features[k] for k in range(tensor)], meta, dp, tensor,
        group,
    )
    received = [swap(partials[k], "dp", k, dp) for k in range(1, group)]
    residual = next_remain(3, residual)
    part = partials[0].astype(f32)
    for value in received:
        part = part + value.astype(f32)
    part_low = part.astype(bf16)
    total = part[0]
    for k in range(1, dp // group):
        total = total + swap(part_low[k], "dp", k * group, dp).astype(f32)
    projected = (total * model_width ** (-0.5)).astype(bf16)
    return (residual, new_masters, projected)


def solution(mesh):
    return jax.shard_map(
        step,
        mesh=mesh,
        in_specs=(
            P("dp", None, "tensor"),
            P("dp", None, "tensor"),
            P("dp", "tensor"),
            P("dp", "tensor"),
            P("tensor", None),
        ),
        out_specs=(P("dp", None, "tensor"), P("dp", "tensor"), P("dp", "tensor")),
        check_vma=False,
    )
```

time: 138 us -> 134 us (0.971)
  Pallas kernels: 60.3 us -> 53 us
  waiting for transfers between devices: 19.2 us -> 24.2 us
    ppermute x8 -> x1, starting transfers between devices: 23.8 us -> 1.7 us  [step(): traded = lax.ppermute(tokens, ('dp', 'tensor'), pairs)]
    ppermute x24 -> x15, starting transfers between devices: 27.1 us -> 48.2 us  [swap(): return lax.ppermute(value, axis, [(k, k ^ mask) for k in range(size)])]
    ppermute x24 -> x15, waiting for transfers between devices: 12.1 us -> 24.2 us  [swap(): return lax.ppermute(value, axis, [(k, k ^ mask) for k in range(size)])]
    pallas_call x6, Pallas kernels: 60.3 us -> 53 us  [the longest x4 27.7 us: remain(): pl.pallas_call(kernel, grid=(steps,), in_specs=specs, out_specs=pl.BlockS...]
    ppermute x8 -> x1, waiting for transfers between devices: 7.15 us -> 0.01 us  [step(): traded = lax.ppermute(tokens, ('dp', 'tensor'), pairs)]
  transfers between devices with their start and end apart: 32 -> 16, of which waited for: 10 -> 11; matrix products, arithmetic and copies ran while one was open for 2% -> 2% of each run, Pallas kernels for 37% -> 34%
where the time goes in v2:
time: 134 us; the launch traced here: 133 us
  Pallas kernels  53 us (40%)
  starting transfers between devices  49.9 us (37%)
  waiting for transfers between devices  24.2 us (18%)
  other arithmetic  3.24 us (2%)
  local copies, waits for them, and re-layouts  2.33 us (2%)
    ppermute x15, starting transfers between devices, swap(): return lax.ppermute(value, axis, [(k, k ^ mask) for k in range(size)])  48.2 us
    pallas_call x4, Pallas kernels, remain(): pl.pallas_call(kernel, grid=(steps,), in_specs=specs, out_specs=pl.BlockS...  27.7 us
    ppermute x15, waiting for transfers between devices, swap(): return lax.ppermute(value, axis, [(k, k ^ mask) for k in range(size)])  24.2 us
    pallas_call x1, Pallas kernels, forward(): pl.pallas_call(kernel, name='forward', grid_spec=pltpu.PrefetchScalarGrid...  18.3 us
    pallas_call x1, Pallas kernels, apply(): pl.pallas_call(kernel, name='apply', grid_spec=pltpu.PrefetchScalarGridSp...  6.99 us
  transfers between devices with their start and end apart: 16, of which 11 were waited for; matrix products, arithmetic and copies ran while one was open for 2% of the time, Pallas kernels for 34%

profile of v2, /device:TPU:0, one launch (start us, length us, event | category | flops | bytes accessed | tf_op | source)
XLA Modules:
  0.0 133.5 jit_solution(11404069959990623092)
XLA Ops:
  0.6 1.7 %collective-permute-start.7 = (bf16[128,2048]{1,0:T(8,128)(2,1)}, bf16[128,2048]{1,0:T(8,128)(2,1)S(1)}, u32[]{:S(2)}, u32[]{:S(2)}) collective-permute-start(bf16[128,2048]{1,0:T(8,128)(2,1)} %param.8), channel_id=1, source_target_pairs={{0,0},{1,8},{2,16},{3,24},{4,4},{5,12},{6,20},{7,28},{8,1},{9,9},{... | collective-permute-start | bytes 1572872 | tf_op jit(solution)/shard_map/ppermute | solution.py:390
  2.3 0.0 collective-permute-done.7
  2.4 3.0 %collective-permute-start.8 = (bf16[128,1024]{1,0:T(8,128)(2,1)S(1)}, bf16[128,1024]{1,0:T(8,128)(2,1)S(1)}, u32[]{:S(2)}, u32[]{:S(2)}) collective-permute-start(bf16[128,1024]{1,0:T(8,128)(2,1)S(1)} %get-tuple-element.26), channel_id=1, source_target_pairs={{0,4},{4,0},{8,12},{12,8},{16,20},{20,16},{24,28},{28,24},{1,5},{5... | collective-permute-start | bytes 786440 | tf_op jit(solution)/shard_map/ppermute | solution.py:367
  5.4 4.4 %collective-permute-done.8 = bf16[128,1024]{1,0:T(8,128)(2,1)S(1)} collective-permute-done((bf16[128,1024]{1,0:T(8,128)(2,1)S(1)}, bf16[128,1024]{1,0:T(8,128)(2,1)S(1)}, u32[]{:S(2)}, u32[]{:S(2)}) %collective-permute-start.8) | collective-permute-done | bytes 262176 | tf_op jit(solution)/shard_map/ppermute | solution.py:367
  9.8 0.1 pad_maximum_fusion.rest_6_
  9.8 0.0 copy-start
  9.8 30.0 %collective-permute-start.10 = (bf16[2,128,1024]{2,1,0:T(8,128)(2,1)S(1)}, bf16[2,128,1024]{2,1,0:T(8,128)(2,1)S(1)}, u32[]{:S(2)}, u32[]{:S(2)}) collective-permute-start(bf16[2,128,1024]{2,1,0:T(8,128)(2,1)S(1)} %pad_maximum_fusion.rest_6_), channel_id=1, source_target_pairs={{0,2},{1,3},{2,0},{3,1},{4,6},{5,7},{6,4},{7,5},{8,10},{9,11},{10,... | collective-permute-start | bytes 1572872 | tf_op jit(solution)/shard_map/ppermute | solution.py:367
  39.8 1.3 broadcast_in_dim.3.freq
  41.1 0.6 pad_add_fusion.meta_ref
  41.7 18.3 %forward.1 = (bf16[256,1024]{1,0:T(8,128)(2,1)}, bf16[64,1024]{1,0:T(8,128)(2,1)}, bf16[64,1024]{1,0:T(8,128)(2,1)}, bf16[64,1024]{1,0:T(8,128)(2,1)}, bf16[64,1...) custom-call(s32[2]{0:T(128)} %pad_add_fusion.meta_ref, s32[2,1,1024]{2,1,0:T(1,128)} %broadcast_in_dim.3.freq, ...), custom_call_target="tpu_custom_call" | custom-call | tf_op jit(solution)/shard_map/forward/pallas_call | solution.py:172
  59.9 1.6 %collective-permute-start.2 = (bf16[64,1024]{1,0:T(8,128)(2,1)}, bf16[64,1024]{1,0:T(8,128)(2,1)S(1)}, u32[]{:S(2)}, u32[]{:S(2)}) collective-permute-start(bf16[64,1024]{1,0:T(8,128)(2,1)} %get-tuple-element.19), channel_id=1, source_target_pairs={{0,12},{4,8},{8,4},{12,0},{16,28},{20,24},{24,20},{28,16},{1,13},{... | collective-permute-start | bytes 393224 | tf_op jit(solution)/shard_map/ppermute | solution.py:367
  61.6 1.3 %collective-permute-start.1 = (bf16[64,1024]{1,0:T(8,128)(2,1)}, bf16[64,1024]{1,0:T(8,128)(2,1)S(1)}, u32[]{:S(2)}, u32[]{:S(2)}) collective-permute-start(bf16[64,1024]{1,0:T(8,128)(2,1)} %get-tuple-element.18), channel_id=1, source_target_pairs={{0,8},{4,12},{8,0},{12,4},{16,24},{20,28},{24,16},{28,20},{1,9},{5... | collective-permute-start | bytes 393224 | tf_op jit(solution)/shard_map/ppermute | solution.py:367
  62.9 0.5 collective-permute-start
  63.4 0.0 copy-done
  63.4 0.0 collective-permute-start.9
  63.4 0.0 collective-permute-done.10.rest_8_
  63.4 0.0 copy-start.1
  63.5 0.5 collective-permute-start.11
  64.0 2.1 %collective-permute-done.2 = bf16[64,1024]{1,0:T(8,128)(2,1)S(1)} collective-permute-done((bf16[64,1024]{1,0:T(8,128)(2,1)}, bf16[64,1024]{1,0:T(8,128)(2,1)S(1)}, u32[]{:S(2)}, u32[]{:S(2)}) %collective-permute-start.2) | collective-permute-done | bytes 131104 | tf_op jit(solution)/shard_map/ppermute | solution.py:367
  66.0 1.4 %collective-permute-done.1 = bf16[64,1024]{1,0:T(8,128)(2,1)S(1)} collective-permute-done((bf16[64,1024]{1,0:T(8,128)(2,1)}, bf16[64,1024]{1,0:T(8,128)(2,1)S(1)}, u32[]{:S(2)}, u32[]{:S(2)}) %collective-permute-start.1) | collective-permute-done | bytes 131104 | tf_op jit(solution)/shard_map/ppermute | solution.py:367
  67.5 0.6 collective-permute-done
  68.1 1.0 add_convert_fusion.1
  69.1 2.1 %collective-permute-start.3 = (bf16[64,1024]{1,0:T(8,128)(2,1)S(1)}, bf16[64,1024]{1,0:T(8,128)(2,1)S(1)}, u32[]{:S(2)}, u32[]{:S(2)}) collective-permute-start(bf16[64,1024]{1,0:T(8,128)(2,1)S(1)} %add_convert_fusion.1), channel_id=1, source_target_pairs={{0,16},{4,20},{8,24},{12,28},{16,0},{20,4},{24,8},{28,12},{1,17},{... | collective-permute-start | bytes 393224 | tf_op jit(solution)/shard_map/ppermute | solution.py:367
  71.1 6.1 %collective-permute-done.3 = bf16[64,1024]{1,0:T(8,128)(2,1)S(1)} collective-permute-done((bf16[64,1024]{1,0:T(8,128)(2,1)S(1)}, bf16[64,1024]{1,0:T(8,128)(2,1)S(1)}, u32[]{:S(2)}, u32[]{:S(2)}) %collective-permute-start.3) | collective-permute-done | bytes 131104 | tf_op jit(solution)/shard_map/ppermute | solution.py:367
  77.2 0.0 copy-start.4
  77.3 1.0 collective-permute-start.4
  78.3 0.0 collective-permute-start.5
  78.3 2.5 %collective-permute-start.6 = (bf16[64,1024]{1,0:T(8,128)(2,1)S(1)}, bf16[64,1024]{1,0:T(8,128)(2,1)S(1)}, u32[]{:S(2)}, u32[]{:S(2)}) collective-permute-start(bf16[64,1024]{1,0:T(8,128)(2,1)S(1)} %add_convert_fusion.rest_2_), channel_id=1, source_target_pairs={{0,12},{4,8},{8,4},{12,0},{16,28},{20,24},{24,20},{28,16},{1,13},{... | collective-permute-start | bytes 393224 | tf_op jit(solution)/shard_map/ppermute | solution.py:367
  80.8 2.1 %collective-permute-done.4.rest_3_ = bf16[64,1024]{1,0:T(8,128)(2,1)S(1)} collective-permute-done((bf16[64,1024]{1,0:T(8,128)(2,1)S(1)}, bf16[64,1024]{1,0:T(8,128)(2,1)S(1)}, u32[]{:S(2)}, u32[]{:S(2)}) %collective-permute-start.4) | collective-permute-done | bytes 131104 | tf_op jit(solution)/shard_map/ppermute | solution.py:367
  82.9 0.0 copy-start.5
  82.9 1.6 %collective-permute-done.5.rest_4_ = bf16[64,1024]{1,0:T(8,128)(2,1)S(1)} collective-permute-done((bf16[64,1024]{1,0:T(8,128)(2,1)S(1)}, bf16[64,1024]{1,0:T(8,128)(2,1)S(1)}, u32[]{:S(2)}, u32[]{:S(2)}) %collective-permute-start.5) | collective-permute-done | bytes 131104 | tf_op jit(solution)/shard_map/ppermute | solution.py:367
  84.5 0.0 copy-start.6
  84.5 1.7 %collective-permute-done.6.rest_5_ = bf16[64,1024]{1,0:T(8,128)(2,1)S(1)} collective-permute-done((bf16[64,1024]{1,0:T(8,128)(2,1)S(1)}, bf16[64,1024]{1,0:T(8,128)(2,1)S(1)}, u32[]{:S(2)}, u32[]{:S(2)}) %collective-permute-start.6) | collective-permute-done | bytes 131104 | tf_op jit(solution)/shard_map/ppermute | solution.py:367
  86.2 0.0 copy-start.7
  86.2 0.0 collective-permute-done.9.rest_7_
  86.2 0.0 copy-start.2
  86.2 0.0 collective-permute-done.11.rest_9_
  86.2 0.0 copy-start.3
  86.3 0.0 copy-done.1
  86.3 0.0 copy-done.4
  86.3 0.0 copy-done.5
  86.3 0.0 copy-done.6
  86.3 0.6 copy-done.7
  86.9 0.2 copy-done.2
  87.1 0.1 copy-done.3
  87.2 7.0 %apply.1 = (f32[1024,256]{1,0:T(8,128)}, bf16[2,128,256]{2,1,0:T(8,128)(2,1)}, bf16[2,128,256]{2,1,0:T(8,128)(2,1)}, bf16[2,128,256]{2,1,0:T(8,128)(2,1)}, bf16[2,128,256]{2,1,0:T(8,128)(2,1)}) custom-call(s32[2]{0:T(128)} %pad_add_fusion.meta_ref, s32[2,1,1024]{2,1,0:T(1,128)} %broadcast_in_dim.3.freq, f32[1024,256]{1,0:T(8,128)} %masters_ref.1, ...), custom_call_target="tpu_custom_call" | custom-call | tf_op jit(solution)/shard_map/apply/pallas_call | solution.py:344
  94.2 0.8 collective-permute-start.14
  95.1 1.7 %collective-permute-start.13 = (bf16[2,128,256]{2,1,0:T(8,128)(2,1)}, bf16[2,128,256]{2,1,0:T(8,128)(2,1)S(1)}, u32[]{:S(2)}, u32[]{:S(2)}) collective-permute-start(bf16[2,128,256]{2,1,0:T(8,128)(2,1)} %get-tuple-element.23), channel_id=1, source_target_pairs={{0,8},{4,12},{8,0},{12,4},{16,24},{20,28},{24,16},{28,20},{1,9},{5... | collective-permute-start | bytes 393224 | tf_op jit(solution)/shard_map/ppermute | solution.py:367
  96.8 0.9 collective-permute-start.12
  97.7 2.6 %collective-permute-done.14 = bf16[2,128,256]{2,1,0:T(8,128)(2,1)S(1)} collective-permute-done((bf16[2,128,256]{2,1,0:T(8,128)(2,1)}, bf16[2,128,256]{2,1,0:T(8,128)(2,1)S(1)}, u32[]{:S(2)}, u32[]{:S(2)}) %collective-permute-start.14) | collective-permute-done | bytes 131104 | tf_op jit(solution)/shard_map/ppermute | solution.py:367
  100.3 1.1 collective-permute-done.13
  101.4 0.6 collective-permute-done.12
  102.0 1.0 convert_add_fusion
  103.0 2.1 %collective-permute-start.15 = (bf16[128,256]{1,0:T(8,128)(2,1)S(1)}, bf16[128,256]{1,0:T(8,128)(2,1)S(1)}, u32[]{:S(2)}, u32[]{:S(2)}) collective-permute-start(bf16[128,256]{1,0:T(8,128)(2,1)S(1)} %fusion.3), channel_id=1, source_target_pairs={{0,16},{4,20},{8,24},{12,28},{16,0},{20,4},{24,8},{28,12},{1,17},{... | collective-permute-start | bytes 196616 | tf_op jit(solution)/shard_map/ppermute | solution.py:367
  105.1 6.9 %shard_map.76.rest_0_ = f32[1,8192,256]{2,1,0:T(8,128)} custom-call(s32[2,1,1024]{2,1,0:T(1,128)} %broadcast_in_dim.3.freq, f32[1,8192,256]{2,1,0:T(8,128)} %mom_b.9, f32[1,8192,256]{2,1,0:T(8,128)} %mom_b.9, bf16[1,8192,256]{2,1,0:T(8,128)(2,1)} %grad_b.9, bf16[1,8192,256]{2,1,0:T(8,128)(2,1)} %grad_b.9, bf16[256,1024]{1,0:T(8,128)(2,1)} %get-tuple-element.14.coeff_ref, ...), custom_call_target="tpu_custom_call" | custom-call | tf_op jit(solution)/shard_map/pallas_call | solution.py:274
  112.0 6.9 %shard_map.77.rest_0_ = f32[1,8192,256]{2,1,0:T(8,128)} custom-call(s32[2,1,1024]{2,1,0:T(1,128)} %broadcast_in_dim.3.freq, f32[1,8192,256]{2,1,0:T(8,128)} %mom_b.9, f32[1,8192,256]{2,1,0:T(8,128)} %mom_b.9, bf16[1,8192,256]{2,1,0:T(8,128)(2,1)} %grad_b.9, bf16[1,8192,256]{2,1,0:T(8,128)(2,1)} %grad_b.9, ...), custom_call_target="tpu_custom_call", output_to_operand_aliasing={{}: (7, {})} | custom-call | tf_op jit(solution)/shard_map/pallas_call | solution.py:274
  118.9 6.9 %shard_map.78.rest_0_ = f32[1,8192,256]{2,1,0:T(8,128)} custom-call(s32[2,1,1024]{2,1,0:T(1,128)} %broadcast_in_dim.3.freq, f32[1,8192,256]{2,1,0:T(8,128)} %mom_b.9, f32[1,8192,256]{2,1,0:T(8,128)} %mom_b.9, bf16[1,8192,256]{2,1,0:T(8,128)(2,1)} %grad_b.9, bf16[1,8192,256]{2,1,0:T(8,128)(2,1)} %grad_b.9, ...), custom_call_target="tpu_custom_call", output_to_operand_aliasing={{}: (7, {})} | custom-call | tf_op jit(solution)/shard_map/pallas_call | solution.py:274
  125.9 6.9 %shard_map.79 = f32[1,8192,256]{2,1,0:T(8,128)} custom-call(s32[2,1,1024]{2,1,0:T(1,128)} %broadcast_in_dim.3.freq, f32[1,8192,256]{2,1,0:T(8,128)} %mom_b.9, f32[1,8192,256]{2,1,0:T(8,128)} %mom_b.9, bf16[1,8192,256]{2,1,0:T(8,128)(2,1)} %grad_b.9, bf16[1,8192,256]{2,1,0:T(8,128)(2,1)} %grad_b.9, ...), custom_call_target="tpu_custom_call", output_to_operand_aliasing={{}: (7, {})} | custom-call | tf_op jit(solution)/shard_map/pallas_call | solution.py:274
  132.8 0.0 collective-permute-done.15
  132.8 0.6 fusion.2
  (3 shorter events, 0.1 us)
Async XLA Ops:
  0.6 1.7 %collective-permute-start.7 = (bf16[128,2048]{1,0:T(8,128)(2,1)}, bf16[128,2048]{1,0:T(8,128)(2,1)S(1)}, u32[]{:S(2)}, u32[]{:S(2)}) collective-permute-start(bf16[128,2048]{1,0:T(8,128)(2,1)} %param.8), channel_id=1, source_target_pairs={{0,0},{1,8},{2,16},{3,24},{4,4},{5,12},{6,20},{7,28},{8,1},{9,9},{... | collective-permute-start | bytes 1572872 | tf_op jit(solution)/shard_map/ppermute | solution.py:390
  2.4 7.4 %collective-permute-start.8 = (bf16[128,1024]{1,0:T(8,128)(2,1)S(1)}, bf16[128,1024]{1,0:T(8,128)(2,1)S(1)}, u32[]{:S(2)}, u32[]{:S(2)}) collective-permute-start(bf16[128,1024]{1,0:T(8,128)(2,1)S(1)} %get-tuple-element.26), channel_id=1, source_target_pairs={{0,4},{4,0},{8,12},{12,8},{16,20},{20,16},{24,28},{28,24},{1,5},{5... | collective-permute-start | bytes 786440 | tf_op jit(solution)/shard_map/ppermute | solution.py:367
  9.8 53.6 %copy-start = (bf16[2,128,1024]{2,1,0:T(8,128)(2,1)}, bf16[2,128,1024]{2,1,0:T(8,128)(2,1)S(1)}, u32[]{:S(2)}) copy-start(bf16[2,128,1024]{2,1,0:T(8,128)(2,1)S(1)} %pad_maximum_fusion.rest_6_) | copy-start | bytes 1572868
  9.8 53.6 %collective-permute-start.10 = (bf16[2,128,1024]{2,1,0:T(8,128)(2,1)S(1)}, bf16[2,128,1024]{2,1,0:T(8,128)(2,1)S(1)}, u32[]{:S(2)}, u32[]{:S(2)}) collective-permute-start(bf16[2,128,1024]{2,1,0:T(8,128)(2,1)S(1)} %pad_maximum_fusion.rest_6_), channel_id=1, source_target_pairs={{0,2},{1,3},{2,0},{3,1},{4,6},{5,7},{6,4},{7,5},{8,10},{9,11},{10,... | collective-permute-start | bytes 1572872 | tf_op jit(solution)/shard_map/ppermute | solution.py:367
  59.9 6.1 %collective-permute-start.2 = (bf16[64,1024]{1,0:T(8,128)(2,1)}, bf16[64,1024]{1,0:T(8,128)(2,1)S(1)}, u32[]{:S(2)}, u32[]{:S(2)}) collective-permute-start(bf16[64,1024]{1,0:T(8,128)(2,1)} %get-tuple-element.19), channel_id=1, source_target_pairs={{0,12},{4,8},{8,4},{12,0},{16,28},{20,24},{24,20},{28,16},{1,13},{... | collective-permute-start | bytes 393224 | tf_op jit(solution)/shard_map/ppermute | solution.py:367
  61.6 5.9 %collective-permute-start.1 = (bf16[64,1024]{1,0:T(8,128)(2,1)}, bf16[64,1024]{1,0:T(8,128)(2,1)S(1)}, u32[]{:S(2)}, u32[]{:S(2)}) collective-permute-start(bf16[64,1024]{1,0:T(8,128)(2,1)} %get-tuple-element.18), channel_id=1, source_target_pairs={{0,8},{4,12},{8,0},{12,4},{16,24},{20,28},{24,16},{28,20},{1,9},{5... | collective-permute-start | bytes 393224 | tf_op jit(solution)/shard_map/ppermute | solution.py:367
  62.9 5.2 %collective-permute-start = (bf16[64,1024]{1,0:T(8,128)(2,1)}, bf16[64,1024]{1,0:T(8,128)(2,1)S(1)}, u32[]{:S(2)}, u32[]{:S(2)}) collective-permute-start(bf16[64,1024]{1,0:T(8,128)(2,1)} %get-tuple-element.17), channel_id=1, source_target_pairs={{0,4},{4,0},{8,12},{12,8},{16,20},{20,16},{24,28},{28,24},{1,5},{5... | collective-permute-start | bytes 393224 | tf_op jit(solution)/shard_map/ppermute | solution.py:367
  63.4 22.8 %collective-permute-start.9 = (bf16[2,128,1024]{2,1,0:T(8,128)(2,1)S(1)}, bf16[2,128,1024]{2,1,0:T(8,128)(2,1)S(1)}, u32[]{:S(2)}, u32[]{:S(2)}) collective-permute-start(bf16[2,128,1024]{2,1,0:T(8,128)(2,1)S(1)} %pad_maximum_fusion.rest_6_), channel_id=1, source_target_pairs={{0,1},{1,0},{2,3},{3,2},{4,5},{5,4},{6,7},{7,6},{8,9},{9,8},{10,11... | collective-permute-start | bytes 1572872 | tf_op jit(solution)/shard_map/ppermute | solution.py:367
  63.4 22.8 %copy-start.1 = (bf16[2,128,1024]{2,1,0:T(8,128)(2,1)}, bf16[2,128,1024]{2,1,0:T(8,128)(2,1)S(1)}, u32[]{:S(2)}) copy-start(bf16[2,128,1024]{2,1,0:T(8,128)(2,1)S(1)} %collective-permute-done.10.rest_8_) | copy-start | bytes 1572868
  63.5 22.8 %collective-permute-start.11 = (bf16[2,128,1024]{2,1,0:T(8,128)(2,1)S(1)}, bf16[2,128,1024]{2,1,0:T(8,128)(2,1)S(1)}, u32[]{:S(2)}, u32[]{:S(2)}) collective-permute-start(bf16[2,128,1024]{2,1,0:T(8,128)(2,1)S(1)} %collective-permute-done.10.rest_8_), channel_id=1, source_target_pairs={{0,1},{1,0},{2,3},{3,2},{4,5},{5,4},{6,7},{7,6},{8,9},{9,8},{10,11... | collective-permute-start | bytes 1572872 | tf_op jit(solution)/shard_map/ppermute | solution.py:367
  69.1 8.1 %collective-permute-start.3 = (bf16[64,1024]{1,0:T(8,128)(2,1)S(1)}, bf16[64,1024]{1,0:T(8,128)(2,1)S(1)}, u32[]{:S(2)}, u32[]{:S(2)}) collective-permute-start(bf16[64,1024]{1,0:T(8,128)(2,1)S(1)} %add_convert_fusion.1), channel_id=1, source_target_pairs={{0,16},{4,20},{8,24},{12,28},{16,0},{20,4},{24,8},{28,12},{1,17},{... | collective-permute-start | bytes 393224 | tf_op jit(solution)/shard_map/ppermute | solution.py:367
  77.2 9.0 %copy-start.4 = (bf16[64,1024]{1,0:T(8,128)(2,1)}, bf16[64,1024]{1,0:T(8,128)(2,1)S(1)}, u32[]{:S(2)}) copy-start(bf16[64,1024]{1,0:T(8,128)(2,1)S(1)} %add_convert_fusion.rest_2_) | copy-start | bytes 393220
  77.3 5.6 %collective-permute-start.4 = (bf16[64,1024]{1,0:T(8,128)(2,1)S(1)}, bf16[64,1024]{1,0:T(8,128)(2,1)S(1)}, u32[]{:S(2)}, u32[]{:S(2)}) collective-permute-start(bf16[64,1024]{1,0:T(8,128)(2,1)S(1)} %add_convert_fusion.rest_2_), channel_id=1, source_target_pairs={{0,4},{4,0},{8,12},{12,8},{16,20},{20,16},{24,28},{28,24},{1,5},{5... | collective-permute-start | bytes 393224 | tf_op jit(solution)/shard_map/ppermute | solution.py:367
  78.3 6.2 %collective-permute-start.5 = (bf16[64,1024]{1,0:T(8,128)(2,1)S(1)}, bf16[64,1024]{1,0:T(8,128)(2,1)S(1)}, u32[]{:S(2)}, u32[]{:S(2)}) collective-permute-start(bf16[64,1024]{1,0:T(8,128)(2,1)S(1)} %add_convert_fusion.rest_2_), channel_id=1, source_target_pairs={{0,8},{4,12},{8,0},{12,4},{16,24},{20,28},{24,16},{28,20},{1,9},{5... | collective-permute-start | bytes 393224 | tf_op jit(solution)/shard_map/ppermute | solution.py:367
  78.3 7.9 %collective-permute-start.6 = (bf16[64,1024]{1,0:T(8,128)(2,1)S(1)}, bf16[64,1024]{1,0:T(8,128)(2,1)S(1)}, u32[]{:S(2)}, u32[]{:S(2)}) collective-permute-start(bf16[64,1024]{1,0:T(8,128)(2,1)S(1)} %add_convert_fusion.rest_2_), channel_id=1, source_target_pairs={{0,12},{4,8},{8,4},{12,0},{16,28},{20,24},{24,20},{28,16},{1,13},{... | collective-permute-start | bytes 393224 | tf_op jit(solution)/shard_map/ppermute | solution.py:367
  82.9 3.4 %copy-start.5 = (bf16[64,1024]{1,0:T(8,128)(2,1)}, bf16[64,1024]{1,0:T(8,128)(2,1)S(1)}, u32[]{:S(2)}) copy-start(bf16[64,1024]{1,0:T(8,128)(2,1)S(1)} %collective-permute-done.4.rest_3_) | copy-start | bytes 393220
  84.5 1.8 %copy-start.6 = (bf16[64,1024]{1,0:T(8,128)(2,1)}, bf16[64,1024]{1,0:T(8,128)(2,1)S(1)}, u32[]{:S(2)}) copy-start(bf16[64,1024]{1,0:T(8,128)(2,1)S(1)} %collective-permute-done.5.rest_4_) | copy-start | bytes 393220
  86.2 0.7 copy-start.7
  86.2 0.9 copy-start.2
  86.2 1.0 copy-start.3
  94.2 6.1 %collective-permute-start.14 = (bf16[2,128,256]{2,1,0:T(8,128)(2,1)}, bf16[2,128,256]{2,1,0:T(8,128)(2,1)S(1)}, u32[]{:S(2)}, u32[]{:S(2)}) collective-permute-start(bf16[2,128,256]{2,1,0:T(8,128)(2,1)} %get-tuple-element.24), channel_id=1, source_target_pairs={{0,12},{4,8},{8,4},{12,0},{16,28},{20,24},{24,20},{28,16},{1,13},{... | collective-permute-start | bytes 393224 | tf_op jit(solution)/shard_map/ppermute | solution.py:367
  95.1 6.4 %collective-permute-start.13 = (bf16[2,128,256]{2,1,0:T(8,128)(2,1)}, bf16[2,128,256]{2,1,0:T(8,128)(2,1)S(1)}, u32[]{:S(2)}, u32[]{:S(2)}) collective-permute-start(bf16[2,128,256]{2,1,0:T(8,128)(2,1)} %get-tuple-element.23), channel_id=1, source_target_pairs={{0,8},{4,12},{8,0},{12,4},{16,24},{20,28},{24,16},{28,20},{1,9},{5... | collective-permute-start | bytes 393224 | tf_op jit(solution)/shard_map/ppermute | solution.py:367
  96.8 5.2 %collective-permute-start.12 = (bf16[2,128,256]{2,1,0:T(8,128)(2,1)}, bf16[2,128,256]{2,1,0:T(8,128)(2,1)S(1)}, u32[]{:S(2)}, u32[]{:S(2)}) collective-permute-start(bf16[2,128,256]{2,1,0:T(8,128)(2,1)} %get-tuple-element.22), channel_id=1, source_target_pairs={{0,4},{4,0},{8,12},{12,8},{16,20},{20,16},{24,28},{28,24},{1,5},{5... | collective-permute-start | bytes 393224 | tf_op jit(solution)/shard_map/ppermute | solution.py:367
  103.0 29.8 %collective-permute-start.15 = (bf16[128,256]{1,0:T(8,128)(2,1)S(1)}, bf16[128,256]{1,0:T(8,128)(2,1)S(1)}, u32[]{:S(2)}, u32[]{:S(2)}) collective-permute-start(bf16[128,256]{1,0:T(8,128)(2,1)S(1)} %fusion.3), channel_id=1, source_target_pairs={{0,16},{4,20},{8,24},{12,28},{16,0},{20,4},{24,8},{28,12},{1,17},{... | collective-permute-start | bytes 196616 | tf_op jit(solution)/shard_map/ppermute | solution.py:367

commit v3 on v2

v3 whole, which is shorter than its diff:
```python
import math

import jax
import jax.numpy as jnp
from jax import lax
from jax.experimental import pallas as pl
from jax.experimental.pallas import tpu as pltpu
from jax.sharding import PartitionSpec as P


momentum_decay = 0.9
step_rate = 1.0
fine_rows = 64
forward_tile = 1024
remain_shares = (0, 4, 8, 12, 13, 15, 16)
apply_rows = 1024
vmem_bytes = 40 * 1024 * 1024
f32 = jnp.float32
bf16 = jnp.bfloat16


def wrap(phase, period):
    return phase & (period - 1) if period & (period - 1) == 0 else phase % period


def sine_cosine(phase, model_width):
    shifted = phase + model_width // 2
    if model_width & (model_width - 1) == 0:
        quarter = shifted >> (model_width.bit_length() - 1)
    else:
        quarter = shifted // model_width
    x = (phase - quarter * model_width).astype(f32) * (math.pi / (2 * model_width))
    z = x * x
    sine = x + x * z * (-1.6666654611e-1 + z * (8.3321608736e-3 + z * -1.9515295891e-4))
    cosine = 1.0 - 0.5 * z + z * z * (
        4.166664568298827e-2 + z * (-1.388731625493765e-3 + z * 2.443315711809948e-5)
    )
    swapped = (quarter & 1) == 1
    cos_sign = (1 - ((quarter + 1) & 2)).astype(f32)
    sin_sign = (1 - (quarter & 2)).astype(f32)
    return (
        cos_sign * jnp.where(swapped, sine, cosine),
        sin_sign * jnp.where(swapped, cosine, sine),
    )


def fill_tables(frequency, coarse_cos, coarse_sin, fine_cos, fine_sin, twice, model_width):
    freqs = frequency.shape[1]
    digit = lax.broadcasted_iota(jnp.int32, (8, freqs), 0)
    scale = jnp.where(
        frequency == 0, math.sqrt(1.0 / model_width), math.sqrt(2.0 / model_width)
    ).astype(f32)

    def angles(multiplier):
        return sine_cosine(wrap(multiplier * frequency, 4 * model_width), model_width)

    def combine(high, low, cos_ref, sin_ref):
        for k in range(cos_ref.shape[0] // 8):
            rows = pl.ds(8 * k, 8)
            cosine, sine = high[0][k : k + 1], high[1][k : k + 1]
            cos_ref[rows, :] = cosine * low[0] - sine * low[1]
            sin_ref[rows, :] = sine * low[0] + cosine * low[1]

    cosine, sine = angles(2 * fine_rows * digit)
    twice[...] = 2.0 * jnp.broadcast_to(cosine[1:2], cosine.shape)
    combine(
        angles(16 * fine_rows * digit), (cosine * scale, sine * scale), coarse_cos, coarse_sin
    )
    combine(angles(16 * digit), angles(2 * digit + 1), fine_cos, fine_sin)


def fill_cosines(target, first_coarse, count, coarse_cos, coarse_sin, fine_cos, fine_sin, twice):
    for lane in range(0, target.shape[1], 128):
        lanes = pl.ds(lane, 128)
        cosine = fine_cos[:, lanes]
        sine = fine_sin[:, lanes]
        coarse_c = coarse_cos[pl.ds(first_coarse, 8), lanes]
        coarse_s = coarse_sin[pl.ds(first_coarse, 8), lanes]
        factor = jnp.broadcast_to(twice[0:1, lanes], cosine.shape)
        older = newer = None
        for k in range(count):
            if k < 2:
                value = coarse_c[k : k + 1] * cosine - coarse_s[k : k + 1] * sine
            else:
                value = factor * newer - older
            older, newer = newer, value
            target[pl.ds(k * fine_rows, fine_rows), lanes] = value.astype(bf16)


def flip(value):
    order = 7 - lax.broadcasted_iota(jnp.int32, (8, value.shape[1]), 0)
    pieces = [
        jnp.take_along_axis(value[row : row + 8], order, axis=0)
        for row in range(value.shape[0] - 8, -1, -8)
    ]
    return jnp.concatenate(pieces, axis=0)


def parity_sign(frequency):
    return (1 - 2 * (frequency & 1)).astype(f32)


def dot_tn(a, b):
    return lax.dot_general(a, b, (((0,), (0,)), ((), ())), preferred_element_type=f32)


def dot_nt(a, b):
    return lax.dot_general(a, b, (((1,), (1,)), ((), ())), preferred_element_type=f32)


def forward(momentum, gradient, freq_rows, meta, group):
    model_width = momentum.shape[1]
    blocks, freqs = freq_rows.shape
    cols = momentum.shape[2]
    block_cols = cols // blocks
    half = model_width // 2
    tile = min(forward_tile, half)
    steps = half // tile
    piece = cols // group

    def kernel(device_ref, rank_ref, freq, mom_a, mom_b, grad_a, grad_b, coeff, *rest):
        pieces = rest[:group]
        table, total, *tables = rest[group:]
        block, step = pl.program_id(0), pl.program_id(1)
        frequency = freq[0:1]
        for other in range(1, blocks):
            frequency = jnp.where(block == other, freq[other : other + 1], frequency)

        @pl.when(step == 0)
        def _():
            fill_tables(frequency, *tables, model_width)

        fill_cosines(
            table, pl.multiple_of(step * (tile // fine_rows), 8), tile // fine_rows, *tables
        )
        low_a = (momentum_decay * mom_a[0] + grad_a[0].astype(f32)).astype(bf16)
        low_b = flip(momentum_decay * mom_b[0] + grad_b[0].astype(f32)).astype(bf16)
        both = jnp.concatenate([low_a, low_b], axis=1)
        partial = dot_tn(both, table[...])

        @pl.when(step == 0)
        def _():
            total[...] = partial

        @pl.when(step > 0)
        def _():
            total[...] += partial

        @pl.when(step == steps - 1)
        def _():
            rows = pl.ds(pl.multiple_of(block * block_cols, block_cols), block_cols)
            coeff[rows, :] = (
                total[:block_cols] + parity_sign(frequency) * total[block_cols:]
            ).astype(bf16)

        @pl.when((step == steps - 1) & (block == blocks - 1))
        def _():
            for k in range(group):
                start = ((device_ref[0] % group) ^ k) * piece
                pieces[k][...] = coeff[pl.ds(pl.multiple_of(start, piece), piece), :]

    def whole(block, step, *scalars):
        return (0, 0)

    def rows(which):
        def index(block, step, *scalars):
            return (0, 2 * steps - 1 - step if which else step, block)

        return pl.BlockSpec((1, tile, block_cols), index)

    return pl.pallas_call(
        kernel,
        name="forward",
        grid_spec=pltpu.PrefetchScalarGridSpec(
            num_scalar_prefetch=2,
            grid=(blocks, steps),
            in_specs=[
                pl.BlockSpec((blocks, freqs), whole),
                rows(0), rows(1), rows(0), rows(1),
            ],
            out_specs=[pl.BlockSpec((cols, freqs), whole)]
            + [pl.BlockSpec((piece, freqs), whole)] * group
            + [pl.BlockSpec(
                (tile, freqs), lambda block, step, *scalars: (block * steps + step, 0)
            )],
            scratch_shapes=[pltpu.VMEM((2 * block_cols, freqs), f32)]
            + [pltpu.VMEM((half // fine_rows, freqs), f32)] * 2
            + [pltpu.VMEM((fine_rows, freqs), f32)] * 2
            + [pltpu.VMEM((8, freqs), f32)],
        ),
        out_shape=[jax.ShapeDtypeStruct((cols, freqs), bf16)]
        + [jax.ShapeDtypeStruct((piece, freqs), bf16)] * group
        + [jax.ShapeDtypeStruct((blocks * half, freqs), bf16)],
    )(*meta, freq_rows, momentum, momentum, gradient, gradient)


def remain(part, momentum, gradient, freq_rows, coeff, table, previous):
    model_width = momentum.shape[1]
    block_cols = momentum.shape[2] // freq_rows.shape[0]
    blocks, freqs = freq_rows.shape
    half = model_width // 2
    tile = min(512 if blocks > 1 else 256, half)
    all_steps = half // tile
    begin, end = (all_steps * blocks * share // 16 for share in remain_shares[part : part + 2])
    column_block, first = divmod(begin, all_steps)
    steps = end - begin

    def kernel(freq, mom_a, mom_b, grad_a, grad_b, coeff_ref, table_ref, *rest):
        residual, both, buffer, sems = rest[-4:]
        step = pl.program_id(0)
        slot = step % 2

        def copies(at, where):
            lanes = pl.ds(column_block * block_cols, block_cols)
            return [
                pltpu.make_async_copy(
                    buffer.at[where, k], residual.at[0, pl.ds(start * tile, tile), lanes],
                    sems.at[where, k],
                )
                for k, start in enumerate((first + at, 2 * all_steps - 1 - first - at))
            ]

        @pl.when(step == 0)
        def _():
            both[:block_cols] = coeff_ref[...]
            both[block_cols:] = (coeff_ref[...].astype(f32) * parity_sign(freq[column_block : column_block + 1])).astype(bf16)

        back = dot_nt(table_ref[...], both[...])

        @pl.when(step >= 2)
        def _():
            for copy in copies(step - 2, slot):
                copy.wait()

        buffer[slot, 0] = (
            momentum_decay * mom_a[0] + grad_a[0].astype(f32) - back[:, :block_cols]
        )
        buffer[slot, 1] = (
            momentum_decay * mom_b[0] + grad_b[0].astype(f32) - flip(back[:, block_cols:])
        )
        for copy in copies(step, slot):
            copy.start()

        @pl.when(step == steps - 1)
        def _():
            if steps > 1:
                for copy in copies(step - 1, 1 - slot):
                    copy.wait()
            for copy in copies(step, slot):
                copy.wait()

    def rows(which):
        def index(step):
            at = first + step
            return (0, 2 * all_steps - 1 - at if which else at, column_block)

        return pl.BlockSpec((1, tile, block_cols), index)

    operands = [freq_rows, momentum, momentum, gradient, gradient, coeff, table]
    specs = [
        pl.BlockSpec((blocks, freqs), lambda step: (0, 0)),
        rows(0), rows(1), rows(0), rows(1),
        pl.BlockSpec((block_cols, freqs), lambda step: (column_block, 0)),
        pl.BlockSpec(
            (tile, freqs), lambda step: (column_block * all_steps + first + step, 0)
        ),
    ]
    aliases = {}
    if previous is not None:
        aliases = {len(operands): 0}
        operands.append(previous)
        specs.append(pl.BlockSpec(memory_space=pl.ANY))
    return pl.pallas_call(
        kernel,
        grid=(steps,),
        in_specs=specs,
        out_specs=pl.BlockSpec(memory_space=pl.ANY),
        scratch_shapes=[
            pltpu.VMEM((2 * block_cols, freqs), bf16),
            pltpu.VMEM((2, 2, tile, block_cols), f32),
            pltpu.SemaphoreType.DMA((2, 2)),
        ],
        out_shape=jax.ShapeDtypeStruct(momentum.shape, f32),
        input_output_aliases=aliases,
    )(*operands)


def apply(masters, freq_rows, table, means, features, meta, dp, tensor, group):
    own_rows, cols = masters.shape
    blocks, freqs = freq_rows.shape
    block_cols = cols // blocks
    piece = cols // group
    ratio, token_rows, _ = features[0].shape
    half_parts = table.shape[0] // blocks // own_rows
    crosses = dp // group

    chunk = min(apply_rows, own_rows)
    steps = own_rows // chunk

    def kernel(device_ref, rank_ref, freq, masters_ref, *rest):
        tables = rest[:blocks]
        mean_refs = rest[blocks : blocks + group]
        feature_refs = rest[blocks + group : blocks + group + tensor]
        new_ref, *outs, mean, products = rest[blocks + group + tensor :]
        device, rank = device_ref[0], rank_ref[0]
        step = pl.program_id(0)
        mirrored = device >= half_parts

        @pl.when(step == 0)
        def _():
            for k in range(group):
                start = ((device % group) ^ k) * piece
                mean[pl.ds(pl.multiple_of(start, piece), piece), :] = mean_refs[k][...]
            for block in range(blocks):
                rows = pl.ds(block * block_cols, block_cols)
                sign = jnp.where(mirrored, parity_sign(freq[block : block + 1]), 1.0)
                mean[rows, :] = (mean[rows, :].astype(f32) * sign).astype(bf16)

        updates = [
            dot_nt(tables[block][...], mean[pl.ds(block * block_cols, block_cols), :])
            for block in range(blocks)
        ]
        update = jnp.concatenate(updates, axis=1) * (1.0 / dp)

        @pl.when(mirrored)
        def _():
            new_ref[...] = masters_ref[...] - step_rate * flip(update)

        @pl.when(jnp.logical_not(mirrored))
        def _():
            new_ref[...] = masters_ref[...] - step_rate * update

        weights = new_ref[...].astype(bf16)
        for other in range(tensor):
            for k in range(ratio):
                product = jnp.dot(
                    feature_refs[other][k, :, pl.ds(pl.multiple_of(step * chunk, chunk), chunk)],
                    weights, preferred_element_type=f32)

                @pl.when(step == 0)
                def _():
                    products[other * ratio + k] = product

                @pl.when(step > 0)
                def _():
                    products[other * ratio + k] += product

        @pl.when(step == steps - 1)
        def _():
            base = (device // ratio) ^ rank
            for k in range(group):
                for cross in range(crosses):
                    target = cross * group + k
                    outs[k][cross] = products[
                        (base ^ (target // ratio)) * ratio + target % ratio
                    ].astype(bf16)

    def whole(*shape):
        return pl.BlockSpec(shape, lambda step, *scalars: (0,) * len(shape))

    def own_table(block):
        def index(step, *scalars):
            device = scalars[0][0]
            mirrored = device >= half_parts
            row = jnp.where(
                mirrored,
                (2 * half_parts - device) * steps - 1 - step,
                device * steps + step,
            )
            return (block * half_parts * steps + row, 0)

        return pl.BlockSpec((chunk, freqs), index)

    own = pl.BlockSpec((chunk, cols), lambda step, *scalars: (step, 0))
    return pl.pallas_call(
        kernel,
        name="apply",
        grid_spec=pltpu.PrefetchScalarGridSpec(
            num_scalar_prefetch=2,
            grid=(steps,),
            in_specs=[whole(*freq_rows.shape), own]
            + [own_table(block) for block in range(blocks)]
            + [pl.BlockSpec(memory_space=pltpu.VMEM)] * (group + tensor),
            out_specs=[own] + [whole(crosses, token_rows, cols)] * group,
            scratch_shapes=[
                pltpu.VMEM((cols, freqs), bf16),
                pltpu.VMEM((dp, token_rows, cols), f32),
            ],
        ),
        out_shape=[jax.ShapeDtypeStruct((own_rows, cols), f32)]
        + [jax.ShapeDtypeStruct((crosses, token_rows, cols), bf16)] * group,
        compiler_params=pltpu.CompilerParams(vmem_limit_bytes=vmem_bytes),
    )(*meta, freq_rows, masters, *[table] * blocks, *map(near, means), *map(near, features))


def near(value):
    return pltpu.with_memory_space_constraint(value, pltpu.VMEM)


def swap(value, axis, mask, size):
    return lax.ppermute(value, axis, [(k, k ^ mask) for k in range(size)])


def sum_low(values):
    total = values[0].astype(f32)
    for value in values[1:]:
        total = total + value.astype(f32)
    return total.astype(bf16)


def step(momentum, gradient, masters, tokens, freq_index):
    dp, tensor = lax.axis_size("dp"), lax.axis_size("tensor")
    group = min(4, dp)
    ratio = dp // tensor
    model_width = momentum.shape[1]
    device, rank = lax.axis_index("dp"), lax.axis_index("tensor")
    meta = (device.reshape(1).astype(jnp.int32), rank.reshape(1).astype(jnp.int32))
    freq_rows = freq_index

    pairs = [
        ((J * ratio + h) * tensor + j, (j * ratio + h) * tensor + J)
        for J in range(tensor) for h in range(ratio) for j in range(tensor)
    ]
    traded = lax.ppermute(tokens, ("dp", "tensor"), pairs)
    width = tokens.shape[1] // ratio

    coeff, *pieces, table = forward(momentum, gradient, freq_rows, meta, group)

    first = [swap(pieces[k], "dp", k, dp) for k in range(1, group)]

    residual = None

    def next_remain(part, residual):
        return remain(part, momentum, gradient, freq_rows, coeff, table, residual)

    def feature_piece(k):
        start = ((device % ratio) ^ k) * width
        return lax.dynamic_slice_in_dim(traded, start, width, axis=1)

    residual = next_remain(0, residual)
    summed = sum_low([pieces[0]] + first)
    summed = sum_low([summed] + [swap(summed, "dp", k * group, dp) for k in range(1, dp // group)])
    parts = [feature_piece(0)]
    for k in range(1, ratio):
        parts.append(swap(feature_piece(k), "dp", k, dp))
    residual = next_remain(1, residual)
    means = [summed] + [swap(summed, "dp", k, dp) for k in range(1, group)]
    features = {0: jnp.stack(parts)}
    mask = tensor // 2
    while mask > 0:
        for held in sorted(features):
            features[held ^ mask] = swap(features[held], "tensor", mask, tensor)
        mask //= 2
    residual = next_remain(2, residual)
    residual = next_remain(3, residual)
    new_masters, *partials = apply(
        masters, freq_rows, table, means, [features[k] for k in range(tensor)], meta, dp, tensor,
        group,
    )
    received = [swap(partials[k], "dp", k, dp) for k in range(1, group)]
    residual = next_remain(4, residual)
    residual = next_remain(5, residual)
    part = partials[0].astype(f32)
    for value in received:
        part = part + value.astype(f32)
    part_low = part.astype(bf16)
    total = part[0]
    for k in range(1, dp // group):
        total = total + swap(part_low[k], "dp", k * group, dp).astype(f32)
    projected = (total * model_width ** (-0.5)).astype(bf16)
    return (residual, new_masters, projected)


def solution(mesh):
    return jax.shard_map(
        step,
        mesh=mesh,
        in_specs=(
            P("dp", None, "tensor"),
            P("dp", None, "tensor"),
            P("dp", "tensor"),
            P("dp", "tensor"),
            P("tensor", None),
        ),
        out_specs=(P("dp", None, "tensor"), P("dp", "tensor"), P("dp", "tensor")),
        check_vma=False,
    )
```

time: 134 us -> 127 us (0.948)
  Pallas kernels: 53 us -> 50.4 us
  local copies, waits for them, and re-layouts: 2.33 us -> 0.05 us
  other arithmetic: 3.24 us -> 1.77 us
    pallas_call x1, Pallas kernels: 6.99 us -> 5.19 us  [apply(): pl.pallas_call(kernel, name='apply', grid_spec=pltpu.PrefetchScalarGridSp...]
    pallas_call x4 -> x6, Pallas kernels: 27.7 us -> 28.2 us  [remain(): pl.pallas_call(kernel, grid=(steps,), in_specs=specs, out_specs=pl.BlockS...]
  transfers between devices with their start and end apart: 16 -> 16, of which waited for: 11 -> 11; matrix products, arithmetic and copies ran while one was open for 2% -> 1% of each run, Pallas kernels for 34% -> 36%
where the time goes in v3:
time: 127 us; the launch traced here: 126 us
  Pallas kernels  50.4 us (40%)
  starting transfers between devices  49.4 us (39%)
  waiting for transfers between devices  24 us (19%)
  other arithmetic  1.77 us (1%)
    ppermute x15, starting transfers between devices, swap(): return lax.ppermute(value, axis, [(k, k ^ mask) for k in range(size)])  47.7 us
    pallas_call x6, Pallas kernels, remain(): pl.pallas_call(kernel, grid=(steps,), in_specs=specs, out_specs=pl.BlockS...  28.2 us
    ppermute x15, waiting for transfers between devices, swap(): return lax.ppermute(value, axis, [(k, k ^ mask) for k in range(size)])  24 us
    pallas_call x1, Pallas kernels, forward(): pl.pallas_call(kernel, name='forward', grid_spec=pltpu.PrefetchScalarGrid...  17.1 us
    pallas_call x1, Pallas kernels, apply(): pl.pallas_call(kernel, name='apply', grid_spec=pltpu.PrefetchScalarGridSp...  5.19 us
  transfers between devices with their start and end apart: 16, of which 11 were waited for; matrix products, arithmetic and copies ran while one was open for 1% of the time, Pallas kernels for 36%

profile of v3, /device:TPU:0, one launch (start us, length us, event | category | flops | bytes accessed | tf_op | source)
XLA Modules:
  0.0 126.4 jit_solution(8360771328418996544)
XLA Ops:
  0.6 1.7 %collective-permute-start.7 = (bf16[128,2048]{1,0:T(8,128)(2,1)}, bf16[128,2048]{1,0:T(8,128)(2,1)S(1)}, u32[]{:S(2)}, u32[]{:S(2)}) collective-permute-start(bf16[128,2048]{1,0:T(8,128)(2,1)} %param.8), channel_id=1, source_target_pairs={{0,0},{1,8},{2,16},{3,24},{4,4},{5,12},{6,20},{7,28},{8,1},{9,9},{... | collective-permute-start | bytes 1572872 | tf_op jit(solution)/shard_map/ppermute | solution.py:424
  2.3 0.0 collective-permute-done.7
  2.4 3.0 %collective-permute-start.8 = (bf16[128,1024]{1,0:T(8,128)(2,1)S(1)}, bf16[128,1024]{1,0:T(8,128)(2,1)S(1)}, u32[]{:S(2)}, u32[]{:S(2)}) collective-permute-start(bf16[128,1024]{1,0:T(8,128)(2,1)S(1)} %get-tuple-element.26), channel_id=1, source_target_pairs={{0,4},{4,0},{8,12},{12,8},{16,20},{20,16},{24,28},{28,24},{1,5},{5... | collective-permute-start | bytes 786440 | tf_op jit(solution)/shard_map/ppermute | solution.py:401
  5.4 4.4 %collective-permute-done.8 = bf16[128,1024]{1,0:T(8,128)(2,1)S(1)} collective-permute-done((bf16[128,1024]{1,0:T(8,128)(2,1)S(1)}, bf16[128,1024]{1,0:T(8,128)(2,1)S(1)}, u32[]{:S(2)}, u32[]{:S(2)}) %collective-permute-start.8) | collective-permute-done | bytes 262176 | tf_op jit(solution)/shard_map/ppermute | solution.py:401
  9.8 0.1 pad_maximum_fusion.rest_6_
  9.8 30.0 %collective-permute-start.10 = (bf16[2,128,1024]{2,1,0:T(8,128)(2,1)S(1)}, bf16[2,128,1024]{2,1,0:T(8,128)(2,1)S(1)}, u32[]{:S(2)}, u32[]{:S(2)}) collective-permute-start(bf16[2,128,1024]{2,1,0:T(8,128)(2,1)S(1)} %pad_maximum_fusion.rest_6_), channel_id=1, source_target_pairs={{0,2},{1,3},{2,0},{3,1},{4,6},{5,7},{6,4},{7,5},{8,10},{9,11},{10,... | collective-permute-start | bytes 1572872 | tf_op jit(solution)/shard_map/ppermute | solution.py:401
  39.8 0.0 copy-start
  39.8 0.0 copy-start.1
  39.8 17.1 %forward.1 = (bf16[256,1024]{1,0:T(8,128)(2,1)}, bf16[64,1024]{1,0:T(8,128)(2,1)}, bf16[64,1024]{1,0:T(8,128)(2,1)}, bf16[64,1024]{1,0:T(8,128)(2,1)}, bf16[64,1...) custom-call(s32[1]{0:T(128)} %bitcast.device_ref, s32[1]{0:T(128)} %bitcast.1.rank_ref, s32[2,1024]{1,0:T(2,128)} %freq.15, ...), custom_call_target="tpu_custom_call" | custom-call | tf_op jit(solution)/shard_map/forward/pallas_call | solution.py:171
  56.9 1.6 %collective-permute-start.2 = (bf16[64,1024]{1,0:T(8,128)(2,1)}, bf16[64,1024]{1,0:T(8,128)(2,1)S(1)}, u32[]{:S(2)}, u32[]{:S(2)}) collective-permute-start(bf16[64,1024]{1,0:T(8,128)(2,1)} %get-tuple-element.19), channel_id=1, source_target_pairs={{0,12},{4,8},{8,4},{12,0},{16,28},{20,24},{24,20},{28,16},{1,13},{... | collective-permute-start | bytes 393224 | tf_op jit(solution)/shard_map/ppermute | solution.py:401
  58.5 1.3 %collective-permute-start.1 = (bf16[64,1024]{1,0:T(8,128)(2,1)}, bf16[64,1024]{1,0:T(8,128)(2,1)S(1)}, u32[]{:S(2)}, u32[]{:S(2)}) collective-permute-start(bf16[64,1024]{1,0:T(8,128)(2,1)} %get-tuple-element.18), channel_id=1, source_target_pairs={{0,8},{4,12},{8,0},{12,4},{16,24},{20,28},{24,16},{28,20},{1,9},{5... | collective-permute-start | bytes 393224 | tf_op jit(solution)/shard_map/ppermute | solution.py:401
  59.8 0.5 collective-permute-start
  60.4 0.0 collective-permute-start.9
  60.4 0.0 collective-permute-done.10.rest_8_
  60.4 0.5 collective-permute-start.11
  60.9 2.1 %collective-permute-done.2 = bf16[64,1024]{1,0:T(8,128)(2,1)S(1)} collective-permute-done((bf16[64,1024]{1,0:T(8,128)(2,1)}, bf16[64,1024]{1,0:T(8,128)(2,1)S(1)}, u32[]{:S(2)}, u32[]{:S(2)}) %collective-permute-start.2) | collective-permute-done | bytes 131104 | tf_op jit(solution)/shard_map/ppermute | solution.py:401
  62.9 1.4 %collective-permute-done.1 = bf16[64,1024]{1,0:T(8,128)(2,1)S(1)} collective-permute-done((bf16[64,1024]{1,0:T(8,128)(2,1)}, bf16[64,1024]{1,0:T(8,128)(2,1)S(1)}, u32[]{:S(2)}, u32[]{:S(2)}) %collective-permute-start.1) | collective-permute-done | bytes 131104 | tf_op jit(solution)/shard_map/ppermute | solution.py:401
  64.4 0.6 collective-permute-done
  65.0 1.0 add_convert_fusion.1
  66.0 2.1 %collective-permute-start.3 = (bf16[64,1024]{1,0:T(8,128)(2,1)S(1)}, bf16[64,1024]{1,0:T(8,128)(2,1)S(1)}, u32[]{:S(2)}, u32[]{:S(2)}) collective-permute-start(bf16[64,1024]{1,0:T(8,128)(2,1)S(1)} %add_convert_fusion.1), channel_id=1, source_target_pairs={{0,16},{4,20},{8,24},{12,28},{16,0},{20,4},{24,8},{28,12},{1,17},{... | collective-permute-start | bytes 393224 | tf_op jit(solution)/shard_map/ppermute | solution.py:401
  68.0 6.1 %collective-permute-done.3 = bf16[64,1024]{1,0:T(8,128)(2,1)S(1)} collective-permute-done((bf16[64,1024]{1,0:T(8,128)(2,1)S(1)}, bf16[64,1024]{1,0:T(8,128)(2,1)S(1)}, u32[]{:S(2)}, u32[]{:S(2)}) %collective-permute-start.3) | collective-permute-done | bytes 131104 | tf_op jit(solution)/shard_map/ppermute | solution.py:401
  74.1 1.1 collective-permute-start.4
  75.2 0.0 collective-permute-start.5
  75.2 2.5 %collective-permute-start.6 = (bf16[64,1024]{1,0:T(8,128)(2,1)S(1)}, bf16[64,1024]{1,0:T(8,128)(2,1)S(1)}, u32[]{:S(2)}, u32[]{:S(2)}) collective-permute-start(bf16[64,1024]{1,0:T(8,128)(2,1)S(1)} %add_convert_fusion.rest_2_), channel_id=1, source_target_pairs={{0,12},{4,8},{8,4},{12,0},{16,28},{20,24},{24,20},{28,16},{1,13},{... | collective-permute-start | bytes 393224 | tf_op jit(solution)/shard_map/ppermute | solution.py:401
  77.7 2.1 %collective-permute-done.4.rest_3_ = bf16[64,1024]{1,0:T(8,128)(2,1)S(1)} collective-permute-done((bf16[64,1024]{1,0:T(8,128)(2,1)S(1)}, bf16[64,1024]{1,0:T(8,128)(2,1)S(1)}, u32[]{:S(2)}, u32[]{:S(2)}) %collective-permute-start.4) | collective-permute-done | bytes 131104 | tf_op jit(solution)/shard_map/ppermute | solution.py:401
  79.8 1.6 %collective-permute-done.5.rest_4_ = bf16[64,1024]{1,0:T(8,128)(2,1)S(1)} collective-permute-done((bf16[64,1024]{1,0:T(8,128)(2,1)S(1)}, bf16[64,1024]{1,0:T(8,128)(2,1)S(1)}, u32[]{:S(2)}, u32[]{:S(2)}) %collective-permute-start.5) | collective-permute-done | bytes 131104 | tf_op jit(solution)/shard_map/ppermute | solution.py:401
  81.4 1.7 %collective-permute-done.6.rest_5_ = bf16[64,1024]{1,0:T(8,128)(2,1)S(1)} collective-permute-done((bf16[64,1024]{1,0:T(8,128)(2,1)S(1)}, bf16[64,1024]{1,0:T(8,128)(2,1)S(1)}, u32[]{:S(2)}, u32[]{:S(2)}) %collective-permute-start.6) | collective-permute-done | bytes 131104 | tf_op jit(solution)/shard_map/ppermute | solution.py:401
  83.1 0.0 collective-permute-done.9.rest_7_
  83.1 0.0 collective-permute-done.11.rest_9_
  83.1 0.0 copy-done
  83.1 0.0 copy-done.1
  83.1 5.2 %apply.1 = (f32[1024,256]{1,0:T(8,128)}, bf16[2,128,256]{2,1,0:T(8,128)(2,1)S(1)}, bf16[2,128,256]{2,1,0:T(8,128)(2,1)S(1)}, bf16[2,128,256]{2,1,0:T(8,128)(2,1)S(1)}, bf16[2,128,256]{2,1,0:T(8,128)(2,1)S(1)}) custom-call(s32[1]{0:T(128)} %bitcast.device_ref, s32[1]{0:T(128)} %bitcast.1.rank_ref, s32[2,1024]{1,0:T(2,128)S(1)} %copy-done.1, ...), custom_call_target="tpu_custom_call" | custom-call | tf_op jit(solution)/shard_map/apply/pallas_call | solution.py:375
  88.3 0.9 collective-permute-start.14
  89.2 1.7 %collective-permute-start.13 = (bf16[2,128,256]{2,1,0:T(8,128)(2,1)S(1)}, bf16[2,128,256]{2,1,0:T(8,128)(2,1)S(1)}, u32[]{:S(2)}, u32[]{:S(2)}) collective-permute-start(bf16[2,128,256]{2,1,0:T(8,128)(2,1)S(1)} %get-tuple-element.23), channel_id=1, source_target_pairs={{0,8},{4,12},{8,0},{12,4},{16,24},{20,28},{24,16},{28,20},{1,9},{5... | collective-permute-start | bytes 393224 | tf_op jit(solution)/shard_map/ppermute | solution.py:401
  90.9 0.9 collective-permute-start.12
  91.8 2.4 %collective-permute-done.14 = bf16[2,128,256]{2,1,0:T(8,128)(2,1)S(1)} collective-permute-done((bf16[2,128,256]{2,1,0:T(8,128)(2,1)S(1)}, bf16[2,128,256]{2,1,0:T(8,128)(2,1)S(1)}, u32[]{:S(2)}, u32[]{:S(2)}) %collective-permute-start.14) | collective-permute-done | bytes 131104 | tf_op jit(solution)/shard_map/ppermute | solution.py:401
  94.2 1.1 collective-permute-done.13
  95.3 0.6 collective-permute-done.12
  95.9 0.1 convert_add_fusion
  96.0 1.6 %collective-permute-start.15 = (bf16[128,256]{1,0:T(8,128)(2,1)S(1)}, bf16[128,256]{1,0:T(8,128)(2,1)S(1)}, u32[]{:S(2)}, u32[]{:S(2)}) collective-permute-start(bf16[128,256]{1,0:T(8,128)(2,1)S(1)} %fusion.3), channel_id=1, source_target_pairs={{0,16},{4,20},{8,24},{12,28},{16,0},{20,4},{24,8},{28,12},{1,17},{... | collective-permute-start | bytes 196616 | tf_op jit(solution)/shard_map/ppermute | solution.py:401
  97.6 6.2 %shard_map.76.rest_0_ = f32[1,8192,256]{2,1,0:T(8,128)} custom-call(s32[2,1024]{1,0:T(2,128)} %freq.15, f32[1,8192,256]{2,1,0:T(8,128)} %mom_b.13, f32[1,8192,256]{2,1,0:T(8,128)} %mom_b.13, bf16[1,8192,256]{2,1,0:T(8,128)(2,1)} %grad_b.13, bf16[1,8192,256]{2,1,0:T(8,128)(2,1)} %grad_b.13, bf16[256,1024]{1,0:T(8,128)(2,1)} %get-tuple-element.14.coeff_ref, ...), custom_call_target="tpu_custom_call" | custom-call | tf_op jit(solution)/shard_map/pallas_call | solution.py:273
  103.8 6.2 %shard_map.77.rest_0_ = f32[1,8192,256]{2,1,0:T(8,128)} custom-call(s32[2,1024]{1,0:T(2,128)} %freq.15, f32[1,8192,256]{2,1,0:T(8,128)} %mom_b.13, f32[1,8192,256]{2,1,0:T(8,128)} %mom_b.13, bf16[1,8192,256]{2,1,0:T(8,128)(2,1)} %grad_b.13, bf16[1,8192,256]{2,1,0:T(8,128)(2,1)} %grad_b.13, ...), custom_call_target="tpu_custom_call", output_to_operand_aliasing={{}: (7, {})} | custom-call | tf_op jit(solution)/shard_map/pallas_call | solution.py:273
  110.0 6.2 %shard_map.78.rest_0_ = f32[1,8192,256]{2,1,0:T(8,128)} custom-call(s32[2,1024]{1,0:T(2,128)} %freq.15, f32[1,8192,256]{2,1,0:T(8,128)} %mom_b.13, f32[1,8192,256]{2,1,0:T(8,128)} %mom_b.13, bf16[1,8192,256]{2,1,0:T(8,128)(2,1)} %grad_b.13, bf16[1,8192,256]{2,1,0:T(8,128)(2,1)} %grad_b.13, ...), custom_call_target="tpu_custom_call", output_to_operand_aliasing={{}: (7, {})} | custom-call | tf_op jit(solution)/shard_map/pallas_call | solution.py:273
  116.2 2.9 %shard_map.79.rest_0_ = f32[1,8192,256]{2,1,0:T(8,128)} custom-call(s32[2,1024]{1,0:T(2,128)} %freq.15, f32[1,8192,256]{2,1,0:T(8,128)} %mom_b.13, f32[1,8192,256]{2,1,0:T(8,128)} %mom_b.13, bf16[1,8192,256]{2,1,0:T(8,128)(2,1)} %grad_b.13, bf16[1,8192,256]{2,1,0:T(8,128)(2,1)} %grad_b.13, ...), custom_call_target="tpu_custom_call", output_to_operand_aliasing={{}: (7, {})} | custom-call | tf_op jit(solution)/shard_map/pallas_call | solution.py:273
  119.1 3.8 %shard_map.80.rest_0_ = f32[1,8192,256]{2,1,0:T(8,128)} custom-call(s32[2,1024]{1,0:T(2,128)} %freq.15, f32[1,8192,256]{2,1,0:T(8,128)} %mom_b.13, f32[1,8192,256]{2,1,0:T(8,128)} %mom_b.13, bf16[1,8192,256]{2,1,0:T(8,128)(2,1)} %grad_b.13, bf16[1,8192,256]{2,1,0:T(8,128)(2,1)} %grad_b.13, ...), custom_call_target="tpu_custom_call", output_to_operand_aliasing={{}: (7, {})} | custom-call | tf_op jit(solution)/shard_map/pallas_call | solution.py:273
  122.9 2.9 %shard_map.81 = f32[1,8192,256]{2,1,0:T(8,128)} custom-call(s32[2,1024]{1,0:T(2,128)} %freq.15, f32[1,8192,256]{2,1,0:T(8,128)} %mom_b.13, f32[1,8192,256]{2,1,0:T(8,128)} %mom_b.13, bf16[1,8192,256]{2,1,0:T(8,128)(2,1)} %grad_b.13, bf16[1,8192,256]{2,1,0:T(8,128)(2,1)} %grad_b.13, ...), custom_call_target="tpu_custom_call", output_to_operand_aliasing={{}: (7, {})} | custom-call | tf_op jit(solution)/shard_map/pallas_call | solution.py:273
  125.8 0.0 collective-permute-done.15
  125.8 0.6 fusion.2
  (3 shorter events, 0.1 us)
Async XLA Ops:
  0.6 1.7 %collective-permute-start.7 = (bf16[128,2048]{1,0:T(8,128)(2,1)}, bf16[128,2048]{1,0:T(8,128)(2,1)S(1)}, u32[]{:S(2)}, u32[]{:S(2)}) collective-permute-start(bf16[128,2048]{1,0:T(8,128)(2,1)} %param.8), channel_id=1, source_target_pairs={{0,0},{1,8},{2,16},{3,24},{4,4},{5,12},{6,20},{7,28},{8,1},{9,9},{... | collective-permute-start | bytes 1572872 | tf_op jit(solution)/shard_map/ppermute | solution.py:424
  2.4 7.4 %collective-permute-start.8 = (bf16[128,1024]{1,0:T(8,128)(2,1)S(1)}, bf16[128,1024]{1,0:T(8,128)(2,1)S(1)}, u32[]{:S(2)}, u32[]{:S(2)}) collective-permute-start(bf16[128,1024]{1,0:T(8,128)(2,1)S(1)} %get-tuple-element.26), channel_id=1, source_target_pairs={{0,4},{4,0},{8,12},{12,8},{16,20},{20,16},{24,28},{28,24},{1,5},{5... | collective-permute-start | bytes 786440 | tf_op jit(solution)/shard_map/ppermute | solution.py:401
  9.8 50.6 %collective-permute-start.10 = (bf16[2,128,1024]{2,1,0:T(8,128)(2,1)S(1)}, bf16[2,128,1024]{2,1,0:T(8,128)(2,1)S(1)}, u32[]{:S(2)}, u32[]{:S(2)}) collective-permute-start(bf16[2,128,1024]{2,1,0:T(8,128)(2,1)S(1)} %pad_maximum_fusion.rest_6_), channel_id=1, source_target_pairs={{0,2},{1,3},{2,0},{3,1},{4,6},{5,7},{6,4},{7,5},{8,10},{9,11},{10,... | collective-permute-start | bytes 1572872 | tf_op jit(solution)/shard_map/ppermute | solution.py:401
  39.8 43.3 %copy-start = (f32[1024,256]{1,0:T(8,128)S(1)}, f32[1024,256]{1,0:T(8,128)}, u32[]{:S(2)}) copy-start(f32[1024,256]{1,0:T(8,128)} %masters_ref.1) | copy-start | bytes 3145732
  39.8 43.3 %copy-start.1 = (s32[2,1024]{1,0:T(2,128)S(1)}, s32[2,1024]{1,0:T(2,128)}, u32[]{:S(2)}) copy-start(s32[2,1024]{1,0:T(2,128)} %freq.15) | copy-start | bytes 24580
  56.9 6.1 %collective-permute-start.2 = (bf16[64,1024]{1,0:T(8,128)(2,1)}, bf16[64,1024]{1,0:T(8,128)(2,1)S(1)}, u32[]{:S(2)}, u32[]{:S(2)}) collective-permute-start(bf16[64,1024]{1,0:T(8,128)(2,1)} %get-tuple-element.19), channel_id=1, source_target_pairs={{0,12},{4,8},{8,4},{12,0},{16,28},{20,24},{24,20},{28,16},{1,13},{... | collective-permute-start | bytes 393224 | tf_op jit(solution)/shard_map/ppermute | solution.py:401
  58.5 5.9 %collective-permute-start.1 = (bf16[64,1024]{1,0:T(8,128)(2,1)}, bf16[64,1024]{1,0:T(8,128)(2,1)S(1)}, u32[]{:S(2)}, u32[]{:S(2)}) collective-permute-start(bf16[64,1024]{1,0:T(8,128)(2,1)} %get-tuple-element.18), channel_id=1, source_target_pairs={{0,8},{4,12},{8,0},{12,4},{16,24},{20,28},{24,16},{28,20},{1,9},{5... | collective-permute-start | bytes 393224 | tf_op jit(solution)/shard_map/ppermute | solution.py:401
  59.8 5.2 %collective-permute-start = (bf16[64,1024]{1,0:T(8,128)(2,1)}, bf16[64,1024]{1,0:T(8,128)(2,1)S(1)}, u32[]{:S(2)}, u32[]{:S(2)}) collective-permute-start(bf16[64,1024]{1,0:T(8,128)(2,1)} %get-tuple-element.17), channel_id=1, source_target_pairs={{0,4},{4,0},{8,12},{12,8},{16,20},{20,16},{24,28},{28,24},{1,5},{5... | collective-permute-start | bytes 393224 | tf_op jit(solution)/shard_map/ppermute | solution.py:401
  60.4 22.7 %collective-permute-start.9 = (bf16[2,128,1024]{2,1,0:T(8,128)(2,1)S(1)}, bf16[2,128,1024]{2,1,0:T(8,128)(2,1)S(1)}, u32[]{:S(2)}, u32[]{:S(2)}) collective-permute-start(bf16[2,128,1024]{2,1,0:T(8,128)(2,1)S(1)} %pad_maximum_fusion.rest_6_), channel_id=1, source_target_pairs={{0,1},{1,0},{2,3},{3,2},{4,5},{5,4},{6,7},{7,6},{8,9},{9,8},{10,11... | collective-permute-start | bytes 1572872 | tf_op jit(solution)/shard_map/ppermute | solution.py:401
  60.4 22.7 %collective-permute-start.11 = (bf16[2,128,1024]{2,1,0:T(8,128)(2,1)S(1)}, bf16[2,128,1024]{2,1,0:T(8,128)(2,1)S(1)}, u32[]{:S(2)}, u32[]{:S(2)}) collective-permute-start(bf16[2,128,1024]{2,1,0:T(8,128)(2,1)S(1)} %collective-permute-done.10.rest_8_), channel_id=1, source_target_pairs={{0,1},{1,0},{2,3},{3,2},{4,5},{5,4},{6,7},{7,6},{8,9},{9,8},{10,11... | collective-permute-start | bytes 1572872 | tf_op jit(solution)/shard_map/ppermute | solution.py:401
  66.0 8.1 %collective-permute-start.3 = (bf16[64,1024]{1,0:T(8,128)(2,1)S(1)}, bf16[64,1024]{1,0:T(8,128)(2,1)S(1)}, u32[]{:S(2)}, u32[]{:S(2)}) collective-permute-start(bf16[64,1024]{1,0:T(8,128)(2,1)S(1)} %add_convert_fusion.1), channel_id=1, source_target_pairs={{0,16},{4,20},{8,24},{12,28},{16,0},{20,4},{24,8},{28,12},{1,17},{... | collective-permute-start | bytes 393224 | tf_op jit(solution)/shard_map/ppermute | solution.py:401
  74.1 5.7 %collective-permute-start.4 = (bf16[64,1024]{1,0:T(8,128)(2,1)S(1)}, bf16[64,1024]{1,0:T(8,128)(2,1)S(1)}, u32[]{:S(2)}, u32[]{:S(2)}) collective-permute-start(bf16[64,1024]{1,0:T(8,128)(2,1)S(1)} %add_convert_fusion.rest_2_), channel_id=1, source_target_pairs={{0,4},{4,0},{8,12},{12,8},{16,20},{20,16},{24,28},{28,24},{1,5},{5... | collective-permute-start | bytes 393224 | tf_op jit(solution)/shard_map/ppermute | solution.py:401
  75.2 6.2 %collective-permute-start.5 = (bf16[64,1024]{1,0:T(8,128)(2,1)S(1)}, bf16[64,1024]{1,0:T(8,128)(2,1)S(1)}, u32[]{:S(2)}, u32[]{:S(2)}) collective-permute-start(bf16[64,1024]{1,0:T(8,128)(2,1)S(1)} %add_convert_fusion.rest_2_), channel_id=1, source_target_pairs={{0,8},{4,12},{8,0},{12,4},{16,24},{20,28},{24,16},{28,20},{1,9},{5... | collective-permute-start | bytes 393224 | tf_op jit(solution)/shard_map/ppermute | solution.py:401
  75.2 7.9 %collective-permute-start.6 = (bf16[64,1024]{1,0:T(8,128)(2,1)S(1)}, bf16[64,1024]{1,0:T(8,128)(2,1)S(1)}, u32[]{:S(2)}, u32[]{:S(2)}) collective-permute-start(bf16[64,1024]{1,0:T(8,128)(2,1)S(1)} %add_convert_fusion.rest_2_), channel_id=1, source_target_pairs={{0,12},{4,8},{8,4},{12,0},{16,28},{20,24},{24,20},{28,16},{1,13},{... | collective-permute-start | bytes 393224 | tf_op jit(solution)/shard_map/ppermute | solution.py:401
  88.3 5.9 %collective-permute-start.14 = (bf16[2,128,256]{2,1,0:T(8,128)(2,1)S(1)}, bf16[2,128,256]{2,1,0:T(8,128)(2,1)S(1)}, u32[]{:S(2)}, u32[]{:S(2)}) collective-permute-start(bf16[2,128,256]{2,1,0:T(8,128)(2,1)S(1)} %get-tuple-element.24), channel_id=1, source_target_pairs={{0,12},{4,8},{8,4},{12,0},{16,28},{20,24},{24,20},{28,16},{1,13},{... | collective-permute-start | bytes 393224 | tf_op jit(solution)/shard_map/ppermute | solution.py:401
  89.2 6.1 %collective-permute-start.13 = (bf16[2,128,256]{2,1,0:T(8,128)(2,1)S(1)}, bf16[2,128,256]{2,1,0:T(8,128)(2,1)S(1)}, u32[]{:S(2)}, u32[]{:S(2)}) collective-permute-start(bf16[2,128,256]{2,1,0:T(8,128)(2,1)S(1)} %get-tuple-element.23), channel_id=1, source_target_pairs={{0,8},{4,12},{8,0},{12,4},{16,24},{20,28},{24,16},{28,20},{1,9},{5... | collective-permute-start | bytes 393224 | tf_op jit(solution)/shard_map/ppermute | solution.py:401
  90.9 5.0 %collective-permute-start.12 = (bf16[2,128,256]{2,1,0:T(8,128)(2,1)S(1)}, bf16[2,128,256]{2,1,0:T(8,128)(2,1)S(1)}, u32[]{:S(2)}, u32[]{:S(2)}) collective-permute-start(bf16[2,128,256]{2,1,0:T(8,128)(2,1)S(1)} %get-tuple-element.22), channel_id=1, source_target_pairs={{0,4},{4,0},{8,12},{12,8},{16,20},{20,16},{24,28},{28,24},{1,5},{5... | collective-permute-start | bytes 393224 | tf_op jit(solution)/shard_map/ppermute | solution.py:401
  96.0 29.8 %collective-permute-start.15 = (bf16[128,256]{1,0:T(8,128)(2,1)S(1)}, bf16[128,256]{1,0:T(8,128)(2,1)S(1)}, u32[]{:S(2)}, u32[]{:S(2)}) collective-permute-start(bf16[128,256]{1,0:T(8,128)(2,1)S(1)} %fusion.3), channel_id=1, source_target_pairs={{0,16},{4,20},{8,24},{12,28},{16,0},{20,4},{24,8},{28,12},{1,17},{... | collective-permute-start | bytes 196616 | tf_op jit(solution)/shard_map/ppermute | solution.py:401

commit v4 on v3

--- a/solution.py
+++ b/solution.py
@@ -12,9 +12,9 @@
 step_rate = 1.0
 fine_rows = 64
 forward_tile = 1024
-remain_shares = (0, 4, 8, 12, 13, 15, 16)
+remain_shares = (0, 4, 8, 12, 14, 16)
 apply_rows = 1024
-vmem_bytes = 40 * 1024 * 1024
+vmem_bytes = 20 * 1024 * 1024
 f32 = jnp.float32
 bf16 = jnp.bfloat16
 
@@ -130,13 +130,15 @@
         def _():
             fill_tables(frequency, *tables, model_width)
 
+        here = table.at[pl.ds(pl.multiple_of((block * steps + step) * tile, tile), tile), :]
+
         fill_cosines(
-            table, pl.multiple_of(step * (tile // fine_rows), 8), tile // fine_rows, *tables
+            here, pl.multiple_of(step * (tile // fine_rows), 8), tile // fine_rows, *tables
         )
         low_a = (momentum_decay * mom_a[0] + grad_a[0].astype(f32)).astype(bf16)
         low_b = flip(momentum_decay * mom_b[0] + grad_b[0].astype(f32)).astype(bf16)
         both = jnp.concatenate([low_a, low_b], axis=1)
-        partial = dot_tn(both, table[...])
+        partial = dot_tn(both, here[...])
 
         @pl.when(step == 0)
         def _():
@@ -180,9 +182,7 @@
             ],
             out_specs=[pl.BlockSpec((cols, freqs), whole)]
             + [pl.BlockSpec((piece, freqs), whole)] * group
-            + [pl.BlockSpec(
-                (tile, freqs), lambda block, step, *scalars: (block * steps + step, 0)
-            )],
+            + [pl.BlockSpec(memory_space=pltpu.VMEM)],
             scratch_shapes=[pltpu.VMEM((2 * block_cols, freqs), f32)]
             + [pltpu.VMEM((half // fine_rows, freqs), f32)] * 2
             + [pltpu.VMEM((fine_rows, freqs), f32)] * 2
@@ -190,7 +190,8 @@
         ),
         out_shape=[jax.ShapeDtypeStruct((cols, freqs), bf16)]
         + [jax.ShapeDtypeStruct((piece, freqs), bf16)] * group
-        + [jax.ShapeDtypeStruct((blocks * half, freqs), bf16)],
+        + [pltpu.VMEM((blocks * half, freqs), bf16)],
+        compiler_params=pltpu.CompilerParams(vmem_limit_bytes=vmem_bytes),
     )(*meta, freq_rows, momentum, momentum, gradient, gradient)
 
 
@@ -206,7 +207,7 @@
     steps = end - begin
 
     def kernel(freq, mom_a, mom_b, grad_a, grad_b, coeff_ref, table_ref, *rest):
-        residual, both, buffer, sems = rest[-4:]
+        residual, _, both, buffer, sems = rest[-5:]
         step = pl.program_id(0)
         slot = step % 2
 
@@ -225,7 +226,8 @@
             both[:block_cols] = coeff_ref[...]
             both[block_cols:] = (coeff_ref[...].astype(f32) * parity_sign(freq[column_block : column_block + 1])).astype(bf16)
 
-        back = dot_nt(table_ref[...], both[...])
+        at = (column_block * all_steps + first + step) * tile
+        back = dot_nt(table_ref[pl.ds(pl.multiple_of(at, tile), tile), :], both[...])
 
         @pl.when(step >= 2)
         def _():
@@ -256,32 +258,33 @@
 
         return pl.BlockSpec((1, tile, block_cols), index)
 
-    operands = [freq_rows, momentum, momentum, gradient, gradient, coeff, table]
+    operands = [freq_rows, momentum, momentum, gradient, gradient, coeff, near(table)]
     specs = [
         pl.BlockSpec((blocks, freqs), lambda step: (0, 0)),
         rows(0), rows(1), rows(0), rows(1),
         pl.BlockSpec((block_cols, freqs), lambda step: (column_block, 0)),
-        pl.BlockSpec(
-            (tile, freqs), lambda step: (column_block * all_steps + first + step, 0)
-        ),
+        pl.BlockSpec(memory_space=pltpu.VMEM),
     ]
-    aliases = {}
+    aliases = {len(operands) - 1: 1}
     if previous is not None:
-        aliases = {len(operands): 0}
+        aliases[len(operands)] = 0
         operands.append(previous)
         specs.append(pl.BlockSpec(memory_space=pl.ANY))
     return pl.pallas_call(
         kernel,
         grid=(steps,),
         in_specs=specs,
-        out_specs=pl.BlockSpec(memory_space=pl.ANY),
+        out_specs=[pl.BlockSpec(memory_space=pl.ANY), pl.BlockSpec(memory_space=pltpu.VMEM)],
         scratch_shapes=[
             pltpu.VMEM((2 * block_cols, freqs), bf16),
             pltpu.VMEM((2, 2, tile, block_cols), f32),
             pltpu.SemaphoreType.DMA((2, 2)),
         ],
-        out_shape=jax.ShapeDtypeStruct(momentum.shape, f32),
+        out_shape=[
+            jax.ShapeDtypeStruct(momentum.shape, f32), pltpu.VMEM(table.shape, table.dtype)
+        ],
         input_output_aliases=aliases,
+        compiler_params=pltpu.CompilerParams(vmem_limit_bytes=vmem_bytes),
     )(*operands)
 
 
@@ -298,10 +301,10 @@
     steps = own_rows // chunk
 
     def kernel(device_ref, rank_ref, freq, masters_ref, *rest):
-        tables = rest[:blocks]
-        mean_refs = rest[blocks : blocks + group]
-        feature_refs = rest[blocks + group : blocks + group + tensor]
-        new_ref, *outs, mean, products = rest[blocks + group + tensor :]
+        table_ref, *rest = rest
+        mean_refs = rest[:group]
+        feature_refs = rest[group : group + tensor]
+        new_ref, *outs, held, mean, products = rest[group + tensor :]
         device, rank = device_ref[0], rank_ref[0]
         step = pl.program_id(0)
         mirrored = device >= half_parts
@@ -316,8 +319,16 @@
                 sign = jnp.where(mirrored, parity_sign(freq[block : block + 1]), 1.0)
                 mean[rows, :] = (mean[rows, :].astype(f32) * sign).astype(bf16)
 
+        row = jnp.where(
+            mirrored, (2 * half_parts - device) * steps - 1 - step, device * steps + step
+        )
+
+        def own_table(block):
+            start = (block * half_parts * steps + row) * chunk
+            return table_ref[pl.ds(pl.multiple_of(start, chunk), chunk), :]
+
         updates = [
-            dot_nt(tables[block][...], mean[pl.ds(block * block_cols, block_cols), :])
+            dot_nt(own_table(block), mean[pl.ds(block * block_cols, block_cols), :])
             for block in range(blocks)
         ]
         update = jnp.concatenate(updates, axis=1) * (1.0 / dp)
@@ -357,19 +368,6 @@
 
     def whole(*shape):
         return pl.BlockSpec(shape, lambda step, *scalars: (0,) * len(shape))
-
-    def own_table(block):
-        def index(step, *scalars):
-            device = scalars[0][0]
-            mirrored = device >= half_parts
-            row = jnp.where(
-                mirrored,
-                (2 * half_parts - device) * steps - 1 - step,
-                device * steps + step,
-            )
-            return (block * half_parts * steps + row, 0)
-
-        return pl.BlockSpec((chunk, freqs), index)
 
     own = pl.BlockSpec((chunk, cols), lambda step, *scalars: (step, 0))
     return pl.pallas_call(
@@ -379,18 +377,44 @@
             num_scalar_prefetch=2,
             grid=(steps,),
             in_specs=[whole(*freq_rows.shape), own]
-            + [own_table(block) for block in range(blocks)]
-            + [pl.BlockSpec(memory_space=pltpu.VMEM)] * (group + tensor),
-            out_specs=[own] + [whole(crosses, token_rows, cols)] * group,
+            + [pl.BlockSpec(memory_space=pltpu.VMEM)] * (1 + group + tensor),
+            out_specs=[own] + [whole(crosses, token_rows, cols)] * group
+            + [pl.BlockSpec(memory_space=pltpu.VMEM)],
             scratch_shapes=[
                 pltpu.VMEM((cols, freqs), bf16),
                 pltpu.VMEM((dp, token_rows, cols), f32),
             ],
         ),
         out_shape=[jax.ShapeDtypeStruct((own_rows, cols), f32)]
-        + [jax.ShapeDtypeStruct((crosses, token_rows, cols), bf16)] * group,
+        + [jax.ShapeDtypeStruct((crosses, token_rows, cols), bf16)] * group
+        + [pltpu.VMEM(table.shape, table.dtype)],
+        input_output_aliases={4: 1 + group},
         compiler_params=pltpu.CompilerParams(vmem_limit_bytes=vmem_bytes),
-    )(*meta, freq_rows, masters, *[table] * blocks, *map(near, means), *map(near, features))
+    )(*meta, freq_rows, masters, near(table), *map(near, means), *map(near, features))
+
+
+def pick(traded, device, ratio):
+    rows, width = traded.shape[0], traded.shape[1] // ratio
+
+    def kernel(device_ref, *refs):
+        for k in range(ratio):
+            refs[ratio + k][...] = refs[k][...]
+
+    def piece(k):
+        return pl.BlockSpec((rows, width), lambda step, scalar: (0, (scalar[0] % ratio) ^ k))
+
+    return pl.pallas_call(
+        kernel,
+        name="pick",
+        grid_spec=pltpu.PrefetchScalarGridSpec(
+            num_scalar_prefetch=1,
+            grid=(1,),
+            in_specs=[piece(k) for k in range(ratio)],
+            out_specs=[pl.BlockSpec((rows, width), lambda step, scalar: (0, 0))] * ratio,
+        ),
+        out_shape=[jax.ShapeDtypeStruct((rows, width), bf16)] * ratio,
+        compiler_params=pltpu.CompilerParams(vmem_limit_bytes=vmem_bytes),
+    )(device, *[pltpu.with_memory_space_constraint(traded, pltpu.HBM)] * ratio)
 
 
 def near(value):
@@ -417,12 +441,14 @@
     meta = (device.reshape(1).astype(jnp.int32), rank.reshape(1).astype(jnp.int32))
     freq_rows = freq_index
 
+    momentum = pltpu.with_memory_space_constraint(momentum, pltpu.HBM)
+    gradient = pltpu.with_memory_space_constraint(gradient, pltpu.HBM)
+
     pairs = [
         ((J * ratio + h) * tensor + j, (j * ratio + h) * tensor + J)
         for J in range(tensor) for h in range(ratio) for j in range(tensor)
     ]
     traded = lax.ppermute(tokens, ("dp", "tensor"), pairs)
-    width = tokens.shape[1] // ratio
 
     coeff, *pieces, table = forward(momentum, gradient, freq_rows, meta, group)
 
@@ -430,20 +456,16 @@
 
     residual = None
 
-    def next_remain(part, residual):
+    def next_remain(part, residual, table):
         return remain(part, momentum, gradient, freq_rows, coeff, table, residual)
 
-    def feature_piece(k):
-        start = ((device % ratio) ^ k) * width
-        return lax.dynamic_slice_in_dim(traded, start, width, axis=1)
-
-    residual = next_remain(0, residual)
     summed = sum_low([pieces[0]] + first)
     summed = sum_low([summed] + [swap(summed, "dp", k * group, dp) for k in range(1, dp // group)])
-    parts = [feature_piece(0)]
+    chosen = pick(traded, meta[0], ratio)
+    parts = [chosen[0]]
     for k in range(1, ratio):
-        parts.append(swap(feature_piece(k), "dp", k, dp))
-    residual = next_remain(1, residual)
+        parts.append(swap(chosen[k], "dp", k, dp))
+    residual, table = next_remain(0, residual, table)
     means = [summed] + [swap(summed, "dp", k, dp) for k in range(1, group)]
     features = {0: jnp.stack(parts)}
     mask = tensor // 2
@@ -451,15 +473,15 @@
         for held in sorted(features):
             features[held ^ mask] = swap(features[held], "tensor", mask, tensor)
         mask //= 2
-    residual = next_remain(2, residual)
-    residual = next_remain(3, residual)
-    new_masters, *partials = apply(
+    residual, table = next_remain(1, residual, table)
+    residual, table = next_remain(2, residual, table)
+    new_masters, *partials, table = apply(
         masters, freq_rows, table, means, [features[k] for k in range(tensor)], meta, dp, tensor,
         group,
     )
     received = [swap(partials[k], "dp", k, dp) for k in range(1, group)]
-    residual = next_remain(4, residual)
-    residual = next_remain(5, residual)
+    residual, table = next_remain(3, residual, table)
+    residual, table = next_remain(4, residual, table)
     part = partials[0].astype(f32)
     for value in received:
         part = part + value.astype(f32)

time: 127 us -> 112 us (0.88)
  Pallas kernels: 50.4 us -> 38.8 us
  waiting for transfers between devices: 24 us -> 18.1 us
  starting transfers between devices: 49.4 us -> 51.5 us
  local copies, waits for them, and re-layouts: 0.05 us -> 1.51 us
    ppermute x15, waiting for transfers between devices: 24 us -> 18.1 us  [swap(): return lax.ppermute(value, axis, [(k, k ^ mask) for k in range(size)])]
    pallas_call x6, Pallas kernels: 28.2 us -> 22.8 us  [the longest x5 21.7 us: remain(): pl.pallas_call(kernel, grid=(steps,), in_specs=specs, out_specs=[pl.Block...]
    pallas_call x1, Pallas kernels: 17.1 us -> 13.1 us  [forward(): pl.pallas_call(kernel, name='forward', grid_spec=pltpu.PrefetchScalarGrid...]
    pallas_call x1, Pallas kernels: 5.19 us -> 2.96 us  [apply(): pl.pallas_call(kernel, name='apply', grid_spec=pltpu.PrefetchScalarGridSp...]
    ppermute x15, starting transfers between devices: 47.7 us -> 49.8 us  [swap(): return lax.ppermute(value, axis, [(k, k ^ mask) for k in range(size)])]
    unnamed x4 -> x6, local copies, waits for them, and re-layouts: 0.01 us -> 1.5 us
  transfers between devices with their start and end apart: 16 -> 16, of which waited for: 11 -> 8; matrix products, arithmetic and copies ran while one was open for 1% -> 0% of each run, Pallas kernels for 36% -> 31%
where the time goes in v4:
time: 112 us
  starting transfers between devices  51.5 us (46%)
  Pallas kernels  38.8 us (35%)
  waiting for transfers between devices  18.1 us (16%)
  local copies, waits for them, and re-layouts  1.51 us (1%)
    ppermute x15, starting transfers between devices, swap(): return lax.ppermute(value, axis, [(k, k ^ mask) for k in range(size)])  49.8 us
    pallas_call x5, Pallas kernels, remain(): pl.pallas_call(kernel, grid=(steps,), in_specs=specs, out_specs=[pl.Block...  21.7 us
    ppermute x15, waiting for transfers between devices, swap(): return lax.ppermute(value, axis, [(k, k ^ mask) for k in range(size)])  18.1 us
    pallas_call x1, Pallas kernels, forward(): pl.pallas_call(kernel, name='forward', grid_spec=pltpu.PrefetchScalarGrid...  13.1 us
    pallas_call x1, Pallas kernels, apply(): pl.pallas_call(kernel, name='apply', grid_spec=pltpu.PrefetchScalarGridSp...  2.96 us
  transfers between devices with their start and end apart: 16, of which 8 were waited for; matrix products, arithmetic and copies ran while one was open for 0% of the time, Pallas kernels for 31%

profile of v4, /device:TPU:0, one launch (start us, length us, event | category | flops | bytes accessed | tf_op | source)
XLA Modules:
  0.0 111.6 jit_solution(5059428991019553512)
XLA Ops:
  0.6 1.7 %collective-permute-start.7 = (bf16[128,2048]{1,0:T(8,128)(2,1)}, bf16[128,2048]{1,0:T(8,128)(2,1)S(1)}, u32[]{:S(2)}, u32[]{:S(2)}) collective-permute-start(bf16[128,2048]{1,0:T(8,128)(2,1)} %param.8), channel_id=1, source_target_pairs={{0,0},{1,8},{2,16},{3,24},{4,4},{5,12},{6,20},{7,28},{8,1},{9,9},{... | collective-permute-start | bytes 1572872 | tf_op jit(solution)/shard_map/ppermute | solution.py:451
  2.3 0.0 collective-permute-done.7.refs_0_.refs_1_
  2.3 0.0 copy-start.2
  2.3 0.8 copy-done.2
  3.1 1.1 pick.1
  4.2 3.0 %collective-permute-start.8 = (bf16[128,1024]{1,0:T(8,128)(2,1)S(1)}, bf16[128,1024]{1,0:T(8,128)(2,1)S(1)}, u32[]{:S(2)}, u32[]{:S(2)}) collective-permute-start(bf16[128,1024]{1,0:T(8,128)(2,1)S(1)} %get-tuple-element.38), channel_id=1, source_target_pairs={{0,4},{4,0},{8,12},{12,8},{16,20},{20,16},{24,28},{28,24},{1,5},{5... | collective-permute-start | bytes 786440 | tf_op jit(solution)/shard_map/ppermute | solution.py:425
  7.2 4.4 %collective-permute-done.8 = bf16[128,1024]{1,0:T(8,128)(2,1)S(1)} collective-permute-done((bf16[128,1024]{1,0:T(8,128)(2,1)S(1)}, bf16[128,1024]{1,0:T(8,128)(2,1)S(1)}, u32[]{:S(2)}, u32[]{:S(2)}) %collective-permute-start.8) | collective-permute-done | bytes 262176 | tf_op jit(solution)/shard_map/ppermute | solution.py:425
  11.6 0.1 pad_maximum_fusion.rest_5_
  11.6 30.0 %collective-permute-start.10 = (bf16[2,128,1024]{2,1,0:T(8,128)(2,1)S(1)}, bf16[2,128,1024]{2,1,0:T(8,128)(2,1)S(1)}, u32[]{:S(2)}, u32[]{:S(2)}) collective-permute-start(bf16[2,128,1024]{2,1,0:T(8,128)(2,1)S(1)} %pad_maximum_fusion.rest_5_), channel_id=1, source_target_pairs={{0,2},{1,3},{2,0},{3,1},{4,6},{5,7},{6,4},{7,5},{8,10},{9,11},{10,... | collective-permute-start | bytes 1572872 | tf_op jit(solution)/shard_map/ppermute | solution.py:425
  41.6 0.0 copy-start.1
  41.6 0.7 copy-done.1
  42.3 13.1 %forward.1 = (bf16[256,1024]{1,0:T(8,128)(2,1)S(1)}, bf16[64,1024]{1,0:T(8,128)(2,1)S(1)}, bf16[64,1024]{1,0:T(8,128)(2,1)S(1)}, bf16[64,1024]{1,0:T(8,128)(2,1)...) custom-call(s32[1]{0:T(128)} %bitcast.device_ref, s32[1]{0:T(128)} %bitcast.1.rank_ref, ...), custom_call_target="tpu_custom_call" | custom-call | tf_op jit(solution)/shard_map/forward/pallas_call | solution.py:173
  55.5 1.6 %collective-permute-start = (bf16[64,1024]{1,0:T(8,128)(2,1)S(1)}, bf16[64,1024]{1,0:T(8,128)(2,1)S(1)}, u32[]{:S(2)}, u32[]{:S(2)}) collective-permute-start(bf16[64,1024]{1,0:T(8,128)(2,1)S(1)} %get-tuple-element.34), channel_id=1, source_target_pairs={{0,4},{4,0},{8,12},{12,8},{16,20},{20,16},{24,28},{28,24},{1,5},{5... | collective-permute-start | bytes 393224 | tf_op jit(solution)/shard_map/ppermute | solution.py:425
  57.0 0.7 collective-permute-start.1
  57.7 1.3 %collective-permute-start.2 = (bf16[64,1024]{1,0:T(8,128)(2,1)S(1)}, bf16[64,1024]{1,0:T(8,128)(2,1)S(1)}, u32[]{:S(2)}, u32[]{:S(2)}) collective-permute-start(bf16[64,1024]{1,0:T(8,128)(2,1)S(1)} %get-tuple-element.36), channel_id=1, source_target_pairs={{0,12},{4,8},{8,4},{12,0},{16,28},{20,24},{24,20},{28,16},{1,13},{... | collective-permute-start | bytes 393224 | tf_op jit(solution)/shard_map/ppermute | solution.py:425
  59.0 0.0 collective-permute-start.9
  59.0 0.0 collective-permute-done.10.rest_7_
  59.0 0.5 collective-permute-start.11
  59.5 1.6 %collective-permute-done = bf16[64,1024]{1,0:T(8,128)(2,1)S(1)} collective-permute-done((bf16[64,1024]{1,0:T(8,128)(2,1)S(1)}, bf16[64,1024]{1,0:T(8,128)(2,1)S(1)}, u32[]{:S(2)}, u32[]{:S(2)}) %collective-permute-start) | collective-permute-done | bytes 131104 | tf_op jit(solution)/shard_map/ppermute | solution.py:425
  61.1 0.9 collective-permute-done.1
  62.0 1.6 %collective-permute-done.2 = bf16[64,1024]{1,0:T(8,128)(2,1)S(1)} collective-permute-done((bf16[64,1024]{1,0:T(8,128)(2,1)S(1)}, bf16[64,1024]{1,0:T(8,128)(2,1)S(1)}, u32[]{:S(2)}, u32[]{:S(2)}) %collective-permute-start.2) | collective-permute-done | bytes 131104 | tf_op jit(solution)/shard_map/ppermute | solution.py:425
  63.6 0.1 add_convert_fusion.1
  63.6 2.2 %collective-permute-start.3 = (bf16[64,1024]{1,0:T(8,128)(2,1)S(1)}, bf16[64,1024]{1,0:T(8,128)(2,1)S(1)}, u32[]{:S(2)}, u32[]{:S(2)}) collective-permute-start(bf16[64,1024]{1,0:T(8,128)(2,1)S(1)} %add_convert_fusion.1), channel_id=1, source_target_pairs={{0,16},{4,20},{8,24},{12,28},{16,0},{20,4},{24,8},{28,12},{1,17},{... | collective-permute-start | bytes 393224 | tf_op jit(solution)/shard_map/ppermute | solution.py:425
  65.8 5.3 %collective-permute-done.3 = bf16[64,1024]{1,0:T(8,128)(2,1)S(1)} collective-permute-done((bf16[64,1024]{1,0:T(8,128)(2,1)S(1)}, bf16[64,1024]{1,0:T(8,128)(2,1)S(1)}, u32[]{:S(2)}, u32[]{:S(2)}) %collective-permute-start.3) | collective-permute-done | bytes 131104 | tf_op jit(solution)/shard_map/ppermute | solution.py:425
  71.1 1.7 %collective-permute-start.4 = (bf16[64,1024]{1,0:T(8,128)(2,1)S(1)}, bf16[64,1024]{1,0:T(8,128)(2,1)S(1)}, u32[]{:S(2)}, u32[]{:S(2)}) collective-permute-start(bf16[64,1024]{1,0:T(8,128)(2,1)S(1)} %add_convert_fusion.rest_1_), channel_id=1, source_target_pairs={{0,4},{4,0},{8,12},{12,8},{16,20},{20,16},{24,28},{28,24},{1,5},{5... | collective-permute-start | bytes 393224 | tf_op jit(solution)/shard_map/ppermute | solution.py:425
  72.8 0.0 collective-permute-start.5
  72.8 1.9 %collective-permute-start.6 = (bf16[64,1024]{1,0:T(8,128)(2,1)S(1)}, bf16[64,1024]{1,0:T(8,128)(2,1)S(1)}, u32[]{:S(2)}, u32[]{:S(2)}) collective-permute-start(bf16[64,1024]{1,0:T(8,128)(2,1)S(1)} %add_convert_fusion.rest_1_), channel_id=1, source_target_pairs={{0,12},{4,8},{8,4},{12,0},{16,28},{20,24},{24,20},{28,16},{1,13},{... | collective-permute-start | bytes 393224 | tf_op jit(solution)/shard_map/ppermute | solution.py:425
  74.7 5.1 %shard_map.76 = (f32[1,8192,256]{2,1,0:T(8,128)}, bf16[8192,1024]{1,0:T(8,128)(2,1)S(1)}) custom-call(s32[2,1024]{1,0:T(2,128)S(1)} %copy-done.1, f32[1,8192,256]{2,1,0:T(8,128)} %mom_b.11, f32[1,8192,256]{2,1,0:T(8,128)} %mom_b.11, bf16[1,8192,256]{2,1,0:T(8,128)(2,1)} %grad_b.11, bf16[1,8192,256]{2,1,0:T(8,128)(2,1)} %grad_b.11, ...), custom_call_target="tpu_custom_call", output_to_operand_aliasing={{1}: (6, {})} | custom-call | tf_op jit(solution)/shard_map/pallas_call | solution.py:273
  79.8 5.1 %shard_map.77 = (f32[1,8192,256]{2,1,0:T(8,128)}, bf16[8192,1024]{1,0:T(8,128)(2,1)S(1)}) custom-call(s32[2,1024]{1,0:T(2,128)S(1)} %copy-done.1, f32[1,8192,256]{2,1,0:T(8,128)} %mom_b.11, f32[1,8192,256]{2,1,0:T(8,128)} %mom_b.11, bf16[1,8192,256]{2,1,0:T(8,128)(2,1)} %grad_b.11, ...), custom_call_target="tpu_custom_call", output_to_operand_aliasing={{1}: (6, {}), {0}: (7, {})} | custom-call | tf_op jit(solution)/shard_map/pallas_call | solution.py:273
  84.9 0.0 copy-start
  84.9 5.2 %shard_map.78 = (f32[1,8192,256]{2,1,0:T(8,128)}, bf16[8192,1024]{1,0:T(8,128)(2,1)S(1)}) custom-call(s32[2,1024]{1,0:T(2,128)S(1)} %copy-done.1, f32[1,8192,256]{2,1,0:T(8,128)} %mom_b.11, f32[1,8192,256]{2,1,0:T(8,128)} %mom_b.11, bf16[1,8192,256]{2,1,0:T(8,128)(2,1)} %grad_b.11, ...), custom_call_target="tpu_custom_call", output_to_operand_aliasing={{1}: (6, {}), {0}: (7, {})} | custom-call | tf_op jit(solution)/shard_map/pallas_call | solution.py:273
  90.1 0.0 collective-permute-done.4.rest_2_
  90.1 0.0 collective-permute-done.5.rest_3_
  90.1 0.0 collective-permute-done.6.rest_4_
  90.1 0.0 collective-permute-done.9.rest_6_
  90.1 0.0 collective-permute-done.11.rest_8_
  90.1 0.0 copy-done
  90.1 3.0 %apply.1 = (f32[1024,256]{1,0:T(8,128)}, bf16[2,128,256]{2,1,0:T(8,128)(2,1)S(1)}, bf16[2,128,256]{2,1,0:T(8,128)(2,1)S(1)}, bf16[2,128,256]{2,1,0:T(8,128)(2,1)...) custom-call(s32[1]{0:T(128)} %bitcast.device_ref, ...), custom_call_target="tpu_custom_call", output_to_operand_aliasing={{5}: (4, {})} | custom-call | tf_op jit(solution)/shard_map/apply/pallas_call | solution.py:373
  93.1 1.6 %collective-permute-start.12 = (bf16[2,128,256]{2,1,0:T(8,128)(2,1)S(1)}, bf16[2,128,256]{2,1,0:T(8,128)(2,1)S(1)}, u32[]{:S(2)}, u32[]{:S(2)}) collective-permute-start(bf16[2,128,256]{2,1,0:T(8,128)(2,1)S(1)} %get-tuple-element.46), channel_id=1, source_target_pairs={{0,4},{4,0},{8,12},{12,8},{16,20},{20,16},{24,28},{28,24},{1,5},{5... | collective-permute-start | bytes 393224 | tf_op jit(solution)/shard_map/ppermute | solution.py:425
  94.7 0.0 collective-permute-start.13
  94.7 1.8 %collective-permute-start.14 = (bf16[2,128,256]{2,1,0:T(8,128)(2,1)S(1)}, bf16[2,128,256]{2,1,0:T(8,128)(2,1)S(1)}, u32[]{:S(2)}, u32[]{:S(2)}) collective-permute-start(bf16[2,128,256]{2,1,0:T(8,128)(2,1)S(1)} %get-tuple-element.48), channel_id=1, source_target_pairs={{0,12},{4,8},{8,4},{12,0},{16,28},{20,24},{24,20},{28,16},{1,13},{... | collective-permute-start | bytes 393224 | tf_op jit(solution)/shard_map/ppermute | solution.py:425
  96.6 2.8 %collective-permute-done.12 = bf16[2,128,256]{2,1,0:T(8,128)(2,1)S(1)} collective-permute-done((bf16[2,128,256]{2,1,0:T(8,128)(2,1)S(1)}, bf16[2,128,256]{2,1,0:T(8,128)(2,1)S(1)}, u32[]{:S(2)}, u32[]{:S(2)}) %collective-permute-start.12) | collective-permute-done | bytes 131104 | tf_op jit(solution)/shard_map/ppermute | solution.py:425
  99.4 0.3 collective-permute-done.13
  99.7 1.2 %collective-permute-done.14 = bf16[2,128,256]{2,1,0:T(8,128)(2,1)S(1)} collective-permute-done((bf16[2,128,256]{2,1,0:T(8,128)(2,1)S(1)}, bf16[2,128,256]{2,1,0:T(8,128)(2,1)S(1)}, u32[]{:S(2)}, u32[]{:S(2)}) %collective-permute-start.14) | collective-permute-done | bytes 131104 | tf_op jit(solution)/shard_map/ppermute | solution.py:425
  100.9 0.1 convert_add_fusion
  101.0 3.6 %collective-permute-start.15 = (bf16[128,256]{1,0:T(8,128)(2,1)S(1)}, bf16[128,256]{1,0:T(8,128)(2,1)S(1)}, u32[]{:S(2)}, u32[]{:S(2)}) collective-permute-start(bf16[128,256]{1,0:T(8,128)(2,1)S(1)} %fusion.3), channel_id=1, source_target_pairs={{0,16},{4,20},{8,24},{12,28},{16,0},{20,4},{24,8},{28,12},{1,17},{... | collective-permute-start | bytes 196616 | tf_op jit(solution)/shard_map/ppermute | solution.py:425
  104.6 3.2 %shard_map.79 = (f32[1,8192,256]{2,1,0:T(8,128)}, bf16[8192,1024]{1,0:T(8,128)(2,1)S(1)}) custom-call(s32[2,1024]{1,0:T(2,128)S(1)} %copy-done.1, f32[1,8192,256]{2,1,0:T(8,128)} %mom_b.11, f32[1,8192,256]{2,1,0:T(8,128)} %mom_b.11, bf16[1,8192,256]{2,1,0:T(8,128)(2,1)} %grad_b.11, ...), custom_call_target="tpu_custom_call", output_to_operand_aliasing={{1}: (6, {}), {0}: (7, {})} | custom-call | tf_op jit(solution)/shard_map/pallas_call | solution.py:273
  107.8 3.2 %shard_map.80 = (f32[1,8192,256]{2,1,0:T(8,128)}, bf16[8192,1024]{1,0:T(8,128)(2,1)S(1)}) custom-call(s32[2,1024]{1,0:T(2,128)S(1)} %copy-done.1, f32[1,8192,256]{2,1,0:T(8,128)} %mom_b.11, f32[1,8192,256]{2,1,0:T(8,128)} %mom_b.11, bf16[1,8192,256]{2,1,0:T(8,128)(2,1)} %grad_b.11, ...), custom_call_target="tpu_custom_call", output_to_operand_aliasing={{1}: (6, {}), {0}: (7, {})} | custom-call | tf_op jit(solution)/shard_map/pallas_call | solution.py:273
  110.9 0.0 collective-permute-done.15
  110.9 0.6 fusion.2
  (2 shorter events, 0.0 us)
Async XLA Ops:
  0.6 1.7 %collective-permute-start.7 = (bf16[128,2048]{1,0:T(8,128)(2,1)}, bf16[128,2048]{1,0:T(8,128)(2,1)S(1)}, u32[]{:S(2)}, u32[]{:S(2)}) collective-permute-start(bf16[128,2048]{1,0:T(8,128)(2,1)} %param.8), channel_id=1, source_target_pairs={{0,0},{1,8},{2,16},{3,24},{4,4},{5,12},{6,20},{7,28},{8,1},{9,9},{... | collective-permute-start | bytes 1572872 | tf_op jit(solution)/shard_map/ppermute | solution.py:451
  2.3 0.8 copy-start.2
  4.2 7.4 %collective-permute-start.8 = (bf16[128,1024]{1,0:T(8,128)(2,1)S(1)}, bf16[128,1024]{1,0:T(8,128)(2,1)S(1)}, u32[]{:S(2)}, u32[]{:S(2)}) collective-permute-start(bf16[128,1024]{1,0:T(8,128)(2,1)S(1)} %get-tuple-element.38), channel_id=1, source_target_pairs={{0,4},{4,0},{8,12},{12,8},{16,20},{20,16},{24,28},{28,24},{1,5},{5... | collective-permute-start | bytes 786440 | tf_op jit(solution)/shard_map/ppermute | solution.py:425
  11.6 47.4 %collective-permute-start.10 = (bf16[2,128,1024]{2,1,0:T(8,128)(2,1)S(1)}, bf16[2,128,1024]{2,1,0:T(8,128)(2,1)S(1)}, u32[]{:S(2)}, u32[]{:S(2)}) collective-permute-start(bf16[2,128,1024]{2,1,0:T(8,128)(2,1)S(1)} %pad_maximum_fusion.rest_5_), channel_id=1, source_target_pairs={{0,2},{1,3},{2,0},{3,1},{4,6},{5,7},{6,4},{7,5},{8,10},{9,11},{10,... | collective-permute-start | bytes 1572872 | tf_op jit(solution)/shard_map/ppermute | solution.py:425
  41.6 0.7 copy-start.1
  55.5 5.7 %collective-permute-start = (bf16[64,1024]{1,0:T(8,128)(2,1)S(1)}, bf16[64,1024]{1,0:T(8,128)(2,1)S(1)}, u32[]{:S(2)}, u32[]{:S(2)}) collective-permute-start(bf16[64,1024]{1,0:T(8,128)(2,1)S(1)} %get-tuple-element.34), channel_id=1, source_target_pairs={{0,4},{4,0},{8,12},{12,8},{16,20},{20,16},{24,28},{28,24},{1,5},{5... | collective-permute-start | bytes 393224 | tf_op jit(solution)/shard_map/ppermute | solution.py:425
  57.0 5.0 %collective-permute-start.1 = (bf16[64,1024]{1,0:T(8,128)(2,1)S(1)}, bf16[64,1024]{1,0:T(8,128)(2,1)S(1)}, u32[]{:S(2)}, u32[]{:S(2)}) collective-permute-start(bf16[64,1024]{1,0:T(8,128)(2,1)S(1)} %get-tuple-element.35), channel_id=1, source_target_pairs={{0,8},{4,12},{8,0},{12,4},{16,24},{20,28},{24,16},{28,20},{1,9},{5... | collective-permute-start | bytes 393224 | tf_op jit(solution)/shard_map/ppermute | solution.py:425
  57.7 5.9 %collective-permute-start.2 = (bf16[64,1024]{1,0:T(8,128)(2,1)S(1)}, bf16[64,1024]{1,0:T(8,128)(2,1)S(1)}, u32[]{:S(2)}, u32[]{:S(2)}) collective-permute-start(bf16[64,1024]{1,0:T(8,128)(2,1)S(1)} %get-tuple-element.36), channel_id=1, source_target_pairs={{0,12},{4,8},{8,4},{12,0},{16,28},{20,24},{24,20},{28,16},{1,13},{... | collective-permute-start | bytes 393224 | tf_op jit(solution)/shard_map/ppermute | solution.py:425
  59.0 31.1 %collective-permute-start.9 = (bf16[2,128,1024]{2,1,0:T(8,128)(2,1)S(1)}, bf16[2,128,1024]{2,1,0:T(8,128)(2,1)S(1)}, u32[]{:S(2)}, u32[]{:S(2)}) collective-permute-start(bf16[2,128,1024]{2,1,0:T(8,128)(2,1)S(1)} %pad_maximum_fusion.rest_5_), channel_id=1, source_target_pairs={{0,1},{1,0},{2,3},{3,2},{4,5},{5,4},{6,7},{7,6},{8,9},{9,8},{10,11... | collective-permute-start | bytes 1572872 | tf_op jit(solution)/shard_map/ppermute | solution.py:425
  59.0 31.1 %collective-permute-start.11 = (bf16[2,128,1024]{2,1,0:T(8,128)(2,1)S(1)}, bf16[2,128,1024]{2,1,0:T(8,128)(2,1)S(1)}, u32[]{:S(2)}, u32[]{:S(2)}) collective-permute-start(bf16[2,128,1024]{2,1,0:T(8,128)(2,1)S(1)} %collective-permute-done.10.rest_7_), channel_id=1, source_target_pairs={{0,1},{1,0},{2,3},{3,2},{4,5},{5,4},{6,7},{7,6},{8,9},{9,8},{10,11... | collective-permute-start | bytes 1572872 | tf_op jit(solution)/shard_map/ppermute | solution.py:425
  63.6 7.5 %collective-permute-start.3 = (bf16[64,1024]{1,0:T(8,128)(2,1)S(1)}, bf16[64,1024]{1,0:T(8,128)(2,1)S(1)}, u32[]{:S(2)}, u32[]{:S(2)}) collective-permute-start(bf16[64,1024]{1,0:T(8,128)(2,1)S(1)} %add_convert_fusion.1), channel_id=1, source_target_pairs={{0,16},{4,20},{8,24},{12,28},{16,0},{20,4},{24,8},{28,12},{1,17},{... | collective-permute-start | bytes 393224 | tf_op jit(solution)/shard_map/ppermute | solution.py:425
  71.1 18.9 %collective-permute-start.4 = (bf16[64,1024]{1,0:T(8,128)(2,1)S(1)}, bf16[64,1024]{1,0:T(8,128)(2,1)S(1)}, u32[]{:S(2)}, u32[]{:S(2)}) collective-permute-start(bf16[64,1024]{1,0:T(8,128)(2,1)S(1)} %add_convert_fusion.rest_1_), channel_id=1, source_target_pairs={{0,4},{4,0},{8,12},{12,8},{16,20},{20,16},{24,28},{28,24},{1,5},{5... | collective-permute-start | bytes 393224 | tf_op jit(solution)/shard_map/ppermute | solution.py:425
  72.8 17.3 %collective-permute-start.5 = (bf16[64,1024]{1,0:T(8,128)(2,1)S(1)}, bf16[64,1024]{1,0:T(8,128)(2,1)S(1)}, u32[]{:S(2)}, u32[]{:S(2)}) collective-permute-start(bf16[64,1024]{1,0:T(8,128)(2,1)S(1)} %add_convert_fusion.rest_1_), channel_id=1, source_target_pairs={{0,8},{4,12},{8,0},{12,4},{16,24},{20,28},{24,16},{28,20},{1,9},{5... | collective-permute-start | bytes 393224 | tf_op jit(solution)/shard_map/ppermute | solution.py:425
  72.8 17.3 %collective-permute-start.6 = (bf16[64,1024]{1,0:T(8,128)(2,1)S(1)}, bf16[64,1024]{1,0:T(8,128)(2,1)S(1)}, u32[]{:S(2)}, u32[]{:S(2)}) collective-permute-start(bf16[64,1024]{1,0:T(8,128)(2,1)S(1)} %add_convert_fusion.rest_1_), channel_id=1, source_target_pairs={{0,12},{4,8},{8,4},{12,0},{16,28},{20,24},{24,20},{28,16},{1,13},{... | collective-permute-start | bytes 393224 | tf_op jit(solution)/shard_map/ppermute | solution.py:425
  84.9 5.3 %copy-start = (f32[1024,256]{1,0:T(8,128)S(1)}, f32[1024,256]{1,0:T(8,128)}, u32[]{:S(2)}) copy-start(f32[1024,256]{1,0:T(8,128)} %masters_ref.1) | copy-start | bytes 3145732
  93.1 6.3 %collective-permute-start.12 = (bf16[2,128,256]{2,1,0:T(8,128)(2,1)S(1)}, bf16[2,128,256]{2,1,0:T(8,128)(2,1)S(1)}, u32[]{:S(2)}, u32[]{:S(2)}) collective-permute-start(bf16[2,128,256]{2,1,0:T(8,128)(2,1)S(1)} %get-tuple-element.46), channel_id=1, source_target_pairs={{0,4},{4,0},{8,12},{12,8},{16,20},{20,16},{24,28},{28,24},{1,5},{5... | collective-permute-start | bytes 393224 | tf_op jit(solution)/shard_map/ppermute | solution.py:425
  94.7 5.0 %collective-permute-start.13 = (bf16[2,128,256]{2,1,0:T(8,128)(2,1)S(1)}, bf16[2,128,256]{2,1,0:T(8,128)(2,1)S(1)}, u32[]{:S(2)}, u32[]{:S(2)}) collective-permute-start(bf16[2,128,256]{2,1,0:T(8,128)(2,1)S(1)} %get-tuple-element.47), channel_id=1, source_target_pairs={{0,8},{4,12},{8,0},{12,4},{16,24},{20,28},{24,16},{28,20},{1,9},{5... | collective-permute-start | bytes 393224 | tf_op jit(solution)/shard_map/ppermute | solution.py:425
  94.7 6.2 %collective-permute-start.14 = (bf16[2,128,256]{2,1,0:T(8,128)(2,1)S(1)}, bf16[2,128,256]{2,1,0:T(8,128)(2,1)S(1)}, u32[]{:S(2)}, u32[]{:S(2)}) collective-permute-start(bf16[2,128,256]{2,1,0:T(8,128)(2,1)S(1)} %get-tuple-element.48), channel_id=1, source_target_pairs={{0,12},{4,8},{8,4},{12,0},{16,28},{20,24},{24,20},{28,16},{1,13},{... | collective-permute-start | bytes 393224 | tf_op jit(solution)/shard_map/ppermute | solution.py:425
  101.0 9.9 %collective-permute-start.15 = (bf16[128,256]{1,0:T(8,128)(2,1)S(1)}, bf16[128,256]{1,0:T(8,128)(2,1)S(1)}, u32[]{:S(2)}, u32[]{:S(2)}) collective-permute-start(bf16[128,256]{1,0:T(8,128)(2,1)S(1)} %fusion.3), channel_id=1, source_target_pairs={{0,16},{4,20},{8,24},{12,28},{16,0},{20,4},{24,8},{28,12},{1,17},{... | collective-permute-start | bytes 196616 | tf_op jit(solution)/shard_map/ppermute | solution.py:425
